TPU v7x, 32 devices: a whole 2x2x4 slice. The times are simulated.
32 devices in a mesh: dp: 8 (over z, core), expert: 4 (over y, x).
Axes of the slice: x: 2, y: 2, z: 4, core: 2. Of those that a mesh axis runs over, the one named last changes fastest.
Arguments:
- token_ids: int32 [32, 512], P('dp'), may hold values from 0 to 31999
- segments: int32 [32, 512], P(('dp', 'expert')), may hold values from 0 to 3, never falling along the last dimension, each value on 1 to 320 neighbouring positions
- routes: int32 [32, 512, 2], P('dp'), may hold values from 0 to 7, all different within a row; in each aligned block of 512 rows (0 to 511, 512 to 1023, ..., all dimensions but the last counted through in order) at most 192 rows name the same one
- positions: int32 [2048], P(('dp', 'expert')), may hold values from 0 to 511
- targets: int32 [2048], P('dp'), may hold values from 0 to 31999
- teacher_ids: int32 [2048, 64], P('dp'), may hold values from 0 to 31999
- teacher_probs: float32 [2048, 64], P('dp'), as said below
- attention: float32 [4, 768, 768], P(None, 'dp'), may hold values from -0.21875 to 0.21875
- attention_moment: float32 [4, 768, 768], P(None, 'dp'), may hold values from -0.013671875 to 0.013671875
- attention_average: float32 [4, 768, 768], P(None, 'dp'), may hold values from -0.21875 to 0.21875
- expert_in: float32 [8, 768, 3072], P('expert', 'dp'), may hold values from -0.21875 to 0.21875
- expert_in_moment: float32 [8, 768, 3072], P('expert', 'dp'), may hold values from -0.0024414062 to 0.0024414062
- expert_in_average: float32 [8, 768, 3072], P('expert', 'dp'), may hold values from -0.21875 to 0.21875
- expert_out: float32 [8, 3072, 768], P('expert', 'dp'), may hold values from -0.02734375 to 0.02734375
- expert_out_moment: float32 [8, 3072, 768], P('expert', 'dp'), may hold values from -0.013671875 to 0.013671875
- expert_out_average: float32 [8, 3072, 768], P('expert', 'dp'), may hold values from -0.02734375 to 0.02734375
- embedding: float32 [32000, 768], P('expert', 'dp'), may hold values from -0.4375 to 0.4375
- embedding_moment: float32 [32000, 768], P('expert', 'dp'), may hold values from -0.0012207031 to 0.0012207031
- embedding_average: float32 [32000, 768], P('expert', 'dp'), may hold values from -0.4375 to 0.4375
- small_params: float32 [11, 768], P(None, 'dp')
- small_moment: float32 [11, 768], P(None, 'dp'), may hold values from -0.0390625 to 0.0390625
- small_average: float32 [11, 768], P(None, 'dp'), may hold values from -3 to 3
Outputs:
- loss_value: float32 [], replicated
- attention_next: float32 [4, 768, 768], P(None, 'dp')
- attention_moment_next: float32 [4, 768, 768], P(None, 'dp')
- attention_average_next: float32 [4, 768, 768], P(None, 'dp')
- attention_copy: bfloat16 [4, 768, 768], P(None, 'dp')
- expert_in_next: float32 [8, 768, 3072], P('expert', 'dp')
- expert_in_moment_next: float32 [8, 768, 3072], P('expert', 'dp')
- expert_in_average_next: float32 [8, 768, 3072], P('expert', 'dp')
- expert_in_copy: bfloat16 [8, 768, 3072], P('expert', 'dp')
- expert_out_next: float32 [8, 3072, 768], P('expert', 'dp')
- expert_out_moment_next: float32 [8, 3072, 768], P('expert', 'dp')
- expert_out_average_next: float32 [8, 3072, 768], P('expert', 'dp')
- expert_out_copy: bfloat16 [8, 3072, 768], P('expert', 'dp')
- embedding_next: float32 [32000, 768], P('expert', 'dp')
- embedding_moment_next: float32 [32000, 768], P('expert', 'dp')
- embedding_average_next: float32 [32000, 768], P('expert', 'dp')
- embedding_copy: bfloat16 [32000, 768], P('expert', 'dp')
- small_next: float32 [11, 768], P(None, 'dp')
- small_moment_next: float32 [11, 768], P(None, 'dp')
- small_average_next: float32 [11, 768], P(None, 'dp')
- small_copy: bfloat16 [11, 768], P(None, 'dp')
Inputs may be any that keep to these rules, and one draw needn't show every extreme that they name: `routes`: each row names 2 different experts; in the rows of one device (aligned blocks of 512 rows) no expert is named by more than 192 rows, a bound that some block reaches. `segments`: never falling along a sequence. `teacher_probs`: Positive; each row sums to one.
All inputs are finite; a program needn't handle non-finite values.
Results may differ from a plain program's by a relative error of at most 0.01195.
The roundings to bfloat16 on the way count: a program that leaves them out, or rounds other values in their place, can miss the bound.
Values may be sent and summed in bfloat16 or wider, within the bound.
No kernel may reach another device: no remote copies, remote signals or barrier semaphores. Data moves between devices by JAX's collectives and lax.ppermute only.
A program may use at most 320 MiB of HBM per device.

v0:
```python
import math

import jax
import jax.numpy as jnp
from jax import lax
from jax.sharding import PartitionSpec as P

HEAD = 64
TOP = 2
STEP = 7


EPSILON = 1e-06
MOMENTUM = 0.9
RATE_TABLE = (0.1, 0.3, 0.01, 0.05, 0.05)
MASKED_SCORE = -1e30


def combined_all(value, axis, join):
    pieces = jax.tree.map(lambda part: lax.all_gather(part, axis), value)
    head = jax.tree.map(lambda part: part[0], pieces)
    tail = jax.tree.map(lambda part: part[1:], pieces)
    total, _ = lax.scan(lambda total, share: (join(total, share), None), head, tail)
    return total


def normal_parts(stream):
    factor = lax.rsqrt(jnp.mean(stream * stream, axis=-1, keepdims=True) + EPSILON)
    return (stream * factor, factor)


def norm_backward(normal, factor, gain, grad):
    gain_grad = jnp.sum(grad * normal, axis=0)
    normal_grad = grad * gain
    inner = jnp.mean(normal_grad * normal, axis=-1, keepdims=True)
    return (factor * (normal_grad - normal * inner), gain_grad)


def slot_table(block_routes, experts):
    flat = block_routes.reshape(-1)
    hits = (flat[:, None] == jnp.arange(experts, dtype=jnp.int32)[None, :]).astype(jnp.int32)
    before = jnp.cumsum(hits, axis=0) - hits
    return (flat, jnp.sum(before * hits, axis=1))


def block_scores(query, keys, seg_ids, block_index, length, block_rows, scaling):
    start = block_index * block_rows
    first_row = start // length * length
    scores = jnp.einsum("qhd,khd->hqk", query, keys, preferred_element_type=jnp.float32) * scaling
    query_place = start - first_row + jnp.arange(block_rows)
    allowed = (jnp.arange(length)[None, :] <= query_place[:, None]) & (
        seg_ids[None, :] == seg_ids[:, None]
    )
    return (jnp.where(allowed[None], scores, MASKED_SCORE), query, keys, first_row)


def combine_stats(earlier, later):
    highest = jnp.maximum(earlier[0], later[0])
    totals = earlier[1] * jnp.exp(earlier[0] - highest) + later[1] * jnp.exp(later[0] - highest)
    return (highest, totals, earlier[2] + later[2])


def nesterov_update(master, moment, average, grad, rate):
    moment_next = MOMENTUM * moment + grad
    master_next = master - rate * (grad + MOMENTUM * moment_next)
    average_next = average + (master_next - average) / (STEP + 1)
    return (master_next, moment_next, average_next, master_next.astype(jnp.bfloat16))


def shards(
    token_ids,
    segments,
    routes,
    positions,
    targets,
    teacher_ids,
    teacher_probs,
    attention,
    attention_moment,
    attention_average,
    expert_in,
    expert_in_moment,
    expert_in_average,
    expert_out,
    expert_out_moment,
    expert_out_average,
    embedding,
    embedding_moment,
    embedding_average,
    small_params,
    small_moment,
    small_average,
):
    members = lax.axis_size("expert")
    replicas = lax.axis_size("dp")
    my_index = lax.axis_index("expert")
    length = segments.shape[1]
    local_rows = segments.shape[0] * length
    width = attention.shape[2]
    head_count = width // HEAD
    local_experts = expert_in.shape[0]
    experts = local_experts * members
    vocab_rows = embedding.shape[0]
    capacity = max(2, 3 * local_rows * TOP // (2 * experts))
    loss_local = positions.shape[0]
    loss_count = loss_local * members * replicas
    block_rows = min(512, length)
    block_count = local_rows // block_rows
    scaling = HEAD ** (-0.5)
    highest_precision = lax.Precision.HIGHEST
    group_count = members * local_rows
    lookup_rows = math.gcd(group_count, 2048)
    vocab_iota = jnp.arange(vocab_rows, dtype=jnp.int32)
    dense_low, small_low = (
        lax.all_gather(attention.astype(jnp.bfloat16), "dp", axis=1, tiled=True),
        lax.all_gather(small_params.astype(jnp.bfloat16), "dp", axis=1, tiled=True),
    )
    in_low, out_low, table_low = (
        lax.all_gather(expert_in.astype(jnp.bfloat16), "dp", axis=1, tiled=True),
        lax.all_gather(expert_out.astype(jnp.bfloat16), "dp", axis=1, tiled=True),
        lax.all_gather(embedding.astype(jnp.bfloat16), "dp", axis=1, tiled=True),
    )
    gain_rows = small_low[:3].astype(jnp.float32)
    router = small_low[3:].astype(jnp.float32)
    group_ids = token_ids.reshape(-1)
    group_routes = routes.reshape(members * local_rows, TOP)
    own_routes = lax.dynamic_slice_in_dim(group_routes, my_index * local_rows, local_rows, 0)
    local_ids = group_ids - my_index * vocab_rows
    id_blocks = local_ids.reshape(group_count // lookup_rows, lookup_rows)

    def lookup_block(ids_block):
        selector = (ids_block[:, None] == vocab_iota[None, :]).astype(jnp.bfloat16)
        return jnp.dot(selector, table_low, preferred_element_type=jnp.float32).astype(jnp.bfloat16)

    partial_value = lax.map(lookup_block, id_blocks).reshape(group_count, width)
    stream = lax.psum_scatter(partial_value, "expert", scatter_dimension=0, tiled=True).astype(
        jnp.float32
    )
    normal_one, factor_one = normal_parts(stream)
    attn_in = (normal_one * gain_rows[0]).astype(jnp.bfloat16)
    projected = jnp.einsum(
        "td,jde->jte", attn_in, dense_low[:3], preferred_element_type=jnp.float32
    ).astype(jnp.bfloat16)
    query = projected[0].reshape(local_rows, head_count, HEAD)
    keys = projected[1].reshape(local_rows, head_count, HEAD)
    values = projected[2].reshape(local_rows, head_count, HEAD)
    seg_ids = segments.reshape(-1)

    def forward_block(block_index):
        scores, query_block, key_block, first_row = block_scores(
            query, keys, seg_ids, block_index, length, block_rows, scaling
        )
        highest = jnp.max(scores, axis=-1, keepdims=True)
        powers = jnp.exp(scores - highest)
        totals = jnp.sum(powers, axis=-1, keepdims=True)
        mixed_block = jnp.einsum(
            "hqk,khd->qhd",
            (powers / totals).astype(jnp.bfloat16),
            values,
            preferred_element_type=jnp.float32,
        )
        return (mixed_block, (highest + jnp.log(totals))[..., 0])

    mixed_blocks, log_totals = lax.map(forward_block, jnp.arange(block_count))
    mixed = mixed_blocks.reshape(local_rows, width).astype(jnp.bfloat16)
    hidden_one = stream + jnp.dot(mixed, dense_low[3], preferred_element_type=jnp.float32)
    normal_two, factor_two = normal_parts(hidden_one)
    moe_in = (normal_two * gain_rows[1]).astype(jnp.bfloat16)
    moe_float = moe_in.astype(jnp.float32)
    router_logits = jnp.dot(moe_float, router.T, precision=highest_precision)
    chosen = jnp.take_along_axis(router_logits, own_routes, axis=1)
    gating = jnp.exp(chosen - jnp.max(chosen, axis=1, keepdims=True))
    gating = gating / jnp.sum(gating, axis=1, keepdims=True)
    flat_routes, slots = slot_table(own_routes, experts)
    landing = flat_routes * capacity + slots
    token_of = jnp.arange(local_rows * TOP) // TOP
    everyone = lax.all_gather(moe_in, "expert", axis=0, tiled=True)
    all_flat, all_slots = jax.vmap(lambda block_routes: slot_table(block_routes, experts))(
        group_routes.reshape(members, local_rows, TOP)
    )
    owned = all_flat - my_index * local_experts
    source = jnp.arange(members)[:, None]
    spot = owned * (members * capacity) + source * capacity + all_slots
    spot = jnp.where(
        (owned >= 0) & (owned < local_experts), spot, local_experts * members * capacity
    )
    source_rows = source * local_rows + token_of[None, :]
    arrived = (
        jnp.zeros((local_experts * members * capacity, width), jnp.bfloat16)
        .at[spot.reshape(-1)]
        .set(jnp.take(everyone, source_rows.reshape(-1), axis=0), mode="drop")
    )
    arrived = arrived.reshape(local_experts, members * capacity, width)
    expert_hidden = jnp.einsum("ecd,edf->ecf", arrived, in_low, preferred_element_type=jnp.float32)
    activated = jax.nn.gelu(expert_hidden, approximate=True).astype(jnp.bfloat16)
    expert_result = jnp.einsum(
        "ecf,efd->ecd", activated, out_low, preferred_element_type=jnp.float32
    ).astype(jnp.bfloat16)
    returned = lax.all_to_all(
        expert_result.reshape(local_experts, members, capacity, width),
        "expert",
        split_axis=1,
        concat_axis=0,
        tiled=True,
    )
    returned = returned.reshape(experts * capacity, width)
    picked = jnp.take(returned, landing, axis=0).reshape(local_rows, TOP, width).astype(jnp.float32)
    hidden_two = hidden_one + jnp.sum(gating[:, :, None] * picked, axis=1)
    normal_three, factor_three = normal_parts(hidden_two)
    final = (normal_three * gain_rows[2]).astype(jnp.bfloat16)
    group_final = lax.all_gather(jnp.take(final, positions, axis=0), "expert", axis=0, tiled=True)
    logits = jnp.einsum("gd,vd->gv", group_final, table_low, preferred_element_type=jnp.float32)
    target_local = targets - my_index * vocab_rows
    teacher_local = teacher_ids - my_index * vocab_rows
    target_inside = (target_local >= 0) & (target_local < vocab_rows)
    teacher_inside = (teacher_local >= 0) & (teacher_local < vocab_rows)
    target_logit = jnp.take_along_axis(
        logits, jnp.clip(target_local, 0, vocab_rows - 1)[:, None], axis=1
    )[:, 0]
    teacher_logit = jnp.take_along_axis(logits, jnp.clip(teacher_local, 0, vocab_rows - 1), axis=1)
    taught = jnp.where(target_inside, target_logit, 0.0) + jnp.sum(
        jnp.where(teacher_inside, teacher_probs * teacher_logit, 0.0), axis=1
    )
    local_max = jnp.max(logits, axis=1)
    local_total = jnp.sum(jnp.exp(logits - local_max[:, None]), axis=1)
    highest, totals, picked_sum = combined_all(
        (local_max, local_total, taught), "expert", combine_stats
    )
    log_total = highest + jnp.log(totals)
    entropy = jnp.sum(teacher_probs * jnp.log(teacher_probs), axis=1)
    terms = 2.0 * log_total - picked_sum + entropy
    loss_part = (
        jnp.sum(lax.dynamic_slice_in_dim(terms, my_index * loss_local, loss_local, 0)) / loss_count
    )
    loss_rows = logits.shape[0]
    target_rows = math.gcd(loss_rows, 128)

    def target_block(triple):
        target_block_ids, teacher_block_ids, prob_block = triple
        hit_target = (target_block_ids[:, None] == vocab_iota[None, :]).astype(jnp.float32)
        hit_teacher = jnp.sum(
            jnp.where(
                teacher_block_ids[:, :, None] == vocab_iota[None, None, :],
                prob_block[:, :, None],
                0.0,
            ),
            axis=1,
        )
        return hit_target + hit_teacher

    taken = lax.map(
        target_block,
        (
            target_local.reshape(-1, target_rows),
            teacher_local.reshape(-1, target_rows, teacher_ids.shape[1]),
            teacher_probs.reshape(-1, target_rows, teacher_ids.shape[1]),
        ),
    ).reshape(loss_rows, vocab_rows)
    soft = jnp.exp(logits - log_total[:, None])
    logit_grad = ((2.0 * soft - taken) / loss_count).astype(jnp.bfloat16)
    embed_head = jnp.einsum(
        "gv,gd->vd", logit_grad, group_final, preferred_element_type=jnp.float32
    )
    final_grad = lax.psum_scatter(
        jnp.dot(logit_grad, table_low, preferred_element_type=jnp.float32),
        "expert",
        scatter_dimension=0,
        tiled=True,
    )
    final_full = jnp.zeros((local_rows, width), jnp.float32).at[positions].add(final_grad)
    grad_two, gain_three = norm_backward(normal_three, factor_three, gain_rows[2], final_full)
    gate_grad = jnp.sum(grad_two[:, None, :] * picked, axis=2)
    chosen_grad = gating * (gate_grad - jnp.sum(gating * gate_grad, axis=1, keepdims=True))
    expert_ids = jnp.arange(experts, dtype=jnp.int32)
    route_grad = jnp.sum(
        chosen_grad[:, :, None] * (own_routes[:, :, None] == expert_ids[None, None, :]), axis=1
    )
    router_grad = jnp.dot(route_grad.T, moe_float, precision=highest_precision)
    moe_grad = jnp.dot(route_grad, router, precision=highest_precision)
    result_grad = (
        (gating[:, :, None] * grad_two[:, None, :])
        .astype(jnp.bfloat16)
        .reshape(local_rows * TOP, width)
    )
    outgoing_grad = (
        jnp.zeros((experts * capacity, width), jnp.bfloat16).at[landing].set(result_grad)
    )
    arrived_grad = lax.all_to_all(
        outgoing_grad.reshape(members, local_experts, capacity, width),
        "expert",
        split_axis=0,
        concat_axis=2,
        tiled=True,
    )
    arrived_grad = arrived_grad.reshape(local_experts, members * capacity, width)
    out_grad = jnp.einsum(
        "ecf,ecd->efd", activated, arrived_grad, preferred_element_type=jnp.float32
    )
    activated_grad = jnp.einsum(
        "ecd,efd->ecf", arrived_grad, out_low, preferred_element_type=jnp.float32
    )
    gelu_pull = jax.vjp(lambda inner: jax.nn.gelu(inner, approximate=True), expert_hidden)[1]
    hidden_grad = gelu_pull(activated_grad)[0].astype(jnp.bfloat16)
    in_grad = jnp.einsum("ecd,ecf->edf", arrived, hidden_grad, preferred_element_type=jnp.float32)
    rows_grad = jnp.einsum("ecf,edf->ecd", hidden_grad, in_low, preferred_element_type=jnp.float32)
    back_rows = lax.all_to_all(
        rows_grad.reshape(local_experts, members, capacity, width),
        "expert",
        split_axis=1,
        concat_axis=0,
        tiled=True,
    )
    back_rows = back_rows.reshape(experts * capacity, width)
    moe_grad = moe_grad + jnp.sum(
        jnp.take(back_rows, landing, axis=0).reshape(local_rows, TOP, width), axis=1
    )
    grad_part, gain_two = norm_backward(normal_two, factor_two, gain_rows[1], moe_grad)
    grad_one = grad_two + grad_part
    attn_grad = grad_one.astype(jnp.bfloat16)
    out_weight_grad = jnp.einsum("tc,td->cd", mixed, attn_grad, preferred_element_type=jnp.float32)
    mixed_grad = jnp.einsum(
        "td,cd->tc", attn_grad, dense_low[3], preferred_element_type=jnp.float32
    )
    mixed_grad = mixed_grad.astype(jnp.bfloat16).reshape(local_rows, head_count, HEAD)

    def backward_block(carry, inputs):
        keys_grad, values_grad = carry
        block_index, log_block = inputs
        scores, query_block, key_block, first_row = block_scores(
            query, keys, seg_ids, block_index, length, block_rows, scaling
        )
        soft_block = jnp.exp(scores - log_block[..., None])
        value_part = jnp.einsum(
            "hqk,qhd->khd",
            soft_block.astype(jnp.bfloat16),
            mixed_grad,
            preferred_element_type=jnp.float32,
        )
        weight_grad = jnp.einsum(
            "qhd,khd->hqk", mixed_grad, values, preferred_element_type=jnp.float32
        )
        score_grad = soft_block * (
            weight_grad - jnp.sum(soft_block * weight_grad, axis=-1, keepdims=True)
        )
        score_grad = score_grad.astype(jnp.bfloat16)
        query_part = (
            jnp.einsum("hqk,khd->qhd", score_grad, key_block, preferred_element_type=jnp.float32)
            * scaling
        )
        key_part = (
            jnp.einsum("hqk,qhd->khd", score_grad, query_block, preferred_element_type=jnp.float32)
            * scaling
        )
        keys_grad = keys_grad + key_part
        values_grad = values_grad + value_part
        return ((keys_grad, values_grad), query_part)

    zero_grad = jnp.zeros((local_rows, head_count, HEAD), jnp.float32)
    (keys_grad, values_grad), query_parts = lax.scan(
        backward_block, (zero_grad, zero_grad), (jnp.arange(block_count), log_totals)
    )
    projected_grad = jnp.stack(
        [
            query_parts.reshape(local_rows, width),
            keys_grad.reshape(local_rows, width),
            values_grad.reshape(local_rows, width),
        ]
    ).astype(jnp.bfloat16)
    qkv_grad = jnp.einsum(
        "td,jte->jde", attn_in, projected_grad, preferred_element_type=jnp.float32
    )
    attn_in_grad = jnp.einsum(
        "jte,jde->td", projected_grad, dense_low[:3], preferred_element_type=jnp.float32
    )
    grad_part, gain_one = norm_backward(normal_one, factor_one, gain_rows[0], attn_in_grad)
    stream_grad = (grad_one + grad_part).astype(jnp.bfloat16)
    group_grad = lax.all_gather(stream_grad, "expert", axis=0, tiled=True)

    def add_rows(total, pair):
        selector = (pair[0][:, None] == vocab_iota[None, :]).astype(jnp.bfloat16)
        return (
            total + jnp.einsum("tv,td->vd", selector, pair[1], preferred_element_type=jnp.float32),
            None,
        )

    embed_grad, _ = lax.scan(
        add_rows,
        embed_head,
        (id_blocks, group_grad.reshape(group_count // lookup_rows, lookup_rows, width)),
    )
    in_sum, out_sum, embed_sum = (
        lax.psum_scatter(
            in_grad.astype(jnp.bfloat16), "dp", scatter_dimension=1, tiled=True
        ).astype(jnp.float32),
        lax.psum_scatter(
            out_grad.astype(jnp.bfloat16), "dp", scatter_dimension=1, tiled=True
        ).astype(jnp.float32),
        lax.psum_scatter(
            embed_grad.astype(jnp.bfloat16), "dp", scatter_dimension=1, tiled=True
        ).astype(jnp.float32),
    )
    attention_grad = jnp.concatenate([qkv_grad, out_weight_grad[None]], axis=0)
    small_grad = jnp.concatenate([jnp.stack([gain_one, gain_two, gain_three]), router_grad], axis=0)
    attention_sum, small_sum, loss_value = lax.psum(
        (attention_grad, small_grad, loss_part), ("dp", "expert")
    )
    share = width // replicas
    share_start = lax.axis_index("dp") * share
    attention_sum = lax.dynamic_slice_in_dim(attention_sum, share_start, share, 1)
    small_sum = lax.dynamic_slice_in_dim(small_sum, share_start, share, 1)
    rate_base = loss_count**0.5
    first_out = nesterov_update(
        attention, attention_moment, attention_average, attention_sum, RATE_TABLE[0] * rate_base
    )
    second_out = nesterov_update(
        expert_in, expert_in_moment, expert_in_average, in_sum, RATE_TABLE[1] * rate_base
    )
    third_out = nesterov_update(
        expert_out, expert_out_moment, expert_out_average, out_sum, RATE_TABLE[2] * rate_base
    )
    fourth_out = nesterov_update(
        embedding, embedding_moment, embedding_average, embed_sum, RATE_TABLE[3] * rate_base
    )
    fifth_out = nesterov_update(
        small_params, small_moment, small_average, small_sum, RATE_TABLE[4] * rate_base
    )
    return (loss_value,) + first_out + second_out + third_out + fourth_out + fifth_out


def solution(mesh):
    return jax.shard_map(
        shards,
        mesh=mesh,
        in_specs=(
            P("dp", None),
            P(("dp", "expert"), None),
            P("dp", None, None),
            P(("dp", "expert")),
            P("dp"),
            P("dp", None),
            P("dp", None),
            P(None, "dp", None),
            P(None, "dp", None),
            P(None, "dp", None),
            P("expert", "dp", None),
            P("expert", "dp", None),
            P("expert", "dp", None),
            P("expert", "dp", None),
            P("expert", "dp", None),
            P("expert", "dp", None),
            P("expert", "dp"),
            P("expert", "dp"),
            P("expert", "dp"),
            P(None, "dp"),
            P(None, "dp"),
            P(None, "dp"),
        ),
        out_specs=(
            P(),
            P(None, "dp", None),
            P(None, "dp", None),
            P(None, "dp", None),
            P(None, "dp", None),
            P("expert", "dp", None),
            P("expert", "dp", None),
            P("expert", "dp", None),
            P("expert", "dp", None),
            P("expert", "dp", None),
            P("expert", "dp", None),
            P("expert", "dp", None),
            P("expert", "dp", None),
            P("expert", "dp"),
            P("expert", "dp"),
            P("expert", "dp"),
            P("expert", "dp"),
            P(None, "dp"),
            P(None, "dp"),
            P(None, "dp"),
            P(None, "dp"),
        ),
        check_vma=False,
    )
```

profile of v0, /device:TPU:0, one launch (start us, length us, event | category | flops | bytes accessed | tf_op | source)
XLA Modules:
  0.0 2224.3 jit_solution(15651792030422284334)
XLA Ops:
  10.6 117.9 %all-gather.14.cloned.1.call-done = bf16[8000,768]{0,1:T(8,128)(2,1)} async-done(((bf16[8000,96]{0,1:T(8,128)(2,1)}), bf16[8000,768]{0,1:T(8,128)(2,1)}) %all-gather.14.cloned.1.call-update) | async-done | bytes 12288016 | tf_op jit(solution)/shard_map/all_gather | solution.py:121
  128.4 35.7 %fusion.26 = bf16[2048,768]{1,0:T(8,128)(2,1)} fusion(bf16[8000,768]{0,1:T(8,128)(2,1)} %all-gather.14.cloned.1.call-done, s32[2048]{0:T(1024)S(1)} %bitcast.287), kind=kOutput, calls=%fused_computation.63 | convolution fusion | flops 25183780864 | bytes 15441920 | tf_op jit(solution)/shard_map/while/body/eval_jaxpr/dot_general | solution.py:133
  166.3 14.2 all-gather.3
  181.5 25.0 %reduce-scatter.6.cloned.1.call-done = bf16[512,768]{1,0:T(8,128)(2,1)} async-done(((bf16[2048,768]{1,0:T(8,128)(2,1)}), bf16[512,768]{1,0:T(8,128)(2,1)}) %reduce-scatter.6.cloned.1.call-update) | async-done | bytes 786448 | tf_op jit(solution)/shard_map/reduce_scatter | solution.py:136
  207.9 52.5 %all-gather.16.cloned.1.call-done = bf16[4,768,768]{2,1,0:T(8,128)(2,1)} async-done(((bf16[4,96,768]{2,1,0:T(8,128)(2,1)}), bf16[4,768,768]{2,1,0:T(8,128)(2,1)}) %all-gather.16.cloned.1.call-update) | async-done | bytes 4718608 | tf_op jit(solution)/shard_map/all_gather | solution.py:115
  293.5 9.0 reduce-window.16
  305.2 298.1 %while.7 = (s32[]{:T(128)}, f32[2,128,8000]{1,0,2:T(2,128)}, s32[2,128]{1,0:T(2,128)S(1)}, s32[2,128,64]{1,2,0:T(8,128)S(1)}, f32[2,128,64]{1,0,2:T(2,128)S(1)}, /*index=5*/s32[]{:T(128)}, s32[]{:T(128)}) while((s32[]{:T(128)}, f32[2,128,8000]{1,0,2:T(2,128)}, s32[2,128]{1,0:T(2,128)S(1)}, ...), condition=%wide.region_26.27_spmd.clone.clone, body=%wide.region_24.26_spmd.clone.clone.sunk | while | flops 198656000 | bytes 20678244 | solution.py:251
  305.3 48.3 %select_reduce_fusion.5 = f32[128,8000]{0,1:T(8,128)S(1)} fusion(f32[128,64]{0,1:T(8,128)S(1)} %bitcast.244, s32[128,64]{0,1:T(8,128)S(1)} %dynamic-slice_bitcast_fusion.2), kind=kLoop, calls=%fused_computation.16.clone.1 | loop fusion | flops 195584000 | bytes 4161536 | tf_op jit(solution)/shard_map/while/body/eval_jaxpr/reduce_sum | solution.py:241
  356.0 98.2 %dynamic_update_slice.18 = f32[2,128,8000]{1,0,2:T(2,128)} dynamic-update-slice(f32[2,128,8000]{1,0,2:T(2,128)} %get-tuple-element.518, f32[1,128,8000]{1,0,2:T(1,128)} %bitcast.229, s32[]{:T(128)S(6)} %copy.333, s32[]{:T(128)} %constant.298.clone.1..sunk, s32[]{:T(128)} %constant.298.clone.1..sunk) | dynamic-update-slice | bytes 8192004 | tf_op jit(solution)/shard_map/while/body/jit(dynamic_update_index_in_dim)/dynamic_update_slice | solution.py:251
  454.3 48.3 %select_reduce_fusion.5 = f32[128,8000]{0,1:T(8,128)S(1)} fusion(f32[128,64]{0,1:T(8,128)S(1)} %bitcast.244, s32[128,64]{0,1:T(8,128)S(1)} %dynamic-slice_bitcast_fusion.2), kind=kLoop, calls=%fused_computation.16.clone.1 | loop fusion | flops 195584000 | bytes 4161536 | tf_op jit(solution)/shard_map/while/body/eval_jaxpr/reduce_sum | solution.py:241
  505.1 98.1 %dynamic_update_slice.18 = f32[2,128,8000]{1,0,2:T(2,128)} dynamic-update-slice(f32[2,128,8000]{1,0,2:T(2,128)} %get-tuple-element.518, f32[1,128,8000]{1,0,2:T(1,128)} %bitcast.229, s32[]{:T(128)S(6)} %copy.333, s32[]{:T(128)} %constant.298.clone.1..sunk, s32[]{:T(128)} %constant.298.clone.1..sunk) | dynamic-update-slice | bytes 8192004 | tf_op jit(solution)/shard_map/while/body/jit(dynamic_update_index_in_dim)/dynamic_update_slice | solution.py:251
  603.3 51.9 %scatter_custom_fusion = bf16[1536,768]{1,0:T(8,128)(2,1)S(1)} fusion(s32[4096]{0:T(1024)S(1)} %bitcast.281, pred[4096]{0:T(1024)(128)(4,1)S(1)} %compare_and_fusion.1, bf16[]{:T(256)} %constant.322.clone.1, bf16[]{:T(256)} %constant.316.clone.1, bf16[2048,768]{1,0:T(8,128)(2,1)} %all-gather.18.cloned.1.call-done, s32[4096]{0:T(1024)S(1)} %broadcast_clamp_fusion), kind=kCustom, calls=%fused_computation.56 | custom fusion | flops 3145728 | bytes 5525508 | tf_op jit(solution)/shard_map/scatter | solution.py:191
  655.2 15.2 fusion.106
  670.4 15.2 convolution_convert_fusion.2
  691.9 6.5 gather_fusion.3
  699.6 19.7 all-to-all-done
  719.2 5.2 gather_fusion
  728.1 6.5 multiply_reduce_fusion.2
  736.5 10.3 all_gather.48
  746.8 8.8 fusion.105
  758.9 7.1 all-gather.5
  766.0 8.0 all-gather.4
  774.1 550.0 %gather_fusion.5 = f32[16384]{0:T(1024)S(1)} fusion(f32[256,8000]{0,1:T(8,128)} %copy-done, s32[16384]{0:T(1024)S(1)} %copy-done.1), kind=kCustom, calls=%fused_computation.6 | custom fusion | bytes 262144 | tf_op jit(solution)/shard_map/jit(take_along_axis)/gather | solution.py:220
  1324.1 7.4 gather_fusion.4
  1331.8 53.6 %all-gather.6 = f32[4,1,256]{2,1,0:T(1,128)S(1)} all-gather(f32[1,1,256]{2,1,0:T(1,128)S(1)} %bitcast.291), channel_id=4, replica_groups=mesh['dp'=8,'expert'=4] {'expert'}, dimensions={0}, use_global_device_ids=true | all-gather | bytes 5120 | tf_op jit(solution)/shard_map/all_gather | solution.py:20
  1386.2 7.6 fusion.17
  1395.8 7.4 fusion.107
  1404.0 23.3 %reduce-scatter.8.cloned.1.call-done = f32[64,768]{1,0:T(8,128)} async-done(((f32[256,768]{1,0:T(8,128)}), f32[64,768]{1,0:T(8,128)}) %reduce-scatter.8.cloned.1.call-update) | async-done | bytes 196624 | tf_op jit(solution)/shard_map/reduce_scatter | solution.py:264
  1438.8 7.4 scatter_custom_fusion.2
  1446.2 32.2 %all_to_all.45 = bf16[4,2,192,768]{3,2,1,0:T(8,128)(2,1)S(1)} all-to-all(bf16[4,2,192,768]{3,2,1,0:T(8,128)(2,1)} %bitcast.236), channel_id=1, replica_groups=mesh['dp'=8,'expert'=4] {'expert'}, dimensions={0} | all-to-all | bytes 4718592 | tf_op jit(solution)/shard_map/all_to_all | solution.py:288
  1480.0 22.0 fusion.13
  1502.0 11.5 fusion.108
  1524.2 48.8 %all-to-all-done.2 = f32[2,4,192,768]{3,2,0,1:T(8,128)} async-done(((f32[2,4,192,768]{3,2,0,1:T(8,128)}), f32[2,4,192,768]{3,2,0,1:T(8,128)}, u32[]{:S(2)}, u32[]{:S(2)}) %all-to-all-start.2) | async-done | bytes 4718624 | tf_op jit(solution)/shard_map/all_to_all | solution.py:306
  1573.0 8.2 gather_fusion.2
  1585.0 16.0 select_reduce_fusion.1
  1605.7 7.3 fusion.54
  1613.0 10.0 multiply_reduce_fusion
  1623.0 7.1 multiply_convert_fusion.1
  1648.4 17.0 convolution_convert_fusion
  1667.0 13.4 convolution_convert_fusion.1
  1681.4 13.2 fusion.109
  1694.7 37.9 %add_convert_fusion = bf16[8000,768]{0,1:T(8,128)(2,1)} fusion(f32[8000,768]{0,1:T(8,128)} %fusion.109, bf16[2048,768]{1,0:T(8,128)(2,1)} %all-gather.24.cloned.1.call-done, s32[2048]{0:T(1024)S(1)} %bitcast.288), kind=kOutput, calls=%fused_computation.30 | convolution fusion | flops 25194496000 | bytes 40017920 | tf_op jit(solution)/shard_map/while/body/eval_jaxpr/tv,td->vd/dot_general | solution.py:382
  1740.9 41.1 %all-reduce = (f32[]{:T(128)}, f32[11,768]{1,0:T(8,128)S(1)}) all-reduce(f32[]{:T(128)S(6)} %div.101, f32[11,768]{1,0:T(8,128)S(1)} %pad_maximum_fusion.4), channel_id=1, replica_groups=mesh['dp'=8,'expert'=4] {'dp','expert'}, use_global_device_ids=true, to_apply=%region_23.24 | all-reduce | flops 8449 | bytes 67592 | tf_op jit(solution)/shard_map/psum | solution.py:404
  1783.3 95.7 %all-reduce.3.cloned.1.call-done = f32[4,768,768]{1,2,0:T(8,128)} async-done(((f32[4,768,768]{1,2,0:T(8,128)}), f32[4,768,768]{1,2,0:T(8,128)}) %all-reduce.3.cloned.1.call-update) | async-done | bytes 9437200 | tf_op jit(solution)/shard_map/psum | solution.py:404
  1895.1 85.7 %reduce-scatter.12.cloned.1.call-done = bf16[2,384,768]{2,1,0:T(8,128)(2,1)} async-done(((bf16[2,3072,768]{2,1,0:T(8,128)(2,1)}), bf16[2,384,768]{2,1,0:T(8,128)(2,1)}) %reduce-scatter.12.cloned.1.call-update) | async-done | bytes 1179664 | tf_op jit(solution)/shard_map/reduce_scatter | solution.py:395
  1988.5 92.6 %reduce-scatter.10.cloned.1.call-done = bf16[2,96,3072]{2,1,0:T(8,128)(2,1)} async-done(((bf16[2,768,3072]{2,1,0:T(8,128)(2,1)}), bf16[2,96,3072]{2,1,0:T(8,128)(2,1)}) %reduce-scatter.10.cloned.1.call-update) | async-done | bytes 1179664 | tf_op jit(solution)/shard_map/reduce_scatter | solution.py:392
  2088.9 120.2 %reduce-scatter.14.cloned.1.call-done = bf16[8000,96]{0,1:T(8,128)(2,1)} async-done(((bf16[8000,768]{0,1:T(8,128)(2,1)}), bf16[8000,96]{0,1:T(8,128)(2,1)}) %reduce-scatter.14.cloned.1.call-update) | async-done | bytes 1536016 | tf_op jit(solution)/shard_map/reduce_scatter | solution.py:398
  2209.2 5.4 fusion.96
  (438 shorter events, 163.9 us)
Async XLA Ops:
  7.2 121.2 %all-gather.14.cloned.1.call-start = ((), (), s32[]{:S(2)}) async-start(), calls=%async_computation.8 | async-start | bytes 13934592 | tf_op jit(solution)/shard_map/all_gather | solution.py:121
  10.4 196.0 %reduce-scatter.6.cloned.1.call-start = ((), (), s32[]{:S(2)}) async-start(), calls=%async_computation.9 | async-start | bytes 3932160 | tf_op jit(solution)/shard_map/reduce_scatter | solution.py:136
  10.5 117.9 %copy-start.91 = (s32[1,4,4,128]{3,1,2,0:T(4,128)}, s32[1,4,4,128]{3,1,2,0:T(4,128)S(1)}, u32[]{:S(2)}) copy-start(s32[1,4,4,128]{3,1,2,0:T(4,128)S(1)} %copy.300) | copy-start | bytes 24580
  164.1 17.2 copy-start.86
  164.1 96.2 %all-gather.16.cloned.1.call-start = ((), (), s32[]{:S(2)}) async-start(), calls=%async_computation.10 | async-start | bytes 5308416 | tf_op jit(solution)/shard_map/all_gather | solution.py:115
  166.3 437.0 %all-gather.18.cloned.1.call-start = ((), (), s32[]{:S(2)}) async-start(), calls=%async_computation.11 | async-start | bytes 3932160 | tf_op jit(solution)/shard_map/all_gather | solution.py:177
  180.6 510.9 %copy-start.57 = (bf16[768,11]{0,1:T(8,128)(2,1)}, bf16[768,11]{0,1:T(8,128)(2,1)S(1)}, u32[]{:S(2)}) copy-start(bf16[768,11]{0,1:T(8,128)(2,1)S(1)} %reshape.708) | copy-start | bytes 50692
  181.3 83.4 %copy-start.82 = (f32[768]{0:T(1024)}, f32[768]{0:T(1024)S(1)}, u32[]{:S(2)}) copy-start(f32[768]{0:T(1024)S(1)} %get-tuple-element.331) | copy-start | bytes 9220
  181.3 95.4 %copy-start.61 = (f32[768]{0:T(1024)}, f32[768]{0:T(1024)S(1)}, u32[]{:S(2)}) copy-start(f32[768]{0:T(1024)S(1)} %get-tuple-element.330) | copy-start | bytes 9220
  181.5 89.0 %copy-start.22 = (pred[512,512]{0,1:T(8,128)(4,1)}, pred[512,512]{0,1:T(8,128)(4,1)S(1)}, u32[]{:S(2)}) copy-start(pred[512,512]{0,1:T(8,128)(4,1)S(1)} %fusion.60) | copy-start | bytes 786436
  207.9 56.8 %copy-start.87 = (f32[512]{0:T(512)}, f32[512]{0:T(512)S(1)}, u32[]{:S(2)}) copy-start(f32[512]{0:T(512)S(1)} %add_rsqrt_fusion.2) | copy-start | bytes 6148
  278.9 376.3 %all-gather.20.cloned.1.call-start = ((), (), s32[]{:S(2)}) async-start(), calls=%async_computation.12 | async-start | bytes 10616832 | tf_op jit(solution)/shard_map/all_gather | solution.py:119
  282.0 388.4 %all-gather.22.cloned.1.call-start = ((), (), s32[]{:S(2)}) async-start(), calls=%async_computation.13 | async-start | bytes 10616832 | tf_op jit(solution)/shard_map/all_gather | solution.py:120
  285.1 413.6 %copy-start.53 = (s32[512,2]{0,1:T(2,128)}, s32[512,2]{0,1:T(2,128)S(1)}, u32[]{:S(2)}) copy-start(s32[512,2]{0,1:T(2,128)S(1)} %get-tuple-element.384) | copy-start | bytes 12292
  287.0 17.0 copy-start.40
  687.1 32.1 %all-to-all-start = ((bf16[2,4,192,768]{3,2,0,1:T(8,128)(2,1)}), bf16[2,4,192,768]{3,2,0,1:T(8,128)(2,1)S(1)}, u32[]{:S(2)}, u32[]{:S(2)}) async-start(bf16[2,4,192,768]{3,2,0,1:T(8,128)(2,1)} %copy.236), calls=%async_computation.1 | async-start | bytes 4718592 | tf_op jit(solution)/shard_map/all_to_all | solution.py:199
  691.0 736.3 %reduce-scatter.8.cloned.1.call-start = ((), (), s32[]{:S(2)}) async-start(), calls=%async_computation.14 | async-start | bytes 983040 | tf_op jit(solution)/shard_map/reduce_scatter | solution.py:264
  691.6 27.7 %copy-start.68 = (s32[1024]{0:T(1024)}, s32[1024]{0:T(1024)S(1)}, u32[]{:S(2)}) copy-start(s32[1024]{0:T(1024)S(1)} %broadcast_clamp_fusion.1) | copy-start | bytes 12292
  699.4 25.1 %copy-start.71 = (f32[512]{0:T(512)}, f32[512]{0:T(512)S(1)}, u32[]{:S(2)}) copy-start(f32[512]{0:T(512)S(1)} %fusion.83) | copy-start | bytes 6148
  699.6 28.5 %copy-start.38 = (f32[512,2]{1,0:T(8,128)}, f32[512,2]{1,0:T(8,128)S(1)}, u32[]{:S(2)}) copy-start(f32[512,2]{1,0:T(8,128)S(1)} %copy.225) | copy-start | bytes 12292
  755.6 18.4 copy-start.1
  774.0 557.6 %copy-start.41 = (s32[256,64]{1,0:T(8,128)S(1)}, s32[256,64]{1,0:T(8,128)}, u32[]{:S(2)}) copy-start(s32[256,64]{1,0:T(8,128)} %copy-done.40) | copy-start | bytes 196612
  774.0 557.6 %copy-start.47 = (f32[256,64]{1,0:T(8,128)S(1)}, f32[256,64]{1,0:T(8,128)}, u32[]{:S(2)}) copy-start(f32[256,64]{1,0:T(8,128)} %copy.239) | copy-start | bytes 196612
  774.0 557.7 %copy-start.96 = (s32[256]{0:T(256)S(1)}, s32[256]{0:T(256)}, u32[]{:S(2)}) copy-start(s32[256]{0:T(256)} %param.30) | copy-start | bytes 3076
  774.0 611.6 %copy-start.94 = (f32[256]{0:T(256)S(1)}, f32[256]{0:T(256)}, u32[]{:S(2)}) copy-start(f32[256]{0:T(256)} %fusion.71) | copy-start | bytes 3076
  1395.8 33.7 %copy-start.64 = (f32[768]{0:T(1024)S(1)}, f32[768]{0:T(1024)}, u32[]{:S(2)}) copy-start(f32[768]{0:T(1024)} %get-tuple-element.329) | copy-start | bytes 9220
  1395.8 33.7 %copy-start.78 = (f32[512]{0:T(512)S(1)}, f32[512]{0:T(512)}, u32[]{:S(2)}) copy-start(f32[512]{0:T(512)} %copy-done.77) | copy-start | bytes 6148
  1516.1 56.9 %all-to-all-start.2 = ((f32[2,4,192,768]{3,2,0,1:T(8,128)}), f32[2,4,192,768]{3,2,0,1:T(8,128)}, u32[]{:S(2)}, u32[]{:S(2)}) async-start(f32[2,4,192,768]{3,2,0,1:T(8,128)} %copy.248), calls=%async_computation.4 | async-start | bytes 9437184 | tf_op jit(solution)/shard_map/all_to_all | solution.py:306
  1521.2 51.8 %copy-start.69 = (s32[1024]{0:T(1024)S(1)}, s32[1024]{0:T(1024)}, u32[]{:S(2)}) copy-start(s32[1024]{0:T(1024)} %copy-done.68) | copy-start | bytes 12292
  1521.2 173.5 %all-gather.24.cloned.1.call-start = ((), (), s32[]{:S(2)}) async-start(), calls=%async_computation.18 | async-start | bytes 3932160 | tf_op jit(solution)/shard_map/all_gather | solution.py:377
  1524.2 76.7 %copy-start.51 = (f32[512,8]{0,1:T(8,128)}, f32[512,8]{0,1:T(8,128)S(1)}, u32[]{:S(2)}) copy-start(f32[512,8]{0,1:T(8,128)S(1)} %select_reduce_fusion.3) | copy-start | bytes 49156
  1584.9 16.0 copy-start.5
  1585.0 16.0 copy-start.58
  1585.0 16.0 copy-start.62
  1585.0 16.0 copy-start.76
  1605.7 17.3 slice-start
  1605.7 17.3 slice-start.1
  1637.9 241.1 %all-reduce.3.cloned.1.call-start = ((), (), s32[]{:S(2)}) async-start(), calls=%async_computation.15 | async-start | bytes 18874368 | tf_op jit(solution)/shard_map/psum | solution.py:404
  1646.8 334.1 %reduce-scatter.12.cloned.1.call-start = ((), (), s32[]{:S(2)}) async-start(), calls=%async_computation.17 | async-start | bytes 10616832 | tf_op jit(solution)/shard_map/reduce_scatter | solution.py:395
  1665.4 415.7 %reduce-scatter.10.cloned.1.call-start = ((), (), s32[]{:S(2)}) async-start(), calls=%async_computation.16 | async-start | bytes 10616832 | tf_op jit(solution)/shard_map/reduce_scatter | solution.py:392
  1680.5 528.7 %reduce-scatter.14.cloned.1.call-start = ((), (), s32[]{:S(2)}) async-start(), calls=%async_computation.19 | async-start | bytes 13934592 | tf_op jit(solution)/shard_map/reduce_scatter | solution.py:398
  1735.6 46.4 %copy-start.74 = (f32[11,96]{1,0:T(8,128)S(1)}, f32[11,96]{1,0:T(8,128)}, u32[]{:S(2)}) copy-start(f32[11,96]{1,0:T(8,128)} %param.45) | copy-start | bytes 12676
  1735.6 46.4 %copy-start.93 = (f32[11,96]{1,0:T(8,128)S(1)}, f32[11,96]{1,0:T(8,128)}, u32[]{:S(2)}) copy-start(f32[11,96]{1,0:T(8,128)} %param.46) | copy-start | bytes 12676
  1735.6 47.1 %copy-start.89 = (f32[11,96]{1,0:T(8,128)S(1)}, f32[11,96]{1,0:T(8,128)}, u32[]{:S(2)}) copy-start(f32[11,96]{1,0:T(8,128)} %param.47) | copy-start | bytes 12676
  1782.7 101.1 %copy-start.70 = (f32[11,96]{1,0:T(8,128)}, f32[11,96]{1,0:T(8,128)S(1)}, u32[]{:S(2)}) copy-start(f32[11,96]{1,0:T(8,128)S(1)} %get-tuple-element.361) | copy-start | bytes 12676
  1886.5 94.3 %copy-start.18 = (f32[2,384,768]{2,1,0:T(8,128)S(1)}, f32[2,384,768]{2,1,0:T(8,128)}, u32[]{:S(2)}) copy-start(f32[2,384,768]{2,1,0:T(8,128)} %param.39) | copy-start | bytes 7077892
  1986.8 94.3 %copy-start.19 = (f32[2,96,3072]{2,1,0:T(8,128)S(1)}, f32[2,96,3072]{2,1,0:T(8,128)}, u32[]{:S(2)}) copy-start(f32[2,96,3072]{2,1,0:T(8,128)} %param.36) | copy-start | bytes 7077892
  2087.1 122.0 %copy-start.12 = (f32[8000,96]{0,1:T(8,128)S(1)}, f32[8000,96]{0,1:T(8,128)}, u32[]{:S(2)}) copy-start(f32[8000,96]{0,1:T(8,128)} %param.42) | copy-start | bytes 9216004
  (74 other events, 268.8 us)
Sparse Core Ops, SparseCore 0:
  10.6 117.8 all-gather.13
  164.3 42.1 reduce-scatter.5
  208.7 51.6 all-gather.15
  279.0 42.8 all-gather.17
  323.9 90.7 all-gather.19
  416.7 89.1 all-gather.21
  1403.4 23.8 reduce-scatter.7
  1638.0 43.9 all-gather.23
  1687.8 191.1 all-reduce.2
  1881.2 99.5 reduce-scatter.11
  1983.2 97.8 reduce-scatter.9
  2083.4 125.6 reduce-scatter.13
where the time goes:
time: 2230 us; the launch traced here: 2220 us
  local copies, waits for them, and re-layouts  838 us (38%)
  waiting for transfers between devices  681 us (31%)
  other arithmetic  270 us (12%)
  matrix products  242 us (11%)
  blocking collectives  166 us (7%)
    gather x3, local copies, waits for them, and re-layouts, shards(): jnp.take_along_axis(logits, jnp.clip(teacher_local, 0, vocab_rows - 1), a...  551 us
    dynamic_update_slice x2, local copies, waits for them, and re-layouts, shards(): lax.map(target_block, (target_local.reshape(-1, target_rows), teacher_loc...  196 us
    reduce_scatter x1, waiting for transfers between devices, shards(): lax.psum_scatter(embed_grad.astype(jnp.bfloat16), 'dp', scatter_dimension...  120 us
    all_gather x1, waiting for transfers between devices, shards(): lax.all_gather(embedding.astype(jnp.bfloat16), 'dp', axis=1, tiled=True)  118 us
    reduce_sum x2, other arithmetic, target_block(): jnp.sum(jnp.where(teacher_block_ids[:, :, None] == vocab_iota[None, None,...  96.5 us
    psum x1, waiting for transfers between devices, shards(): lax.psum((attention_grad, small_grad, loss_part), ('dp', 'expert'))  95.7 us
    reduce_scatter x1, waiting for transfers between devices, shards(): lax.psum_scatter(in_grad.astype(jnp.bfloat16), 'dp', scatter_dimension=1,...  92.6 us
    reduce_scatter x1, waiting for transfers between devices, shards(): lax.psum_scatter(out_grad.astype(jnp.bfloat16), 'dp', scatter_dimension=1...  85.7 us
  transfers between devices with their start and end apart: 14, of which 10 were waited for; matrix products, arithmetic and copies ran while one was open for 24% of the time, Pallas kernels for 0%

commit v1 on v0

--- a/solution.py
+++ b/solution.py
@@ -39,8 +39,10 @@
 def slot_table(block_routes, experts):
     flat = block_routes.reshape(-1)
     hits = (flat[:, None] == jnp.arange(experts, dtype=jnp.int32)[None, :]).astype(jnp.int32)
-    before = jnp.cumsum(hits, axis=0) - hits
-    return (flat, jnp.sum(before * hits, axis=1))
+    place = jnp.arange(flat.shape[0], dtype=jnp.int32)
+    earlier = (place[None, :] < place[:, None]).astype(jnp.bfloat16)
+    before = jnp.dot(earlier, hits.astype(jnp.bfloat16), preferred_element_type=jnp.float32)
+    return (flat, jnp.sum(before.astype(jnp.int32) * hits, axis=1))
 
 
 def block_scores(query, keys, seg_ids, block_index, length, block_rows, scaling):

time: 2230 us -> 2240 us (level)
  local copies, waits for them, and re-layouts: 838 us -> 887 us
  blocking collectives: 166 us -> 119 us
    gather x3, local copies, waits for them, and re-layouts: 551 us -> 601 us  [shards(): jnp.take_along_axis(logits, jnp.clip(teacher_local, 0, vocab_rows - 1), a...]
    all_gather x3, blocking collectives: 68.7 us -> 21.4 us  [combined_all(): pieces = jax.tree.map(lambda part: lax.all_gather(part, axis), value)]
  transfers between devices with their start and end apart: 14 -> 14, of which waited for: 10 -> 10; matrix products, arithmetic and copies ran while one was open for 24% -> 23% of each run, Pallas kernels for 0% -> 0%
where the time goes in v1:
time: 2240 us; the launch traced here: 2220 us
  local copies, waits for them, and re-layouts  887 us (40%)
  waiting for transfers between devices  683 us (30%)
  other arithmetic  257 us (11%)
  matrix products  242 us (11%)
  blocking collectives  119 us (5%)
    gather x3, local copies, waits for them, and re-layouts, shards(): jnp.take_along_axis(logits, jnp.clip(teacher_local, 0, vocab_rows - 1), a...  601 us
    dynamic_update_slice x2, local copies, waits for them, and re-layouts, shards(): lax.map(target_block, (target_local.reshape(-1, target_rows), teacher_loc...  196 us
    reduce_scatter x1, waiting for transfers between devices, shards(): lax.psum_scatter(embed_grad.astype(jnp.bfloat16), 'dp', scatter_dimension...  120 us
    all_gather x1, waiting for transfers between devices, shards(): lax.all_gather(embedding.astype(jnp.bfloat16), 'dp', axis=1, tiled=True)  118 us
    reduce_sum x2, other arithmetic, target_block(): jnp.sum(jnp.where(teacher_block_ids[:, :, None] == vocab_iota[None, None,...  96.5 us
    psum x1, waiting for transfers between devices, shards(): lax.psum((attention_grad, small_grad, loss_part), ('dp', 'expert'))  95.7 us
    reduce_scatter x1, waiting for transfers between devices, shards(): lax.psum_scatter(in_grad.astype(jnp.bfloat16), 'dp', scatter_dimension=1,...  92.6 us
    reduce_scatter x1, waiting for transfers between devices, shards(): lax.psum_scatter(out_grad.astype(jnp.bfloat16), 'dp', scatter_dimension=1...  85.7 us
  transfers between devices with their start and end apart: 14, of which 10 were waited for; matrix products, arithmetic and copies ran while one was open for 23% of the time, Pallas kernels for 0%

profile of v1, /device:TPU:0, one launch (start us, length us, event | category | flops | bytes accessed | tf_op | source)
XLA Modules:
  0.0 2215.3 jit_solution(16382387263972116120)
XLA Ops:
  10.6 117.9 %all-gather.14.cloned.1.call-done = bf16[8000,768]{0,1:T(8,128)(2,1)} async-done(((bf16[8000,96]{0,1:T(8,128)(2,1)}), bf16[8000,768]{0,1:T(8,128)(2,1)}) %all-gather.14.cloned.1.call-update) | async-done | bytes 12288016 | tf_op jit(solution)/shard_map/all_gather | solution.py:123
  128.4 35.7 %fusion.28 = bf16[2048,768]{1,0:T(8,128)(2,1)} fusion(bf16[8000,768]{0,1:T(8,128)(2,1)} %all-gather.14.cloned.1.call-done, s32[2048]{0:T(1024)S(1)} %bitcast.276), kind=kOutput, calls=%fused_computation.66 | convolution fusion | flops 25183780864 | bytes 15441920 | tf_op jit(solution)/shard_map/while/body/eval_jaxpr/dot_general | solution.py:135
  166.4 14.2 all-gather.3
  181.5 25.0 %reduce-scatter.6.cloned.1.call-done = bf16[512,768]{1,0:T(8,128)(2,1)} async-done(((bf16[2048,768]{1,0:T(8,128)(2,1)}), bf16[512,768]{1,0:T(8,128)(2,1)}) %reduce-scatter.6.cloned.1.call-update) | async-done | bytes 786448 | tf_op jit(solution)/shard_map/reduce_scatter | solution.py:138
  207.9 52.5 %all-gather.16.cloned.1.call-done = bf16[4,768,768]{2,1,0:T(8,128)(2,1)} async-done(((bf16[4,96,768]{2,1,0:T(8,128)(2,1)}), bf16[4,768,768]{2,1,0:T(8,128)(2,1)}) %all-gather.16.cloned.1.call-update) | async-done | bytes 4718608 | tf_op jit(solution)/shard_map/all_gather | solution.py:117
  292.5 298.1 %while.7 = (s32[]{:T(128)}, f32[2,128,8000]{1,0,2:T(2,128)}, s32[2,128]{1,0:T(2,128)S(1)}, s32[2,128,64]{1,2,0:T(8,128)S(1)}, f32[2,128,64]{1,0,2:T(2,128)S(1)}, /*index=5*/s32[]{:T(128)}, s32[]{:T(128)}) while((s32[]{:T(128)}, f32[2,128,8000]{1,0,2:T(2,128)}, s32[2,128]{1,0:T(2,128)S(1)}, ...), condition=%wide.region_22.23_spmd.clone.clone, body=%wide.region_20.22_spmd.clone.clone.sunk | while | flops 198656000 | bytes 20678244 | solution.py:253
  292.5 48.3 %select_reduce_fusion.5 = f32[128,8000]{0,1:T(8,128)S(1)} fusion(f32[128,64]{0,1:T(8,128)S(1)} %bitcast.234, s32[128,64]{0,1:T(8,128)S(1)} %dynamic-slice_bitcast_fusion.2), kind=kLoop, calls=%fused_computation.16.clone.1 | loop fusion | flops 195584000 | bytes 4161536 | tf_op jit(solution)/shard_map/while/body/eval_jaxpr/reduce_sum | solution.py:243
  343.3 98.2 %dynamic_update_slice.18 = f32[2,128,8000]{1,0,2:T(2,128)} dynamic-update-slice(f32[2,128,8000]{1,0,2:T(2,128)} %get-tuple-element.518, f32[1,128,8000]{1,0,2:T(1,128)} %bitcast.221, s32[]{:T(128)S(6)} %copy.319, s32[]{:T(128)} %constant.224.clone.1..sunk, s32[]{:T(128)} %constant.224.clone.1..sunk) | dynamic-update-slice | bytes 8192004 | tf_op jit(solution)/shard_map/while/body/jit(dynamic_update_index_in_dim)/dynamic_update_slice | solution.py:253
  441.6 48.3 %select_reduce_fusion.5 = f32[128,8000]{0,1:T(8,128)S(1)} fusion(f32[128,64]{0,1:T(8,128)S(1)} %bitcast.234, s32[128,64]{0,1:T(8,128)S(1)} %dynamic-slice_bitcast_fusion.2), kind=kLoop, calls=%fused_computation.16.clone.1 | loop fusion | flops 195584000 | bytes 4161536 | tf_op jit(solution)/shard_map/while/body/eval_jaxpr/reduce_sum | solution.py:243
  492.4 98.2 %dynamic_update_slice.18 = f32[2,128,8000]{1,0,2:T(2,128)} dynamic-update-slice(f32[2,128,8000]{1,0,2:T(2,128)} %get-tuple-element.518, f32[1,128,8000]{1,0,2:T(1,128)} %bitcast.221, s32[]{:T(128)S(6)} %copy.319, s32[]{:T(128)} %constant.224.clone.1..sunk, s32[]{:T(128)} %constant.224.clone.1..sunk) | dynamic-update-slice | bytes 8192004 | tf_op jit(solution)/shard_map/while/body/jit(dynamic_update_index_in_dim)/dynamic_update_slice | solution.py:253
  590.6 51.9 %scatter_custom_fusion = bf16[1536,768]{1,0:T(8,128)(2,1)S(1)} fusion(s32[4096]{0:T(1024)S(1)} %bitcast.270, pred[4096]{0:T(1024)(128)(4,1)S(1)} %compare_and_fusion.1, bf16[]{:T(256)} %constant.316.clone.1, bf16[]{:T(256)} %constant.310.clone.1, bf16[2048,768]{1,0:T(8,128)(2,1)} %all-gather.18.cloned.1.call-done, s32[4096]{0:T(1024)S(1)} %broadcast_clamp_fusion), kind=kCustom, calls=%fused_computation.56 | custom fusion | flops 3145728 | bytes 5525508 | tf_op jit(solution)/shard_map/scatter | solution.py:193
  642.6 15.0 fusion.113
  657.6 15.2 convolution_convert_fusion.2
  679.1 6.5 gather_fusion.3
  686.7 19.7 all-to-all-done
  706.4 5.2 gather_fusion
  715.3 6.5 multiply_reduce_fusion.2
  723.7 10.3 all_gather.48
  734.0 8.9 fusion.112
  746.1 7.1 all-gather.5
  753.3 8.0 all-gather.4
  761.3 600.6 %gather_fusion.5 = f32[16384]{0:T(1024)S(1)} fusion(f32[256,8000]{0,1:T(8,128)} %copy-done, s32[16384]{0:T(1024)S(1)} %copy-done.1), kind=kCustom, calls=%fused_computation.6 | custom fusion | bytes 262144 | tf_op jit(solution)/shard_map/jit(take_along_axis)/gather | solution.py:222
  1361.9 6.8 gather_fusion.4
  1369.0 6.3 all-gather.6
  1376.1 7.6 fusion.17
  1385.7 7.4 fusion.114
  1393.9 24.4 %reduce-scatter.8.cloned.1.call-done = f32[64,768]{1,0:T(8,128)} async-done(((f32[256,768]{1,0:T(8,128)}), f32[64,768]{1,0:T(8,128)}) %reduce-scatter.8.cloned.1.call-update) | async-done | bytes 196624 | tf_op jit(solution)/shard_map/reduce_scatter | solution.py:266
  1429.8 7.4 scatter_custom_fusion.2
  1437.2 32.2 %all_to_all.45 = bf16[4,2,192,768]{3,2,1,0:T(8,128)(2,1)S(1)} all-to-all(bf16[4,2,192,768]{3,2,1,0:T(8,128)(2,1)} %bitcast.228), channel_id=1, replica_groups=mesh['dp'=8,'expert'=4] {'expert'}, dimensions={0} | all-to-all | bytes 4718592 | tf_op jit(solution)/shard_map/all_to_all | solution.py:290
  1471.0 22.0 fusion.13
  1493.0 11.5 fusion.115
  1507.0 5.1 all-to-all-start.2
  1515.2 48.8 %all-to-all-done.2 = f32[2,4,192,768]{3,2,0,1:T(8,128)} async-done(((f32[2,4,192,768]{3,2,0,1:T(8,128)}), f32[2,4,192,768]{3,2,0,1:T(8,128)}, u32[]{:S(2)}, u32[]{:S(2)}) %all-to-all-start.2) | async-done | bytes 4718624 | tf_op jit(solution)/shard_map/all_to_all | solution.py:308
  1564.0 8.2 gather_fusion.2
  1575.9 16.0 select_reduce_fusion.1
  1596.6 7.3 fusion.56
  1604.0 10.0 multiply_reduce_fusion
  1614.0 7.1 multiply_convert_fusion.1
  1639.4 16.9 convolution_convert_fusion
  1657.9 13.5 convolution_convert_fusion.1
  1672.4 13.2 fusion.116
  1685.6 37.8 %add_convert_fusion = bf16[8000,768]{0,1:T(8,128)(2,1)} fusion(f32[8000,768]{0,1:T(8,128)} %fusion.116, bf16[2048,768]{1,0:T(8,128)(2,1)} %all-gather.24.cloned.1.call-done, s32[2048]{0:T(1024)S(1)} %bitcast.277), kind=kOutput, calls=%fused_computation.30 | convolution fusion | flops 25194496000 | bytes 40017920 | tf_op jit(solution)/shard_map/while/body/eval_jaxpr/tv,td->vd/dot_general | solution.py:384
  1731.7 41.3 %all-reduce = (f32[]{:T(128)}, f32[11,768]{1,0:T(8,128)S(1)}) all-reduce(f32[]{:T(128)S(6)} %div.101, f32[11,768]{1,0:T(8,128)S(1)} %pad_maximum_fusion.4), channel_id=1, replica_groups=mesh['dp'=8,'expert'=4] {'dp','expert'}, use_global_device_ids=true, to_apply=%region_19.20 | all-reduce | flops 8449 | bytes 67592 | tf_op jit(solution)/shard_map/psum | solution.py:406
  1774.3 95.7 %all-reduce.3.cloned.1.call-done = f32[4,768,768]{1,2,0:T(8,128)} async-done(((f32[4,768,768]{1,2,0:T(8,128)}), f32[4,768,768]{1,2,0:T(8,128)}) %all-reduce.3.cloned.1.call-update) | async-done | bytes 9437200 | tf_op jit(solution)/shard_map/psum | solution.py:406
  1886.1 85.7 %reduce-scatter.12.cloned.1.call-done = bf16[2,384,768]{2,1,0:T(8,128)(2,1)} async-done(((bf16[2,3072,768]{2,1,0:T(8,128)(2,1)}), bf16[2,384,768]{2,1,0:T(8,128)(2,1)}) %reduce-scatter.12.cloned.1.call-update) | async-done | bytes 1179664 | tf_op jit(solution)/shard_map/reduce_scatter | solution.py:397
  1979.5 92.6 %reduce-scatter.10.cloned.1.call-done = bf16[2,96,3072]{2,1,0:T(8,128)(2,1)} async-done(((bf16[2,768,3072]{2,1,0:T(8,128)(2,1)}), bf16[2,96,3072]{2,1,0:T(8,128)(2,1)}) %reduce-scatter.10.cloned.1.call-update) | async-done | bytes 1179664 | tf_op jit(solution)/shard_map/reduce_scatter | solution.py:394
  2079.9 120.2 %reduce-scatter.14.cloned.1.call-done = bf16[8000,96]{0,1:T(8,128)(2,1)} async-done(((bf16[8000,768]{0,1:T(8,128)(2,1)}), bf16[8000,96]{0,1:T(8,128)(2,1)}) %reduce-scatter.14.cloned.1.call-update) | async-done | bytes 1536016 | tf_op jit(solution)/shard_map/reduce_scatter | solution.py:400
  2200.1 5.4 fusion.103
  (425 shorter events, 155.1 us)
Async XLA Ops:
  7.2 121.2 %all-gather.14.cloned.1.call-start = ((), (), s32[]{:S(2)}) async-start(), calls=%async_computation.8 | async-start | bytes 13934592 | tf_op jit(solution)/shard_map/all_gather | solution.py:123
  10.4 196.1 %reduce-scatter.6.cloned.1.call-start = ((), (), s32[]{:S(2)}) async-start(), calls=%async_computation.9 | async-start | bytes 3932160 | tf_op jit(solution)/shard_map/reduce_scatter | solution.py:138
  10.5 117.9 %copy-start.91 = (s32[1,4,4,128]{3,1,2,0:T(4,128)}, s32[1,4,4,128]{3,1,2,0:T(4,128)S(1)}, u32[]{:S(2)}) copy-start(s32[1,4,4,128]{3,1,2,0:T(4,128)S(1)} %copy.288) | copy-start | bytes 24580
  164.1 17.2 copy-start.86
  164.2 96.2 %all-gather.16.cloned.1.call-start = ((), (), s32[]{:S(2)}) async-start(), calls=%async_computation.10 | async-start | bytes 5308416 | tf_op jit(solution)/shard_map/all_gather | solution.py:117
  166.3 424.3 %all-gather.18.cloned.1.call-start = ((), (), s32[]{:S(2)}) async-start(), calls=%async_computation.11 | async-start | bytes 3932160 | tf_op jit(solution)/shard_map/all_gather | solution.py:179
  180.7 498.1 %copy-start.57 = (bf16[768,11]{0,1:T(8,128)(2,1)}, bf16[768,11]{0,1:T(8,128)(2,1)S(1)}, u32[]{:S(2)}) copy-start(bf16[768,11]{0,1:T(8,128)(2,1)S(1)} %reshape.679) | copy-start | bytes 50692
  181.3 83.4 %copy-start.82 = (f32[768]{0:T(1024)}, f32[768]{0:T(1024)S(1)}, u32[]{:S(2)}) copy-start(f32[768]{0:T(1024)S(1)} %get-tuple-element.331) | copy-start | bytes 9220
  181.3 95.4 %copy-start.61 = (f32[768]{0:T(1024)}, f32[768]{0:T(1024)S(1)}, u32[]{:S(2)}) copy-start(f32[768]{0:T(1024)S(1)} %get-tuple-element.330) | copy-start | bytes 9220
  181.5 89.0 %copy-start.22 = (pred[512,512]{0,1:T(8,128)(4,1)}, pred[512,512]{0,1:T(8,128)(4,1)S(1)}, u32[]{:S(2)}) copy-start(pred[512,512]{0,1:T(8,128)(4,1)S(1)} %fusion.70) | copy-start | bytes 786436
  207.9 56.8 %copy-start.87 = (f32[512]{0:T(512)}, f32[512]{0:T(512)S(1)}, u32[]{:S(2)}) copy-start(f32[512]{0:T(512)S(1)} %add_rsqrt_fusion.2) | copy-start | bytes 6148
  278.9 363.6 %all-gather.20.cloned.1.call-start = ((), (), s32[]{:S(2)}) async-start(), calls=%async_computation.12 | async-start | bytes 10616832 | tf_op jit(solution)/shard_map/all_gather | solution.py:121
  282.0 375.5 %all-gather.22.cloned.1.call-start = ((), (), s32[]{:S(2)}) async-start(), calls=%async_computation.13 | async-start | bytes 10616832 | tf_op jit(solution)/shard_map/all_gather | solution.py:122
  285.2 400.7 %copy-start.53 = (s32[512,2]{0,1:T(2,128)}, s32[512,2]{0,1:T(2,128)S(1)}, u32[]{:S(2)}) copy-start(s32[512,2]{0,1:T(2,128)S(1)} %get-tuple-element.384) | copy-start | bytes 12292
  642.5 15.1 copy-start.36
  674.3 32.1 %all-to-all-start = ((bf16[2,4,192,768]{3,2,0,1:T(8,128)(2,1)}), bf16[2,4,192,768]{3,2,0,1:T(8,128)(2,1)S(1)}, u32[]{:S(2)}, u32[]{:S(2)}) async-start(bf16[2,4,192,768]{3,2,0,1:T(8,128)(2,1)} %copy.224), calls=%async_computation.1 | async-start | bytes 4718592 | tf_op jit(solution)/shard_map/all_to_all | solution.py:201
  678.1 740.2 %reduce-scatter.8.cloned.1.call-start = ((), (), s32[]{:S(2)}) async-start(), calls=%async_computation.14 | async-start | bytes 983040 | tf_op jit(solution)/shard_map/reduce_scatter | solution.py:266
  678.7 27.7 %copy-start.68 = (s32[1024]{0:T(1024)}, s32[1024]{0:T(1024)S(1)}, u32[]{:S(2)}) copy-start(s32[1024]{0:T(1024)S(1)} %broadcast_clamp_fusion.1) | copy-start | bytes 12292
  686.6 25.1 %copy-start.71 = (f32[512]{0:T(512)}, f32[512]{0:T(512)S(1)}, u32[]{:S(2)}) copy-start(f32[512]{0:T(512)S(1)} %fusion.90) | copy-start | bytes 6148
  686.7 28.6 %copy-start.38 = (f32[512,2]{1,0:T(8,128)}, f32[512,2]{1,0:T(8,128)S(1)}, u32[]{:S(2)}) copy-start(f32[512,2]{1,0:T(8,128)S(1)} %copy.216) | copy-start | bytes 12292
  742.9 18.4 copy-start.1
  761.2 607.5 %copy-start.41 = (s32[256,64]{1,0:T(8,128)S(1)}, s32[256,64]{1,0:T(8,128)}, u32[]{:S(2)}) copy-start(s32[256,64]{1,0:T(8,128)} %copy-done.40) | copy-start | bytes 196612
  761.3 607.5 %copy-start.47 = (f32[256,64]{1,0:T(8,128)S(1)}, f32[256,64]{1,0:T(8,128)}, u32[]{:S(2)}) copy-start(f32[256,64]{1,0:T(8,128)} %copy.227) | copy-start | bytes 196612
  761.3 607.7 %copy-start.96 = (s32[256]{0:T(256)S(1)}, s32[256]{0:T(256)}, u32[]{:S(2)}) copy-start(s32[256]{0:T(256)} %param.30) | copy-start | bytes 3076
  761.3 614.2 %copy-start.94 = (f32[256]{0:T(256)S(1)}, f32[256]{0:T(256)}, u32[]{:S(2)}) copy-start(f32[256]{0:T(256)} %fusion.78) | copy-start | bytes 3076
  1385.7 34.9 %copy-start.64 = (f32[768]{0:T(1024)S(1)}, f32[768]{0:T(1024)}, u32[]{:S(2)}) copy-start(f32[768]{0:T(1024)} %get-tuple-element.329) | copy-start | bytes 9220
  1385.7 34.9 %copy-start.78 = (f32[512]{0:T(512)S(1)}, f32[512]{0:T(512)}, u32[]{:S(2)}) copy-start(f32[512]{0:T(512)} %copy-done.77) | copy-start | bytes 6148
  1507.0 56.9 %all-to-all-start.2 = ((f32[2,4,192,768]{3,2,0,1:T(8,128)}), f32[2,4,192,768]{3,2,0,1:T(8,128)}, u32[]{:S(2)}, u32[]{:S(2)}) async-start(f32[2,4,192,768]{3,2,0,1:T(8,128)} %copy.236), calls=%async_computation.4 | async-start | bytes 9437184 | tf_op jit(solution)/shard_map/all_to_all | solution.py:308
  1512.2 51.8 %copy-start.69 = (s32[1024]{0:T(1024)S(1)}, s32[1024]{0:T(1024)}, u32[]{:S(2)}) copy-start(s32[1024]{0:T(1024)} %copy-done.68) | copy-start | bytes 12292
  1512.2 173.4 %all-gather.24.cloned.1.call-start = ((), (), s32[]{:S(2)}) async-start(), calls=%async_computation.18 | async-start | bytes 3932160 | tf_op jit(solution)/shard_map/all_gather | solution.py:379
  1515.2 76.7 %copy-start.51 = (f32[512,8]{0,1:T(8,128)}, f32[512,8]{0,1:T(8,128)S(1)}, u32[]{:S(2)}) copy-start(f32[512,8]{0,1:T(8,128)S(1)} %select_reduce_fusion.3) | copy-start | bytes 49156
  1575.9 16.0 copy-start.5
  1575.9 16.0 copy-start.58
  1575.9 16.0 copy-start.62
  1575.9 16.0 copy-start.76
  1596.6 17.4 slice-start
  1596.6 17.4 slice-start.1
  1628.8 241.1 %all-reduce.3.cloned.1.call-start = ((), (), s32[]{:S(2)}) async-start(), calls=%async_computation.15 | async-start | bytes 18874368 | tf_op jit(solution)/shard_map/psum | solution.py:406
  1637.7 334.1 %reduce-scatter.12.cloned.1.call-start = ((), (), s32[]{:S(2)}) async-start(), calls=%async_computation.17 | async-start | bytes 10616832 | tf_op jit(solution)/shard_map/reduce_scatter | solution.py:397
  1656.3 415.8 %reduce-scatter.10.cloned.1.call-start = ((), (), s32[]{:S(2)}) async-start(), calls=%async_computation.16 | async-start | bytes 10616832 | tf_op jit(solution)/shard_map/reduce_scatter | solution.py:394
  1671.4 528.7 %reduce-scatter.14.cloned.1.call-start = ((), (), s32[]{:S(2)}) async-start(), calls=%async_computation.19 | async-start | bytes 13934592 | tf_op jit(solution)/shard_map/reduce_scatter | solution.py:400
  1726.4 46.6 %copy-start.74 = (f32[11,96]{1,0:T(8,128)S(1)}, f32[11,96]{1,0:T(8,128)}, u32[]{:S(2)}) copy-start(f32[11,96]{1,0:T(8,128)} %param.45) | copy-start | bytes 12676
  1726.4 46.6 %copy-start.93 = (f32[11,96]{1,0:T(8,128)S(1)}, f32[11,96]{1,0:T(8,128)}, u32[]{:S(2)}) copy-start(f32[11,96]{1,0:T(8,128)} %param.46) | copy-start | bytes 12676
  1726.4 47.2 %copy-start.89 = (f32[11,96]{1,0:T(8,128)S(1)}, f32[11,96]{1,0:T(8,128)}, u32[]{:S(2)}) copy-start(f32[11,96]{1,0:T(8,128)} %param.47) | copy-start | bytes 12676
  1773.7 101.1 %copy-start.70 = (f32[11,96]{1,0:T(8,128)}, f32[11,96]{1,0:T(8,128)S(1)}, u32[]{:S(2)}) copy-start(f32[11,96]{1,0:T(8,128)S(1)} %get-tuple-element.361) | copy-start | bytes 12676
  1877.5 94.3 %copy-start.18 = (f32[2,384,768]{2,1,0:T(8,128)S(1)}, f32[2,384,768]{2,1,0:T(8,128)}, u32[]{:S(2)}) copy-start(f32[2,384,768]{2,1,0:T(8,128)} %param.39) | copy-start | bytes 7077892
  1977.8 94.3 %copy-start.19 = (f32[2,96,3072]{2,1,0:T(8,128)S(1)}, f32[2,96,3072]{2,1,0:T(8,128)}, u32[]{:S(2)}) copy-start(f32[2,96,3072]{2,1,0:T(8,128)} %param.36) | copy-start | bytes 7077892
  2078.1 122.0 %copy-start.12 = (f32[8000,96]{0,1:T(8,128)S(1)}, f32[8000,96]{0,1:T(8,128)}, u32[]{:S(2)}) copy-start(f32[8000,96]{0,1:T(8,128)} %param.42) | copy-start | bytes 9216004
  (74 other events, 256.1 us)
Sparse Core Ops, SparseCore 0:
  10.6 117.8 all-gather.13
  164.3 42.1 reduce-scatter.5
  208.7 51.6 all-gather.15
  279.0 42.8 all-gather.17
  323.9 90.7 all-gather.19
  416.7 89.1 all-gather.21
  1393.3 25.0 reduce-scatter.7
  1629.0 43.9 all-gather.23
  1678.8 191.1 all-reduce.2
  1872.2 99.5 reduce-scatter.11
  1974.2 97.8 reduce-scatter.9
  2074.4 125.6 reduce-scatter.13

commit v2 on v1

--- a/solution.py
+++ b/solution.py
@@ -16,12 +16,33 @@
 MASKED_SCORE = -1e30
 
 
-def combined_all(value, axis, join):
-    pieces = jax.tree.map(lambda part: lax.all_gather(part, axis), value)
-    head = jax.tree.map(lambda part: part[0], pieces)
-    tail = jax.tree.map(lambda part: part[1:], pieces)
-    total, _ = lax.scan(lambda total, share: (join(total, share), None), head, tail)
-    return total
+def partner_order(members):
+    if members & (members - 1) == 0:
+        return [[(i, i ^ k) for i in range(members)] for k in range(members)]
+    return [[(i, (k - i) % members) for i in range(members)] for k in range(members)]
+
+
+def partner_of(me, k, members):
+    return me ^ k if members & (members - 1) == 0 else (k - me) % members
+
+
+def swap(value, k, members):
+    return value if k == 0 else lax.ppermute(value, "expert", partner_order(members)[k])
+
+
+def in_order(parts, me):
+    members = len(parts)
+    stacked = jnp.stack(parts)
+    return jnp.stack(
+        [
+            lax.dynamic_index_in_dim(stacked, partner_of(me, k, members), 0, keepdims=False)
+            for k in range(members)
+        ]
+    )
+
+
+def shared(value, members):
+    return [swap(value, k, members) for k in range(members)]
 
 
 def normal_parts(stream):
@@ -42,7 +63,7 @@
     place = jnp.arange(flat.shape[0], dtype=jnp.int32)
     earlier = (place[None, :] < place[:, None]).astype(jnp.bfloat16)
     before = jnp.dot(earlier, hits.astype(jnp.bfloat16), preferred_element_type=jnp.float32)
-    return (flat, jnp.sum(before.astype(jnp.int32) * hits, axis=1))
+    return jnp.sum(before.astype(jnp.int32) * hits, axis=1).reshape(block_routes.shape)
 
 
 def block_scores(query, keys, seg_ids, block_index, length, block_rows, scaling):
@@ -56,10 +77,25 @@
     return (jnp.where(allowed[None], scores, MASKED_SCORE), query, keys, first_row)
 
 
-def combine_stats(earlier, later):
-    highest = jnp.maximum(earlier[0], later[0])
-    totals = earlier[1] * jnp.exp(earlier[0] - highest) + later[1] * jnp.exp(later[0] - highest)
-    return (highest, totals, earlier[2] + later[2])
+def label_weights(ids, weights, vocab_rows):
+    lanes = 128
+    tiles = (vocab_rows + lanes - 1) // lanes
+    parts = []
+    rest = weights
+    for _ in range(3):
+        part = lax.reduce_precision(rest, 8, 7)
+        parts.append(part)
+        rest = rest - part
+    high = jnp.arange(tiles, dtype=jnp.int32)
+    low = jnp.arange(lanes, dtype=jnp.int32)
+    high_hits = (ids >> 7)[:, :, None] == high[None, None, :]
+    rows = jnp.concatenate(
+        [jnp.where(high_hits, part[:, :, None], 0.0).astype(jnp.bfloat16) for part in parts], axis=1
+    )
+    columns = ((ids & (lanes - 1))[:, :, None] == low[None, None, :]).astype(jnp.bfloat16)
+    columns = jnp.concatenate([columns] * len(parts), axis=1)
+    spread = jnp.einsum("pih,pil->phl", rows, columns, preferred_element_type=jnp.float32)
+    return spread.reshape(ids.shape[0], tiles * lanes)[:, :vocab_rows]
 
 
 def nesterov_update(master, moment, average, grad, rate):
@@ -113,9 +149,27 @@
     group_count = members * local_rows
     lookup_rows = math.gcd(group_count, 2048)
     vocab_iota = jnp.arange(vocab_rows, dtype=jnp.int32)
-    dense_low, small_low = (
-        lax.all_gather(attention.astype(jnp.bfloat16), "dp", axis=1, tiled=True),
-        lax.all_gather(small_params.astype(jnp.bfloat16), "dp", axis=1, tiled=True),
+    share = width // replicas
+    chunk = attention.shape[0] * share // members
+    small_rows = small_params.size // width + 1
+    small_flat = jnp.pad(
+        small_params.reshape(-1), (0, small_rows * width - small_params.size)
+    ).reshape(small_rows, width)
+    dense_part = lax.dynamic_slice_in_dim(
+        attention.reshape(attention.shape[0] * share, width), my_index * chunk, chunk, 0
+    )
+    dense_part = lax.all_gather(
+        jnp.concatenate([dense_part, small_flat], axis=0).astype(jnp.bfloat16), "dp", axis=0
+    )
+    small_low = dense_part[:, chunk:].reshape(replicas, small_rows * width)
+    small_low = small_low[:, : small_params.size].reshape(replicas, small_params.shape[0], share)
+    small_low = small_low.transpose(1, 0, 2).reshape(small_params.shape[0], width)
+    dense_parts = in_order(shared(dense_part[:, :chunk], members), my_index)
+    dense_low = (
+        dense_parts.transpose(1, 0, 2, 3)
+        .reshape(replicas, attention.shape[0], share, width)
+        .transpose(1, 0, 2, 3)
+        .reshape(attention.shape[0], width, width)
     )
     in_low, out_low, table_low = (
         lax.all_gather(expert_in.astype(jnp.bfloat16), "dp", axis=1, tiled=True),
@@ -125,19 +179,20 @@
     gain_rows = small_low[:3].astype(jnp.float32)
     router = small_low[3:].astype(jnp.float32)
     group_ids = token_ids.reshape(-1)
-    group_routes = routes.reshape(members * local_rows, TOP)
-    own_routes = lax.dynamic_slice_in_dim(group_routes, my_index * local_rows, local_rows, 0)
+    own_routes = lax.dynamic_slice_in_dim(
+        routes.reshape(members * local_rows, TOP), my_index * local_rows, local_rows, 0
+    )
     local_ids = group_ids - my_index * vocab_rows
     id_blocks = local_ids.reshape(group_count // lookup_rows, lookup_rows)
-
-    def lookup_block(ids_block):
-        selector = (ids_block[:, None] == vocab_iota[None, :]).astype(jnp.bfloat16)
-        return jnp.dot(selector, table_low, preferred_element_type=jnp.float32).astype(jnp.bfloat16)
-
-    partial_value = lax.map(lookup_block, id_blocks).reshape(group_count, width)
-    stream = lax.psum_scatter(partial_value, "expert", scatter_dimension=0, tiled=True).astype(
-        jnp.float32
-    )
+    own_ids = lax.dynamic_slice_in_dim(group_ids, my_index * local_rows, local_rows, 0)
+    column_ids = lax.all_gather(own_ids, "dp", axis=0, tiled=True)
+    rows_table = jnp.concatenate(shared(embedding.astype(jnp.bfloat16), members), axis=0)
+    places = partner_of(my_index, column_ids // vocab_rows, members) * vocab_rows
+    places = places + column_ids % vocab_rows
+    stream_parts = jnp.take(rows_table, places, axis=0, mode="clip")
+    stream = lax.all_to_all(
+        stream_parts, "dp", split_axis=0, concat_axis=1, tiled=True
+    ).astype(jnp.float32)
     normal_one, factor_one = normal_parts(stream)
     attn_in = (normal_one * gain_rows[0]).astype(jnp.bfloat16)
     projected = jnp.einsum(
@@ -170,131 +225,113 @@
     moe_in = (normal_two * gain_rows[1]).astype(jnp.bfloat16)
     moe_float = moe_in.astype(jnp.float32)
     router_logits = jnp.dot(moe_float, router.T, precision=highest_precision)
-    chosen = jnp.take_along_axis(router_logits, own_routes, axis=1)
+    expert_ids = jnp.arange(experts, dtype=jnp.int32)
+    route_hits = (own_routes[:, :, None] == expert_ids[None, None, :]).astype(jnp.float32)
+    chosen = jnp.sum(router_logits[:, None, :] * route_hits, axis=2)
     gating = jnp.exp(chosen - jnp.max(chosen, axis=1, keepdims=True))
     gating = gating / jnp.sum(gating, axis=1, keepdims=True)
-    flat_routes, slots = slot_table(own_routes, experts)
-    landing = flat_routes * capacity + slots
-    token_of = jnp.arange(local_rows * TOP) // TOP
-    everyone = lax.all_gather(moe_in, "expert", axis=0, tiled=True)
-    all_flat, all_slots = jax.vmap(lambda block_routes: slot_table(block_routes, experts))(
-        group_routes.reshape(members, local_rows, TOP)
-    )
-    owned = all_flat - my_index * local_experts
-    source = jnp.arange(members)[:, None]
-    spot = owned * (members * capacity) + source * capacity + all_slots
-    spot = jnp.where(
-        (owned >= 0) & (owned < local_experts), spot, local_experts * members * capacity
-    )
-    source_rows = source * local_rows + token_of[None, :]
+    slots = slot_table(own_routes, experts)
+    block = local_experts * capacity
+    landing = partner_of(my_index, own_routes // local_experts, members) * block
+    landing = landing + own_routes % local_experts * capacity + slots
+    landing_iota = jnp.arange(members * block, dtype=jnp.int32)
+    picks = [
+        (landing[:, j][:, None] == landing_iota[None, :]).astype(jnp.bfloat16) for j in range(TOP)
+    ]
+    any_pick = sum(picks)
+
+    def exchanged(rows):
+        parts = rows.reshape(members, block, rows.shape[1])
+        return jnp.stack([swap(parts[k], k, members) for k in range(members)])
+
+    outgoing = jnp.einsum("tr,td->rd", any_pick, moe_in, preferred_element_type=jnp.float32)
+    arrived = exchanged(outgoing.astype(jnp.bfloat16))
     arrived = (
-        jnp.zeros((local_experts * members * capacity, width), jnp.bfloat16)
-        .at[spot.reshape(-1)]
-        .set(jnp.take(everyone, source_rows.reshape(-1), axis=0), mode="drop")
-    )
-    arrived = arrived.reshape(local_experts, members * capacity, width)
+        arrived.reshape(members, local_experts, capacity, width)
+        .transpose(1, 0, 2, 3)
+        .reshape(local_experts, members * capacity, width)
+    )
+
+    def sent_back(rows):
+        rows = rows.reshape(local_experts, members, capacity, width).transpose(1, 0, 2, 3)
+        return exchanged(rows.reshape(members * block, width)).reshape(members * block, width)
+
     expert_hidden = jnp.einsum("ecd,edf->ecf", arrived, in_low, preferred_element_type=jnp.float32)
     activated = jax.nn.gelu(expert_hidden, approximate=True).astype(jnp.bfloat16)
     expert_result = jnp.einsum(
         "ecf,efd->ecd", activated, out_low, preferred_element_type=jnp.float32
     ).astype(jnp.bfloat16)
-    returned = lax.all_to_all(
-        expert_result.reshape(local_experts, members, capacity, width),
-        "expert",
-        split_axis=1,
-        concat_axis=0,
-        tiled=True,
-    )
-    returned = returned.reshape(experts * capacity, width)
-    picked = jnp.take(returned, landing, axis=0).reshape(local_rows, TOP, width).astype(jnp.float32)
-    hidden_two = hidden_one + jnp.sum(gating[:, :, None] * picked, axis=1)
+    returned = sent_back(expert_result)
+    picked = [jnp.dot(pick, returned, preferred_element_type=jnp.float32) for pick in picks]
+    hidden_two = hidden_one + sum(gating[:, j][:, None] * picked[j] for j in range(TOP))
     normal_three, factor_three = normal_parts(hidden_two)
     final = (normal_three * gain_rows[2]).astype(jnp.bfloat16)
-    group_final = lax.all_gather(jnp.take(final, positions, axis=0), "expert", axis=0, tiled=True)
+    place_hits = positions[:, None] == jnp.arange(local_rows, dtype=jnp.int32)[None, :]
+    final_rows = jnp.dot(
+        place_hits.astype(jnp.bfloat16), final, preferred_element_type=jnp.float32
+    ).astype(jnp.bfloat16)
+    group_final = lax.all_gather(final_rows, "expert", axis=0, tiled=True)
     logits = jnp.einsum("gd,vd->gv", group_final, table_low, preferred_element_type=jnp.float32)
     target_local = targets - my_index * vocab_rows
     teacher_local = teacher_ids - my_index * vocab_rows
-    target_inside = (target_local >= 0) & (target_local < vocab_rows)
-    teacher_inside = (teacher_local >= 0) & (teacher_local < vocab_rows)
-    target_logit = jnp.take_along_axis(
-        logits, jnp.clip(target_local, 0, vocab_rows - 1)[:, None], axis=1
-    )[:, 0]
-    teacher_logit = jnp.take_along_axis(logits, jnp.clip(teacher_local, 0, vocab_rows - 1), axis=1)
-    taught = jnp.where(target_inside, target_logit, 0.0) + jnp.sum(
-        jnp.where(teacher_inside, teacher_probs * teacher_logit, 0.0), axis=1
-    )
+    taken = label_weights(
+        jnp.concatenate([teacher_local, target_local[:, None]], axis=1),
+        jnp.concatenate([teacher_probs, jnp.ones_like(teacher_probs[:, :1])], axis=1),
+        vocab_rows,
+    )
+    taught = jnp.sum(taken * logits, axis=1)
     local_max = jnp.max(logits, axis=1)
     local_total = jnp.sum(jnp.exp(logits - local_max[:, None]), axis=1)
-    highest, totals, picked_sum = combined_all(
-        (local_max, local_total, taught), "expert", combine_stats
-    )
+    stats = lax.all_gather(jnp.stack([local_max, local_total, taught]), "expert")
+    highest = jnp.max(stats[:, 0], axis=0)
+    totals = jnp.sum(stats[:, 1] * jnp.exp(stats[:, 0] - highest[None]), axis=0)
+    picked_sum = jnp.sum(stats[:, 2], axis=0)
     log_total = highest + jnp.log(totals)
     entropy = jnp.sum(teacher_probs * jnp.log(teacher_probs), axis=1)
     terms = 2.0 * log_total - picked_sum + entropy
     loss_part = (
         jnp.sum(lax.dynamic_slice_in_dim(terms, my_index * loss_local, loss_local, 0)) / loss_count
     )
-    loss_rows = logits.shape[0]
-    target_rows = math.gcd(loss_rows, 128)
-
-    def target_block(triple):
-        target_block_ids, teacher_block_ids, prob_block = triple
-        hit_target = (target_block_ids[:, None] == vocab_iota[None, :]).astype(jnp.float32)
-        hit_teacher = jnp.sum(
-            jnp.where(
-                teacher_block_ids[:, :, None] == vocab_iota[None, None, :],
-                prob_block[:, :, None],
-                0.0,
-            ),
-            axis=1,
-        )
-        return hit_target + hit_teacher
-
-    taken = lax.map(
-        target_block,
-        (
-            target_local.reshape(-1, target_rows),
-            teacher_local.reshape(-1, target_rows, teacher_ids.shape[1]),
-            teacher_probs.reshape(-1, target_rows, teacher_ids.shape[1]),
-        ),
-    ).reshape(loss_rows, vocab_rows)
     soft = jnp.exp(logits - log_total[:, None])
     logit_grad = ((2.0 * soft - taken) / loss_count).astype(jnp.bfloat16)
     embed_head = jnp.einsum(
         "gv,gd->vd", logit_grad, group_final, preferred_element_type=jnp.float32
     )
-    final_grad = lax.psum_scatter(
-        jnp.dot(logit_grad, table_low, preferred_element_type=jnp.float32),
-        "expert",
-        scatter_dimension=0,
-        tiled=True,
-    )
-    final_full = jnp.zeros((local_rows, width), jnp.float32).at[positions].add(final_grad)
+    final_parts = jnp.dot(logit_grad, table_low, preferred_element_type=jnp.float32)
+    final_grad = sum(
+        swap(
+            lax.dynamic_slice_in_dim(
+                final_parts, partner_of(my_index, k, members) * loss_local, loss_local, 0
+            ),
+            k,
+            members,
+        )
+        for k in range(members)
+    )
+    final_full = jnp.dot(
+        place_hits.astype(jnp.float32).T, final_grad, precision=highest_precision
+    )
     grad_two, gain_three = norm_backward(normal_three, factor_three, gain_rows[2], final_full)
-    gate_grad = jnp.sum(grad_two[:, None, :] * picked, axis=2)
+    gate_grad = jnp.stack([jnp.sum(grad_two * part, axis=1) for part in picked], axis=1)
     chosen_grad = gating * (gate_grad - jnp.sum(gating * gate_grad, axis=1, keepdims=True))
-    expert_ids = jnp.arange(experts, dtype=jnp.int32)
-    route_grad = jnp.sum(
-        chosen_grad[:, :, None] * (own_routes[:, :, None] == expert_ids[None, None, :]), axis=1
-    )
+    route_grad = jnp.sum(chosen_grad[:, :, None] * route_hits, axis=1)
     router_grad = jnp.dot(route_grad.T, moe_float, precision=highest_precision)
     moe_grad = jnp.dot(route_grad, router, precision=highest_precision)
-    result_grad = (
-        (gating[:, :, None] * grad_two[:, None, :])
-        .astype(jnp.bfloat16)
-        .reshape(local_rows * TOP, width)
-    )
-    outgoing_grad = (
-        jnp.zeros((experts * capacity, width), jnp.bfloat16).at[landing].set(result_grad)
-    )
-    arrived_grad = lax.all_to_all(
-        outgoing_grad.reshape(members, local_experts, capacity, width),
-        "expert",
-        split_axis=0,
-        concat_axis=2,
-        tiled=True,
-    )
-    arrived_grad = arrived_grad.reshape(local_experts, members * capacity, width)
+    outgoing_grad = sum(
+        jnp.einsum(
+            "tr,td->rd",
+            picks[j],
+            (gating[:, j][:, None] * grad_two).astype(jnp.bfloat16),
+            preferred_element_type=jnp.float32,
+        )
+        for j in range(TOP)
+    ).astype(jnp.bfloat16)
+    arrived_grad = (
+        exchanged(outgoing_grad)
+        .reshape(members, local_experts, capacity, width)
+        .transpose(1, 0, 2, 3)
+        .reshape(local_experts, members * capacity, width)
+    )
     out_grad = jnp.einsum(
         "ecf,ecd->efd", activated, arrived_grad, preferred_element_type=jnp.float32
     )
@@ -305,17 +342,8 @@
     hidden_grad = gelu_pull(activated_grad)[0].astype(jnp.bfloat16)
     in_grad = jnp.einsum("ecd,ecf->edf", arrived, hidden_grad, preferred_element_type=jnp.float32)
     rows_grad = jnp.einsum("ecf,edf->ecd", hidden_grad, in_low, preferred_element_type=jnp.float32)
-    back_rows = lax.all_to_all(
-        rows_grad.reshape(local_experts, members, capacity, width),
-        "expert",
-        split_axis=1,
-        concat_axis=0,
-        tiled=True,
-    )
-    back_rows = back_rows.reshape(experts * capacity, width)
-    moe_grad = moe_grad + jnp.sum(
-        jnp.take(back_rows, landing, axis=0).reshape(local_rows, TOP, width), axis=1
-    )
+    back_rows = sent_back(rows_grad.astype(jnp.bfloat16))
+    moe_grad = moe_grad + jnp.dot(any_pick, back_rows, preferred_element_type=jnp.float32)
     grad_part, gain_two = norm_backward(normal_two, factor_two, gain_rows[1], moe_grad)
     grad_one = grad_two + grad_part
     attn_grad = grad_one.astype(jnp.bfloat16)
@@ -376,7 +404,9 @@
     )
     grad_part, gain_one = norm_backward(normal_one, factor_one, gain_rows[0], attn_in_grad)
     stream_grad = (grad_one + grad_part).astype(jnp.bfloat16)
-    group_grad = lax.all_gather(stream_grad, "expert", axis=0, tiled=True)
+    group_grad = jnp.concatenate(shared(stream_grad, members), axis=0)
+    id_blocks = jnp.stack(in_order(list(local_ids.reshape(members, local_rows)), my_index))
+    id_blocks = id_blocks.reshape(group_count // lookup_rows, lookup_rows)
 
     def add_rows(total, pair):
         selector = (pair[0][:, None] == vocab_iota[None, :]).astype(jnp.bfloat16)
@@ -403,13 +433,40 @@
     )
     attention_grad = jnp.concatenate([qkv_grad, out_weight_grad[None]], axis=0)
     small_grad = jnp.concatenate([jnp.stack([gain_one, gain_two, gain_three]), router_grad], axis=0)
-    attention_sum, small_sum, loss_value = lax.psum(
-        (attention_grad, small_grad, loss_part), ("dp", "expert")
-    )
-    share = width // replicas
-    share_start = lax.axis_index("dp") * share
-    attention_sum = lax.dynamic_slice_in_dim(attention_sum, share_start, share, 1)
-    small_sum = lax.dynamic_slice_in_dim(small_sum, share_start, share, 1)
+    dense_grads = (
+        attention_grad.reshape(attention.shape[0], replicas, share, width)
+        .transpose(1, 0, 2, 3)
+        .reshape(replicas, members, chunk, width)
+        .astype(jnp.bfloat16)
+    )
+    dense_sum = sum(
+        swap(
+            lax.dynamic_index_in_dim(
+                dense_grads, partner_of(my_index, k, members), 1, keepdims=False
+            ),
+            k,
+            members,
+        ).astype(jnp.float32)
+        for k in range(members)
+    )
+    small_grads = small_grad.reshape(-1, replicas, share).transpose(1, 0, 2).reshape(replicas, -1)
+    small_grads = jnp.concatenate(
+        [
+            small_grads,
+            jnp.full((replicas, 1), loss_part),
+            jnp.zeros((replicas, small_rows * width - small_params.size - 1), jnp.float32),
+        ],
+        axis=1,
+    ).reshape(replicas, small_rows, width)
+    small_grads = sum(shared(small_grads, members))
+    summed = lax.psum_scatter(
+        jnp.concatenate([dense_sum, small_grads], axis=1), "dp", scatter_dimension=0
+    )
+    small_sum = summed[chunk:].reshape(-1)
+    loss_value = small_sum[small_params.size]
+    small_sum = small_sum[: small_params.size].reshape(small_params.shape[0], share)
+    attention_sum = in_order(shared(summed[:chunk], members), my_index)
+    attention_sum = attention_sum.reshape(attention.shape[0], share, width)
     rate_base = loss_count**0.5
     first_out = nesterov_update(
         attention, attention_moment, attention_average, attention_sum, RATE_TABLE[0] * rate_base

time: 2240 us -> 998 us (0.45)
  local copies, waits for them, and re-layouts: 887 us -> 89.2 us
  waiting for transfers between devices: 683 us -> 469 us
  other arithmetic: 257 us -> 90.8 us
  blocking collectives: 119 us -> 31.8 us
  starting transfers between devices: 9.97 us -> 45 us
    gather x14 -> x1, local copies, waits for them, and re-layouts: 637 us -> 15.5 us  [shards(): stream_parts = jnp.take(rows_table, places, axis=0, mode='clip')]
    ppermute x0 -> x33, waiting for transfers between devices: none -> 202 us  [swap(): lax.ppermute(value, 'expert', partner_order(members)[k])]
    dynamic_update_slice x2 -> x0, local copies, waits for them, and re-layouts: 196 us -> none  [shards(): lax.map(target_block, (target_local.reshape(-1, target_rows), teacher_loc...]
    reduce_sum x8 -> x4, other arithmetic: 122 us -> 0.81 us  [the longest x1 0.76 us: shards(): jnp.sum(grad_two * part, axis=1)]
    all_gather x1, waiting for transfers between devices: 118 us -> 19.9 us  [shards(): lax.all_gather(embedding.astype(jnp.bfloat16), 'dp', axis=1, tiled=True)]
    psum x1 -> x0, waiting for transfers between devices: 95.7 us -> none  [shards(): lax.psum((attention_grad, small_grad, loss_part), ('dp', 'expert'))]
    reduce_scatter x1, waiting for transfers between devices: 85.7 us -> 7.82 us  [shards(): lax.psum_scatter(out_grad.astype(jnp.bfloat16), 'dp', scatter_dimension=1...]
    scatter x2 -> x0, other arithmetic: 59.4 us -> none  [the longest x1 51.9 us: shards(): arrived = jnp.zeros((local_experts * members * capacity, width), jnp.bflo...]
  transfers between devices with their start and end apart: 14 -> 42, of which waited for: 10 -> 24; matrix products, arithmetic and copies ran while one was open for 23% -> 28% of each run, Pallas kernels for 0% -> 0%
where the time goes in v2:
time: 998 us; the launch traced here: 991 us
  waiting for transfers between devices  469 us (47%)
  matrix products  249 us (25%)
  other arithmetic  90.8 us (9%)
  local copies, waits for them, and re-layouts  89.2 us (9%)
  starting transfers between devices  45 us (5%)
  blocking collectives  31.8 us (3%)
  between operations  16.5 us (2%)
    ppermute x33, waiting for transfers between devices, swap(): lax.ppermute(value, 'expert', partner_order(members)[k])  202 us
    reduce_scatter x1, waiting for transfers between devices, shards(): lax.psum_scatter(embed_grad.astype(jnp.bfloat16), 'dp', scatter_dimension...  120 us
    reduce_scatter x1, waiting for transfers between devices, shards(): lax.psum_scatter(in_grad.astype(jnp.bfloat16), 'dp', scatter_dimension=1,...  92.6 us
    ppermute x33, starting transfers between devices, swap(): lax.ppermute(value, 'expert', partner_order(members)[k])  39.6 us
    dot_general x1, matrix products, add_rows(): jnp.einsum('tv,td->vd', selector, pair[1], preferred_element_type=jnp.flo...  37.1 us
    all_to_all x1, waiting for transfers between devices, shards(): lax.all_to_all(stream_parts, 'dp', split_axis=0, concat_axis=1, tiled=True)  25.8 us
    dot_general x1, matrix products, shards(): jnp.einsum('ecd,efd->ecf', arrived_grad, out_low, preferred_element_type=...  22.9 us
    concatenate x2, local copies, waits for them, and re-layouts, shards(): jnp.concatenate(shared(embedding.astype(jnp.bfloat16), members), axis=0)  20.3 us
  transfers between devices with their start and end apart: 42, of which 24 were waited for; matrix products, arithmetic and copies ran while one was open for 28% of the time, Pallas kernels for 0%

profile of v2, /device:TPU:0, one launch (start us, length us, event | category | flops | bytes accessed | tf_op | source)
XLA Modules:
  0.0 991.2 jit_solution(7886446975149442867)
XLA Ops:
  21.7 13.4 %all-gather.1 = s32[8,1,512]{2,1,0:T(1,128)S(1)} all-gather(s32[1,1,512]{2,1,0:T(1,128)S(1)} %bitcast.284), channel_id=1, replica_groups=mesh['dp'=8,'expert'=4] {'dp'}, dimensions={0}, use_global_device_ids=true | all-gather | bytes 18432 | tf_op jit(solution)/shard_map/all_gather | solution.py:188
  37.5 6.0 iota_compare_fusion.4
  43.5 6.5 select_convert_fusion.2
  50.0 6.0 collective-permute-done.5
  56.0 32.4 %collective-permute-done.4 = bf16[8000,96]{0,1:T(8,128)(2,1)} collective-permute-done((bf16[8000,96]{0,1:T(8,128)(2,1)}, bf16[8000,96]{0,1:T(8,128)(2,1)}, u32[]{:S(2)}, u32[]{:S(2)}) %collective-permute-start.4) | collective-permute-done | bytes 1536032 | tf_op jit(solution)/shard_map/ppermute | solution.py:30
  88.7 10.4 %concatenate.79 = bf16[32000,96]{0,1:T(8,128)(2,1)} concatenate(bf16[8000,96]{0,1:T(8,128)(2,1)} %convert_element_type.201, bf16[8000,96]{0,1:T(8,128)(2,1)} %collective-permute-done.3, bf16[8000,96]{0,1:T(8,128)(2,1)} %collective-permute-done.4, bf16[8000,96]{0,1:T(8,128)(2,1)S(1)} %collective-permute-done.5), dimensions={0} | concatenate | bytes 12288000 | tf_op jit(solution)/shard_map/concatenate | solution.py:189
  99.0 10.0 %copy.224 = bf16[32000,96]{1,0:T(8,128)(2,1)} copy(bf16[32000,96]{0,1:T(8,128)(2,1)} %concatenate.79) | data formatting | bytes 12288000 | tf_op jit(solution)/shard_map/concatenate | solution.py:189
  109.0 15.5 %gather_fusion = bf16[4096,96]{1,0:T(8,128)(2,1)S(1)} fusion(bf16[32000,96]{1,0:T(8,128)(2,1)} %copy.224, s32[4096]{0:T(1024)S(1)} %fusion.114), kind=kCustom, calls=%fused_computation | custom fusion | bytes 1589248 | tf_op jit(solution)/shard_map/jit(_take)/gather | solution.py:192
  125.7 4.8 all-to-all-start
  139.7 25.8 %all-to-all-done = bf16[8,512,96]{1,2,0:T(8,128)(2,1)S(1)} async-done(((bf16[8,512,96]{1,2,0:T(8,128)(2,1)}), bf16[8,512,96]{1,2,0:T(8,128)(2,1)S(1)}, u32[]{:S(2)}, u32[]{:S(2)}) %all-to-all-start) | async-done | bytes 786464 | tf_op jit(solution)/shard_map/all_to_all | solution.py:193
  169.1 19.9 %collective-permute-done.2 = bf16[8,96,768]{2,1,0:T(8,128)(2,1)} collective-permute-done((bf16[8,96,768]{2,1,0:T(8,128)(2,1)}, bf16[8,96,768]{2,1,0:T(8,128)(2,1)}, u32[]{:S(2)}, u32[]{:S(2)}) %collective-permute-start.2) | collective-permute-done | bytes 1179680 | tf_op jit(solution)/shard_map/ppermute | solution.py:30
  214.3 19.6 %fusion.2 = f32[256,63,128]{2,1,0:T(8,128)} fusion(pred[256,65,128]{2,1,0:T(8,128)(4,1)} %iota_compare_fusion.4, bf16[256,65,63]{1,2,0:T(8,128)(2,1)} %get-tuple-element.160, bf16[256,65,63]{1,2,0:T(8,128)(2,1)} %get-tuple-element.161, bf16[256,65,63]{1,2,0:T(8,128)(2,1)} %get-tuple-element.159), kind=kOutput, calls=%fused_computation.6 | convolution fusion | flops 836759040 | bytes 16677376 | tf_op jit(solution)/shard_map/pih,pil->phl/dot_general | solution.py:97
  234.0 9.6 copy.238
  248.0 15.4 %fusion.157 = f32[2,768,3072]{2,1,0:T(8,128)} fusion(bf16[2,768,768]{2,1,0:T(8,128)(2,1)} %bitcast.245, bf16[2,768,3072]{2,1,0:T(8,128)(2,1)} %all-gather.10.cloned.1.call-done), kind=kOutput, calls=%fused_computation.310 | convolution fusion | flops 7247757312 | bytes 30670848 | tf_op jit(solution)/shard_map/ecd,edf->ecf/dot_general | solution.py:259
  263.4 15.2 %convolution_convert_fusion.5 = bf16[2,768,768]{2,1,0:T(8,128)(2,1)S(1)} fusion(bf16[2,3072,768]{2,1,0:T(8,128)(2,1)} %all-gather.12.cloned.1.call-done, f32[2,768,3072]{2,1,0:T(8,128)} %fusion.157), kind=kOutput, calls=%fused_computation.104 | convolution fusion | flops 7291404288 | bytes 30670848 | tf_op jit(solution)/shard_map/ecf,efd->ecd/dot_general | solution.py:261
  283.4 13.8 %collective-permute-done.11 = bf16[384,768]{1,0:T(8,128)(2,1)S(1)} collective-permute-done((bf16[384,768]{1,0:T(8,128)(2,1)}, bf16[384,768]{1,0:T(8,128)(2,1)S(1)}, u32[]{:S(2)}, u32[]{:S(2)}) %collective-permute-start.11) | collective-permute-done | bytes 589856 | tf_op jit(solution)/shard_map/ppermute | solution.py:30
  297.2 10.2 %collective-permute-done.10 = bf16[384,768]{1,0:T(8,128)(2,1)} collective-permute-done((bf16[384,768]{1,0:T(8,128)(2,1)}, bf16[384,768]{1,0:T(8,128)(2,1)}, u32[]{:S(2)}, u32[]{:S(2)}) %collective-permute-start.10) | collective-permute-done | bytes 589856 | tf_op jit(solution)/shard_map/ppermute | solution.py:30
  314.9 10.1 %all_gather.29 = bf16[256,768]{1,0:T(8,128)(2,1)} all-gather(bf16[64,768]{1,0:T(8,128)(2,1)S(1)} %convolution_convert_fusion.8), channel_id=1, replica_groups=mesh['dp'=8,'expert'=4] {'expert'}, dimensions={0}, use_global_device_ids=true | all-gather | bytes 491520 | tf_op jit(solution)/shard_map/all_gather | solution.py:273
  325.0 19.9 %all-gather.14.cloned.1.call-done = bf16[8000,768]{0,1:T(8,128)(2,1)} async-done(((bf16[8000,96]{0,1:T(8,128)(2,1)}), bf16[8000,768]{0,1:T(8,128)(2,1)}) %all-gather.14.cloned.1.call-update) | async-done | bytes 12288016 | tf_op jit(solution)/shard_map/all_gather | solution.py:177
  344.9 8.7 fusion.155
  353.6 4.6 exponential_reduce_fusion
  358.3 8.3 all-gather.2
  370.4 12.5 %fusion.158 = f32[256,768]{1,0:T(8,128)S(1)} fusion(bf16[256,8000]{0,1:T(8,128)(2,1)} %multiply_convert_fusion.2, bf16[8000,768]{0,1:T(8,128)(2,1)} %all-gather.14.cloned.1.call-done), kind=kOutput, calls=%fused_computation.311 | convolution fusion | flops 3145728000 | bytes 17170432 | tf_op jit(solution)/shard_map/dot_general | solution.py:300
  416.3 5.9 collective-permute-done.17
  422.2 7.9 collective-permute-done.16
  432.1 22.9 %fusion.14 = bf16[2,768,3072]{2,1,0:T(8,128)(2,1)} fusion(f32[2,768,3072]{2,1,0:T(8,128)} %fusion.157, bf16[2,768,768]{2,1,0:T(8,128)(2,1)S(1)} %bitcast.247, bf16[2,3072,768]{2,1,0:T(8,128)(2,1)} %all-gather.12.cloned.1.call-done), kind=kOutput, calls=%fused_computation.19 | convolution fusion | flops 7342129152 | bytes 40108032 | tf_op jit(solution)/shard_map/ecd,efd->ecf/dot_general | solution.py:338
  455.0 12.8 %convolution_convert_fusion.4 = bf16[2,768,768]{2,1,0:T(8,128)(2,1)S(1)} fusion(bf16[2,768,3072]{2,1,0:T(8,128)(2,1)} %fusion.14, bf16[2,768,3072]{2,1,0:T(8,128)(2,1)} %all-gather.10.cloned.1.call-done), kind=kOutput, calls=%fused_computation.103 | convolution fusion | flops 7248936960 | bytes 21233664 | tf_op jit(solution)/shard_map/ecf,edf->ecd/dot_general | solution.py:344
  472.4 12.8 %collective-permute-done.20 = bf16[384,768]{1,0:T(8,128)(2,1)S(1)} collective-permute-done((bf16[384,768]{1,0:T(8,128)(2,1)S(1)}, bf16[384,768]{1,0:T(8,128)(2,1)S(1)}, u32[]{:S(2)}, u32[]{:S(2)}) %collective-permute-start.20) | collective-permute-done | bytes 589856 | tf_op jit(solution)/shard_map/ppermute | solution.py:30
  485.2 11.7 %collective-permute-done.19 = bf16[384,768]{1,0:T(8,128)(2,1)S(1)} collective-permute-done((bf16[384,768]{1,0:T(8,128)(2,1)S(1)}, bf16[384,768]{1,0:T(8,128)(2,1)S(1)}, u32[]{:S(2)}, u32[]{:S(2)}) %collective-permute-start.19) | collective-permute-done | bytes 589856 | tf_op jit(solution)/shard_map/ppermute | solution.py:30
  501.7 7.8 fusion.66
  509.5 9.6 multiply_reduce_fusion
  519.1 7.1 multiply_convert_fusion.1
  551.2 6.0 multiply_reduce_fusion.2
  559.6 42.4 %collective-permute-done.25 = f32[8,2,768]{2,1,0:T(2,128)S(1)} collective-permute-done((f32[8,2,768]{2,1,0:T(2,128)S(1)}, f32[8,2,768]{2,1,0:T(2,128)S(1)}, u32[]{:S(2)}, u32[]{:S(2)}) %collective-permute-start.25) | collective-permute-done | bytes 49184 | tf_op jit(solution)/shard_map/ppermute | solution.py:30
  612.0 19.1 %convolution_convert_fusion = bf16[2,3072,768]{2,1,0:T(8,128)(2,1)} fusion(bf16[2,768,768]{2,1,0:T(8,128)(2,1)} %bitcast.248, f32[2,768,3072]{2,1,0:T(8,128)} %fusion.157), kind=kOutput, calls=%fused_computation.46 | convolution fusion | flops 7294943232 | bytes 30670848 | tf_op jit(solution)/shard_map/ecf,ecd->efd/dot_general | solution.py:335
  631.2 14.2 %convolution_convert_fusion.1 = bf16[2,768,3072]{2,1,0:T(8,128)(2,1)} fusion(bf16[2,768,768]{2,1,0:T(8,128)(2,1)} %bitcast.246, bf16[2,768,3072]{2,1,0:T(8,128)(2,1)} %fusion.14), kind=kOutput, calls=%fused_computation.47 | convolution fusion | flops 7252475904 | bytes 21233664 | tf_op jit(solution)/shard_map/ecd,ecf->edf/dot_general | solution.py:343
  651.7 10.3 %fusion.160 = f32[8000,768]{0,1:T(8,128)} fusion(bf16[256,8000]{0,1:T(8,128)(2,1)S(1)} %copy-done.1, bf16[256,768]{1,0:T(8,128)(2,1)S(1)} %copy-done.30), kind=kOutput, calls=%fused_computation.313 | convolution fusion | flops 3145728000 | bytes 29065216 | tf_op jit(solution)/shard_map/gv,gd->vd/dot_general | solution.py:297
  662.0 7.6 collective-permute-done.32
  669.6 10.0 %collective-permute-done.31 = bf16[512,768]{1,0:T(8,128)(2,1)S(1)} collective-permute-done((bf16[512,768]{1,0:T(8,128)(2,1)S(1)}, bf16[512,768]{1,0:T(8,128)(2,1)S(1)}, u32[]{:S(2)}, u32[]{:S(2)}) %collective-permute-start.31) | collective-permute-done | bytes 786464 | tf_op jit(solution)/shard_map/ppermute | solution.py:30
  679.9 37.1 %add_convert_fusion = bf16[8000,768]{0,1:T(8,128)(2,1)} fusion(f32[8000,768]{0,1:T(8,128)} %fusion.160, s32[2048]{0:T(1024)S(1)} %bitcast.286, bf16[2048,768]{1,0:T(8,128)(2,1)S(1)} %fusion.205), kind=kOutput, calls=%fused_computation.12 | convolution fusion | flops 25194496000 | bytes 40017920 | tf_op jit(solution)/shard_map/while/body/eval_jaxpr/tv,td->vd/dot_general | solution.py:414
  724.3 4.7 collective-permute-done.29
  729.0 5.4 collective-permute-done.28
  739.7 7.8 reduce-scatter.9.cloned.1.call-done
  747.5 4.6 fusion.140
  755.2 92.6 %reduce-scatter.7.cloned.1.call-done = bf16[2,96,3072]{2,1,0:T(8,128)(2,1)} async-done(((bf16[2,768,3072]{2,1,0:T(8,128)(2,1)}), bf16[2,96,3072]{2,1,0:T(8,128)(2,1)}) %reduce-scatter.7.cloned.1.call-update) | async-done | bytes 1179664 | tf_op jit(solution)/shard_map/reduce_scatter | solution.py:424
  847.8 4.6 fusion.142
  855.6 120.4 %reduce-scatter.11.cloned.1.call-done = bf16[8000,96]{0,1:T(8,128)(2,1)} async-done(((bf16[8000,768]{0,1:T(8,128)(2,1)}), bf16[8000,96]{0,1:T(8,128)(2,1)}) %reduce-scatter.11.cloned.1.call-update) | async-done | bytes 1536016 | tf_op jit(solution)/shard_map/reduce_scatter | solution.py:430
  976.0 5.4 fusion.138
  (402 shorter events, 185.6 us)
Async XLA Ops:
  7.2 123.8 %all-gather.8.cloned.1.call-start = ((), (), s32[]{:S(2)}) async-start(), calls=%async_computation.5 | async-start | bytes 1437696 | tf_op jit(solution)/shard_map/all_gather | solution.py:161
  9.7 238.2 %all-gather.10.cloned.1.call-start = ((), (), s32[]{:S(2)}) async-start(), calls=%async_computation.6 | async-start | bytes 10616832 | tf_op jit(solution)/shard_map/all_gather | solution.py:175
  12.7 250.7 %all-gather.12.cloned.1.call-start = ((), (), s32[]{:S(2)}) async-start(), calls=%async_computation.7 | async-start | bytes 10616832 | tf_op jit(solution)/shard_map/all_gather | solution.py:176
  15.7 329.2 %all-gather.14.cloned.1.call-start = ((), (), s32[]{:S(2)}) async-start(), calls=%async_computation.8 | async-start | bytes 13934592 | tf_op jit(solution)/shard_map/all_gather | solution.py:177
  17.1 38.8 %collective-permute-start.5 = (bf16[8000,96]{0,1:T(8,128)(2,1)}, bf16[8000,96]{0,1:T(8,128)(2,1)S(1)}, u32[]{:S(2)}, u32[]{:S(2)}) collective-permute-start(bf16[8000,96]{0,1:T(8,128)(2,1)} %convert_element_type.201), channel_id=1, source_target_pairs={{0,3},{1,2},{2,1},{3,0},{4,7},{5,6},{6,5},{7,4},{8,11},{9,10},{10,... | collective-permute-start | bytes 4608008 | tf_op jit(solution)/shard_map/ppermute | solution.py:30
  21.0 67.4 %collective-permute-start.4 = (bf16[8000,96]{0,1:T(8,128)(2,1)}, bf16[8000,96]{0,1:T(8,128)(2,1)}, u32[]{:S(2)}, u32[]{:S(2)}) collective-permute-start(bf16[8000,96]{0,1:T(8,128)(2,1)} %convert_element_type.201), channel_id=1, source_target_pairs={{0,2},{1,3},{2,0},{3,1},{4,6},{5,7},{6,4},{7,5},{8,10},{9,11},{10,... | collective-permute-start | bytes 4608008 | tf_op jit(solution)/shard_map/ppermute | solution.py:30
  21.5 67.1 %collective-permute-start.3 = (bf16[8000,96]{0,1:T(8,128)(2,1)}, bf16[8000,96]{0,1:T(8,128)(2,1)}, u32[]{:S(2)}, u32[]{:S(2)}) collective-permute-start(bf16[8000,96]{0,1:T(8,128)(2,1)} %convert_element_type.201), channel_id=1, source_target_pairs={{0,1},{1,0},{2,3},{3,2},{4,5},{5,4},{6,7},{7,6},{8,9},{9,8},{10,11... | collective-permute-start | bytes 4608008 | tf_op jit(solution)/shard_map/ppermute | solution.py:30
  37.4 162.8 %copy-start.19 = (pred[512,512]{0,1:T(8,128)(4,1)}, pred[512,512]{0,1:T(8,128)(4,1)S(1)}, u32[]{:S(2)}) copy-start(pred[512,512]{0,1:T(8,128)(4,1)S(1)} %fusion.81) | copy-start | bytes 786436
  125.7 39.9 %all-to-all-start = ((bf16[8,512,96]{1,2,0:T(8,128)(2,1)}), bf16[8,512,96]{1,2,0:T(8,128)(2,1)S(1)}, u32[]{:S(2)}, u32[]{:S(2)}) async-start(bf16[8,512,96]{1,2,0:T(8,128)(2,1)} %copy.225), calls=%async_computation | async-start | bytes 1572864 | tf_op jit(solution)/shard_map/all_to_all | solution.py:193
  130.6 586.5 %reduce-scatter.5.cloned.1.call-start = ((), (), s32[]{:S(2)}) async-start(), calls=%async_computation.9 | async-start | bytes 2875392 | tf_op jit(solution)/shard_map/reduce_scatter | solution.py:462
  133.9 35.2 %collective-permute-start.1 = (bf16[8,96,768]{2,1,0:T(8,128)(2,1)}, bf16[8,96,768]{2,1,0:T(8,128)(2,1)}, u32[]{:S(2)}, u32[]{:S(2)}) collective-permute-start(bf16[8,96,768]{2,1,0:T(8,128)(2,1)} %get-tuple-element.149), channel_id=1, source_target_pairs={{0,2},{1,3},{2,0},{3,1},{4,6},{5,7},{6,4},{7,5},{8,10},{9,11},{10,... | collective-permute-start | bytes 3538952 | tf_op jit(solution)/shard_map/ppermute | solution.py:30
  135.3 33.8 %collective-permute-start = (bf16[8,96,768]{2,1,0:T(8,128)(2,1)}, bf16[8,96,768]{2,1,0:T(8,128)(2,1)}, u32[]{:S(2)}, u32[]{:S(2)}) collective-permute-start(bf16[8,96,768]{2,1,0:T(8,128)(2,1)} %get-tuple-element.149), channel_id=1, source_target_pairs={{0,1},{1,0},{2,3},{3,2},{4,5},{5,4},{6,7},{7,6},{8,9},{9,8},{10,11... | collective-permute-start | bytes 3538952 | tf_op jit(solution)/shard_map/ppermute | solution.py:30
  136.3 52.7 %collective-permute-start.2 = (bf16[8,96,768]{2,1,0:T(8,128)(2,1)}, bf16[8,96,768]{2,1,0:T(8,128)(2,1)}, u32[]{:S(2)}, u32[]{:S(2)}) collective-permute-start(bf16[8,96,768]{2,1,0:T(8,128)(2,1)} %get-tuple-element.149), channel_id=1, source_target_pairs={{0,3},{1,2},{2,1},{3,0},{4,7},{5,6},{6,5},{7,4},{8,11},{9,10},{10,... | collective-permute-start | bytes 3538952 | tf_op jit(solution)/shard_map/ppermute | solution.py:30
  139.0 29.8 %copy-start.48 = (bf16[8,11,96]{2,1,0:T(8,128)(2,1)}, bf16[8,11,96]{2,1,0:T(8,128)(2,1)S(1)}, u32[]{:S(2)}) copy-start(bf16[8,11,96]{2,1,0:T(8,128)(2,1)S(1)} %reshape.481) | copy-start | bytes 50692
  168.8 37.4 %copy-start.4 = (f32[512,768]{1,0:T(8,128)}, f32[512,768]{1,0:T(8,128)S(1)}, u32[]{:S(2)}) copy-start(f32[512,768]{1,0:T(8,128)S(1)} %copy.227) | copy-start | bytes 4718596
  210.8 33.8 %collective-permute-start.8 = (bf16[384,768]{1,0:T(8,128)(2,1)}, bf16[384,768]{1,0:T(8,128)(2,1)}, u32[]{:S(2)}, u32[]{:S(2)}) collective-permute-start(bf16[384,768]{1,0:T(8,128)(2,1)} %get-tuple-element.142), channel_id=1, source_target_pairs={{0,3},{1,2},{2,1},{3,0},{4,7},{5,6},{6,5},{7,4},{8,11},{9,10},{10,... | collective-permute-start | bytes 1769480 | tf_op jit(solution)/shard_map/ppermute | solution.py:30
  212.7 32.0 %collective-permute-start.7 = (bf16[384,768]{1,0:T(8,128)(2,1)}, bf16[384,768]{1,0:T(8,128)(2,1)}, u32[]{:S(2)}, u32[]{:S(2)}) collective-permute-start(bf16[384,768]{1,0:T(8,128)(2,1)} %get-tuple-element.143), channel_id=1, source_target_pairs={{0,2},{1,3},{2,0},{3,1},{4,6},{5,7},{6,4},{7,5},{8,10},{9,11},{10,... | collective-permute-start | bytes 1769480 | tf_op jit(solution)/shard_map/ppermute | solution.py:30
  213.8 30.9 %collective-permute-start.6 = (bf16[384,768]{1,0:T(8,128)(2,1)}, bf16[384,768]{1,0:T(8,128)(2,1)}, u32[]{:S(2)}, u32[]{:S(2)}) collective-permute-start(bf16[384,768]{1,0:T(8,128)(2,1)} %get-tuple-element.144), channel_id=1, source_target_pairs={{0,1},{1,0},{2,3},{3,2},{4,5},{5,4},{6,7},{7,6},{8,9},{9,8},{10,11... | collective-permute-start | bytes 1769480 | tf_op jit(solution)/shard_map/ppermute | solution.py:30
  279.8 17.4 %collective-permute-start.11 = (bf16[384,768]{1,0:T(8,128)(2,1)}, bf16[384,768]{1,0:T(8,128)(2,1)S(1)}, u32[]{:S(2)}, u32[]{:S(2)}) collective-permute-start(bf16[384,768]{1,0:T(8,128)(2,1)} %bitcast.44), channel_id=1, source_target_pairs={{0,3},{1,2},{2,1},{3,0},{4,7},{5,6},{6,5},{7,4},{8,11},{9,10},{10,... | collective-permute-start | bytes 1769480 | tf_op jit(solution)/shard_map/ppermute | solution.py:30
  281.8 25.6 %collective-permute-start.10 = (bf16[384,768]{1,0:T(8,128)(2,1)}, bf16[384,768]{1,0:T(8,128)(2,1)}, u32[]{:S(2)}, u32[]{:S(2)}) collective-permute-start(bf16[384,768]{1,0:T(8,128)(2,1)} %bitcast.42), channel_id=1, source_target_pairs={{0,2},{1,3},{2,0},{3,1},{4,6},{5,7},{6,4},{7,5},{8,10},{9,11},{10,... | collective-permute-start | bytes 1769480 | tf_op jit(solution)/shard_map/ppermute | solution.py:30
  282.9 24.5 %collective-permute-start.9 = (bf16[384,768]{1,0:T(8,128)(2,1)S(1)}, bf16[384,768]{1,0:T(8,128)(2,1)}, u32[]{:S(2)}, u32[]{:S(2)}) collective-permute-start(bf16[384,768]{1,0:T(8,128)(2,1)S(1)} %bitcast.258), channel_id=1, source_target_pairs={{0,1},{1,0},{2,3},{3,2},{4,5},{5,4},{6,7},{7,6},{8,9},{9,8},{10,11... | collective-permute-start | bytes 1769480 | tf_op jit(solution)/shard_map/ppermute | solution.py:30
  283.4 27.1 %copy-start.77 = (f32[512,1]{0,1:T(1,128)}, f32[512,1]{0,1:T(1,128)S(1)}, u32[]{:S(2)}) copy-start(f32[512,1]{0,1:T(1,128)S(1)} %get-tuple-element.183) | copy-start | bytes 6148
  384.6 7.4 collective-permute-start.12
  386.1 9.1 collective-permute-start.14
  387.5 9.0 collective-permute-start.13
  404.8 17.5 %collective-permute-start.17 = (bf16[384,768]{1,0:T(8,128)(2,1)}, bf16[384,768]{1,0:T(8,128)(2,1)}, u32[]{:S(2)}, u32[]{:S(2)}) collective-permute-start(bf16[384,768]{1,0:T(8,128)(2,1)} %get-tuple-element.134), channel_id=1, source_target_pairs={{0,3},{1,2},{2,1},{3,0},{4,7},{5,6},{6,5},{7,4},{8,11},{9,10},{10,... | collective-permute-start | bytes 1769480 | tf_op jit(solution)/shard_map/ppermute | solution.py:30
  406.2 23.9 %collective-permute-start.16 = (bf16[384,768]{1,0:T(8,128)(2,1)}, bf16[384,768]{1,0:T(8,128)(2,1)}, u32[]{:S(2)}, u32[]{:S(2)}) collective-permute-start(bf16[384,768]{1,0:T(8,128)(2,1)} %get-tuple-element.135), channel_id=1, source_target_pairs={{0,2},{1,3},{2,0},{3,1},{4,6},{5,7},{6,4},{7,5},{8,10},{9,11},{10,... | collective-permute-start | bytes 1769480 | tf_op jit(solution)/shard_map/ppermute | solution.py:30
  406.8 23.4 %collective-permute-start.15 = (bf16[384,768]{1,0:T(8,128)(2,1)}, bf16[384,768]{1,0:T(8,128)(2,1)}, u32[]{:S(2)}, u32[]{:S(2)}) collective-permute-start(bf16[384,768]{1,0:T(8,128)(2,1)} %get-tuple-element.136), channel_id=1, source_target_pairs={{0,1},{1,0},{2,3},{3,2},{4,5},{5,4},{6,7},{7,6},{8,9},{9,8},{10,11... | collective-permute-start | bytes 1769480 | tf_op jit(solution)/shard_map/ppermute | solution.py:30
  468.0 17.2 %collective-permute-start.20 = (bf16[384,768]{1,0:T(8,128)(2,1)S(1)}, bf16[384,768]{1,0:T(8,128)(2,1)S(1)}, u32[]{:S(2)}, u32[]{:S(2)}) collective-permute-start(bf16[384,768]{1,0:T(8,128)(2,1)S(1)} %bitcast.262), channel_id=1, source_target_pairs={{0,3},{1,2},{2,1},{3,0},{4,7},{5,6},{6,5},{7,4},{8,11},{9,10},{10,... | collective-permute-start | bytes 1769480 | tf_op jit(solution)/shard_map/ppermute | solution.py:30
  469.5 27.3 %collective-permute-start.19 = (bf16[384,768]{1,0:T(8,128)(2,1)S(1)}, bf16[384,768]{1,0:T(8,128)(2,1)S(1)}, u32[]{:S(2)}, u32[]{:S(2)}) collective-permute-start(bf16[384,768]{1,0:T(8,128)(2,1)S(1)} %bitcast.260), channel_id=1, source_target_pairs={{0,2},{1,3},{2,0},{3,1},{4,6},{5,7},{6,4},{7,5},{8,10},{9,11},{10,... | collective-permute-start | bytes 1769480 | tf_op jit(solution)/shard_map/ppermute | solution.py:30
  470.1 26.7 %collective-permute-start.18 = (bf16[384,768]{1,0:T(8,128)(2,1)S(1)}, bf16[384,768]{1,0:T(8,128)(2,1)S(1)}, u32[]{:S(2)}, u32[]{:S(2)}) collective-permute-start(bf16[384,768]{1,0:T(8,128)(2,1)S(1)} %bitcast.256), channel_id=1, source_target_pairs={{0,1},{1,0},{2,3},{3,2},{4,5},{5,4},{6,7},{7,6},{8,9},{9,8},{10,11... | collective-permute-start | bytes 1769480 | tf_op jit(solution)/shard_map/ppermute | solution.py:30
  546.7 60.3 %collective-permute-start.21 = (bf16[8,96,768]{2,1,0:T(8,128)(2,1)}, bf16[8,96,768]{2,1,0:T(8,128)(2,1)}, u32[]{:S(2)}, u32[]{:S(2)}) collective-permute-start(bf16[8,96,768]{2,1,0:T(8,128)(2,1)} %get-tuple-element.122), channel_id=1, source_target_pairs={{0,1},{1,0},{2,3},{3,2},{4,5},{5,4},{6,7},{7,6},{8,9},{9,8},{10,11... | collective-permute-start | bytes 3538952 | tf_op jit(solution)/shard_map/ppermute | solution.py:30
  547.3 59.7 %collective-permute-start.22 = (bf16[8,96,768]{2,1,0:T(8,128)(2,1)}, bf16[8,96,768]{2,1,0:T(8,128)(2,1)}, u32[]{:S(2)}, u32[]{:S(2)}) collective-permute-start(bf16[8,96,768]{2,1,0:T(8,128)(2,1)} %get-tuple-element.123), channel_id=1, source_target_pairs={{0,2},{1,3},{2,0},{3,1},{4,6},{5,7},{6,4},{7,5},{8,10},{9,11},{10,... | collective-permute-start | bytes 3538952 | tf_op jit(solution)/shard_map/ppermute | solution.py:30
  548.7 58.3 %collective-permute-start.23 = (bf16[8,96,768]{2,1,0:T(8,128)(2,1)}, bf16[8,96,768]{2,1,0:T(8,128)(2,1)}, u32[]{:S(2)}, u32[]{:S(2)}) collective-permute-start(bf16[8,96,768]{2,1,0:T(8,128)(2,1)} %get-tuple-element.124), channel_id=1, source_target_pairs={{0,3},{1,2},{2,1},{3,0},{4,7},{5,6},{6,5},{7,4},{8,11},{9,10},{10,... | collective-permute-start | bytes 3538952 | tf_op jit(solution)/shard_map/ppermute | solution.py:30
  557.5 44.4 %collective-permute-start.25 = (f32[8,2,768]{2,1,0:T(2,128)S(1)}, f32[8,2,768]{2,1,0:T(2,128)S(1)}, u32[]{:S(2)}, u32[]{:S(2)}) collective-permute-start(f32[8,2,768]{2,1,0:T(2,128)S(1)} %copy.252), channel_id=1, source_target_pairs={{0,2},{1,3},{2,0},{3,1},{4,6},{5,7},{6,4},{7,5},{8,10},{9,11},{10,... | collective-permute-start | bytes 147464 | tf_op jit(solution)/shard_map/ppermute | solution.py:30
  558.2 45.2 %collective-permute-start.24 = (f32[8,2,768]{2,1,0:T(2,128)S(1)}, f32[8,2,768]{2,1,0:T(2,128)S(1)}, u32[]{:S(2)}, u32[]{:S(2)}) collective-permute-start(f32[8,2,768]{2,1,0:T(2,128)S(1)} %copy.252), channel_id=1, source_target_pairs={{0,1},{1,0},{2,3},{3,2},{4,5},{5,4},{6,7},{7,6},{8,9},{9,8},{10,11... | collective-permute-start | bytes 147464 | tf_op jit(solution)/shard_map/ppermute | solution.py:30
  602.0 5.0 collective-permute-start.26
  612.0 135.5 %reduce-scatter.9.cloned.1.call-start = ((), (), s32[]{:S(2)}) async-start(), calls=%async_computation.11 | async-start | bytes 10616832 | tf_op jit(solution)/shard_map/reduce_scatter | solution.py:427
  631.1 216.7 %reduce-scatter.7.cloned.1.call-start = ((), (), s32[]{:S(2)}) async-start(), calls=%async_computation.10 | async-start | bytes 10616832 | tf_op jit(solution)/shard_map/reduce_scatter | solution.py:424
  645.4 330.6 %reduce-scatter.11.cloned.1.call-start = ((), (), s32[]{:S(2)}) async-start(), calls=%async_computation.12 | async-start | bytes 13934592 | tf_op jit(solution)/shard_map/reduce_scatter | solution.py:430
  648.1 21.4 %collective-permute-start.32 = (bf16[512,768]{1,0:T(8,128)(2,1)S(1)}, bf16[512,768]{1,0:T(8,128)(2,1)S(1)}, u32[]{:S(2)}, u32[]{:S(2)}) collective-permute-start(bf16[512,768]{1,0:T(8,128)(2,1)S(1)} %add_convert_fusion.2), channel_id=1, source_target_pairs={{0,3},{1,2},{2,1},{3,0},{4,7},{5,6},{6,5},{7,4},{8,11},{9,10},{10,... | collective-permute-start | bytes 2359304 | tf_op jit(solution)/shard_map/ppermute | solution.py:30
  649.4 30.1 %collective-permute-start.31 = (bf16[512,768]{1,0:T(8,128)(2,1)S(1)}, bf16[512,768]{1,0:T(8,128)(2,1)S(1)}, u32[]{:S(2)}, u32[]{:S(2)}) collective-permute-start(bf16[512,768]{1,0:T(8,128)(2,1)S(1)} %add_convert_fusion.2), channel_id=1, source_target_pairs={{0,2},{1,3},{2,0},{3,1},{4,6},{5,7},{6,4},{7,5},{8,10},{9,11},{10,... | collective-permute-start | bytes 2359304 | tf_op jit(solution)/shard_map/ppermute | solution.py:30
  651.1 28.5 %collective-permute-start.30 = (bf16[512,768]{1,0:T(8,128)(2,1)S(1)}, bf16[512,768]{1,0:T(8,128)(2,1)S(1)}, u32[]{:S(2)}, u32[]{:S(2)}) collective-permute-start(bf16[512,768]{1,0:T(8,128)(2,1)S(1)} %add_convert_fusion.2), channel_id=1, source_target_pairs={{0,1},{1,0},{2,3},{3,2},{4,5},{5,4},{6,7},{7,6},{8,9},{9,8},{10,11... | collective-permute-start | bytes 2359304 | tf_op jit(solution)/shard_map/ppermute | solution.py:30
  718.1 10.9 %collective-permute-start.29 = (f32[96,768]{1,0:T(8,128)S(1)}, f32[96,768]{1,0:T(8,128)S(1)}, u32[]{:S(2)}, u32[]{:S(2)}) collective-permute-start(f32[96,768]{1,0:T(8,128)S(1)} %get-tuple-element.158), channel_id=1, source_target_pairs={{0,3},{1,2},{2,1},{3,0},{4,7},{5,6},{6,5},{7,4},{8,11},{9,10},{10,... | collective-permute-start | bytes 884744 | tf_op jit(solution)/shard_map/ppermute | solution.py:30
  719.6 14.8 %collective-permute-start.28 = (f32[96,768]{1,0:T(8,128)S(1)}, f32[96,768]{1,0:T(8,128)S(1)}, u32[]{:S(2)}, u32[]{:S(2)}) collective-permute-start(f32[96,768]{1,0:T(8,128)S(1)} %get-tuple-element.158), channel_id=1, source_target_pairs={{0,2},{1,3},{2,0},{3,1},{4,6},{5,7},{6,4},{7,5},{8,10},{9,11},{10,... | collective-permute-start | bytes 884744 | tf_op jit(solution)/shard_map/ppermute | solution.py:30
  721.1 13.3 %collective-permute-start.27 = (f32[96,768]{1,0:T(8,128)S(1)}, f32[96,768]{1,0:T(8,128)S(1)}, u32[]{:S(2)}, u32[]{:S(2)}) collective-permute-start(f32[96,768]{1,0:T(8,128)S(1)} %get-tuple-element.158), channel_id=1, source_target_pairs={{0,1},{1,0},{2,3},{3,2},{4,5},{5,4},{6,7},{7,6},{8,9},{9,8},{10,11... | collective-permute-start | bytes 884744 | tf_op jit(solution)/shard_map/ppermute | solution.py:30
  753.5 94.3 %copy-start.16 = (f32[2,96,3072]{2,1,0:T(8,128)S(1)}, f32[2,96,3072]{2,1,0:T(8,128)}, u32[]{:S(2)}) copy-start(f32[2,96,3072]{2,1,0:T(8,128)} %param.32) | copy-start | bytes 7077892
  853.9 122.1 %copy-start.9 = (f32[8000,96]{0,1:T(8,128)S(1)}, f32[8000,96]{0,1:T(8,128)}, u32[]{:S(2)}) copy-start(f32[8000,96]{0,1:T(8,128)} %param.38) | copy-start | bytes 9216004
  (82 other events, 610.1 us)
Sparse Core Ops, SparseCore 0:
  10.2 26.1 all-gather.7
  38.6 90.0 all-gather.9
  130.9 98.4 all-gather.11
  231.5 113.3 all-gather.13
  612.1 34.4 reduce-scatter.4
  648.9 98.5 reduce-scatter.8
  749.9 97.8 reduce-scatter.6
  850.3 125.6 reduce-scatter.10

commit v3 on v2

--- a/solution.py
+++ b/solution.py
@@ -3,6 +3,8 @@
 import jax
 import jax.numpy as jnp
 from jax import lax
+from jax.experimental import pallas as pl
+from jax.experimental.pallas import tpu as pltpu
 from jax.sharding import PartitionSpec as P
 
 HEAD = 64
@@ -28,6 +30,10 @@
 
 def swap(value, k, members):
     return value if k == 0 else lax.ppermute(value, "expert", partner_order(members)[k])
+
+
+def dp_swap(value, k, replicas):
+    return lax.ppermute(value, "dp", [(i, i ^ k) for i in range(replicas)]) if k else value
 
 
 def in_order(parts, me):
@@ -77,15 +83,19 @@
     return (jnp.where(allowed[None], scores, MASKED_SCORE), query, keys, first_row)
 
 
+def in_thirds(values):
+    parts = []
+    for _ in range(3):
+        part = lax.reduce_precision(values, 8, 7)
+        parts.append(part)
+        values = values - part
+    return parts
+
+
 def label_weights(ids, weights, vocab_rows):
     lanes = 128
     tiles = (vocab_rows + lanes - 1) // lanes
-    parts = []
-    rest = weights
-    for _ in range(3):
-        part = lax.reduce_precision(rest, 8, 7)
-        parts.append(part)
-        rest = rest - part
+    parts = in_thirds(weights)
     high = jnp.arange(tiles, dtype=jnp.int32)
     low = jnp.arange(lanes, dtype=jnp.int32)
     high_hits = (ids >> 7)[:, :, None] == high[None, None, :]
@@ -96,6 +106,113 @@
     columns = jnp.concatenate([columns] * len(parts), axis=1)
     spread = jnp.einsum("pih,pil->phl", rows, columns, preferred_element_type=jnp.float32)
     return spread.reshape(ids.shape[0], tiles * lanes)[:, :vocab_rows]
+
+
+LANES = 128
+WAYS = 4
+GRID_ROWS = 32768
+VMEM_LIMIT = 56 * 2**20
+
+
+def add_rows_kernel(count_ref, row_ref, source_ref, *refs):
+    pieces = len(refs) - 2 - WAYS
+    grad_refs, out_ref, grads, sums = refs[:pieces], refs[pieces], refs[pieces + 1], refs[-WAYS:]
+    start_ref = None
+    if grad_refs[-1].dtype == jnp.float32:
+        start_ref, grad_refs = grad_refs[-1], grad_refs[:-1]
+    width, piece = grad_refs[0].shape
+    pad = jnp.zeros((LANES - width, LANES), jnp.float32)
+    for k, grad_ref in enumerate(grad_refs):
+
+        def turn(i, _, k=k, grad_ref=grad_ref):
+            lanes = pl.ds(pl.multiple_of(i * LANES, LANES), LANES)
+            tile = jnp.concatenate([grad_ref[:, lanes].astype(jnp.float32), pad], axis=0)
+            grads[pl.ds(pl.multiple_of(k * piece + i * LANES, LANES), LANES), :] = tile.T
+            return 0
+
+        lax.fori_loop(0, piece // LANES, turn, 0)
+    step = 64
+    for total in sums:
+
+        def clear(i, _, total=total):
+            total[pl.ds(pl.multiple_of(i * step, step), step), :] = jnp.zeros(
+                (step, LANES), jnp.float32
+            )
+            return 0
+
+        lax.fori_loop(0, total.shape[0] // step, clear, 0)
+
+    def one_block(b, _):
+        def one_step(i, _):
+            for w in range(WAYS):
+                row = row_ref[b, i * WAYS + w]
+                source = source_ref[b, i * WAYS + w]
+                sums[w][pl.ds(row, 1), :] += grads[pl.ds(source, 1), :]
+            return 0
+
+        return lax.fori_loop(0, count_ref[b], one_step, 0)
+
+    lax.fori_loop(0, row_ref.shape[0], one_block, 0)
+
+    def finish(i, _):
+        place = pl.ds(pl.multiple_of(i * LANES, LANES), LANES)
+        total = sum(part[place, :] for part in sums)
+        if start_ref is None:
+            out_ref[place, :] = total
+        else:
+            out_ref[:, place] = (total + start_ref[place, :]).T[:width]
+        return 0
+
+    lax.fori_loop(0, sums[0].shape[0] // LANES, finish, 0)
+
+
+def row_lists(local_ids, vocab_rows, offset):
+    ids = local_ids.reshape(-1, LANES)
+    inside = (ids >= 0) & (ids < vocab_rows)
+    place = jnp.arange(LANES, dtype=jnp.int32)
+    earlier = (place[:, None] < place[None, :]).astype(jnp.bfloat16)
+    before = jnp.dot(inside.astype(jnp.bfloat16), earlier, preferred_element_type=jnp.float32)
+    chosen = inside[:, :, None] & (before.astype(jnp.int32)[:, :, None] == place[None, None, :])
+    filled = jnp.sum(chosen.astype(jnp.int32), axis=1)
+    rows = jnp.sum(jnp.where(chosen, ids[:, :, None], 0), axis=1)
+    rows = jnp.where(filled > 0, rows, vocab_rows)
+    origin = jnp.sum(jnp.where(chosen, place[None, :, None], 0), axis=1)
+    origin = origin + offset + jnp.arange(ids.shape[0], dtype=jnp.int32)[:, None] * LANES
+    counts = (jnp.sum(inside.astype(jnp.int32), axis=1) + WAYS - 1) // WAYS
+    return counts, rows, origin
+
+
+def add_rows(local_ids, grads, vocab_rows, start):
+    width, piece = grads[0].shape
+    if piece * len(grads) * 2 > GRID_ROWS or width > LANES or piece % LANES:
+        vocab_iota = jnp.arange(vocab_rows, dtype=jnp.int32)
+        total = jnp.zeros((width, vocab_rows), jnp.float32) if start is None else start
+        for ids, part in zip(local_ids, grads):
+            hits = (ids[:, None] == vocab_iota[None, :]).astype(jnp.bfloat16)
+            total = total + jnp.dot(part, hits, preferred_element_type=jnp.float32)
+        return total
+    lists = [row_lists(ids, vocab_rows, k * piece) for k, ids in enumerate(local_ids)]
+    lists = [jnp.concatenate(parts, axis=0) for parts in zip(*lists)]
+    smem = pl.BlockSpec(memory_space=pltpu.SMEM)
+    vmem = pl.BlockSpec(memory_space=pltpu.VMEM)
+    padded_rows = -(-(vocab_rows + 1) // LANES) * LANES
+    extra = [] if start is None else [start]
+    shape = (padded_rows, LANES) if start is None else (width, padded_rows)
+    summed = pl.pallas_call(
+        add_rows_kernel,
+        out_shape=jax.ShapeDtypeStruct(shape, jnp.float32),
+        in_specs=[smem] * 3 + [vmem] * (len(grads) + len(extra)),
+        out_specs=vmem,
+        scratch_shapes=[pltpu.VMEM((len(grads) * piece, LANES), jnp.float32)]
+        + [pltpu.VMEM((padded_rows, LANES), jnp.float32) for _ in range(WAYS)],
+        compiler_params=pltpu.CompilerParams(vmem_limit_bytes=VMEM_LIMIT),
+        cost_estimate=pl.CostEstimate(
+            flops=len(grads) * piece * LANES * 8,
+            bytes_accessed=4 * LANES * (2 * len(grads) * piece + 3 * WAYS * padded_rows) * 4,
+            transcendentals=0,
+        ),
+    )(*lists, *grads, *extra)
+    return summed if start is None else summed[:, :vocab_rows]
 
 
 def nesterov_update(master, moment, average, grad, rate):
@@ -146,9 +263,6 @@
     block_count = local_rows // block_rows
     scaling = HEAD ** (-0.5)
     highest_precision = lax.Precision.HIGHEST
-    group_count = members * local_rows
-    lookup_rows = math.gcd(group_count, 2048)
-    vocab_iota = jnp.arange(vocab_rows, dtype=jnp.int32)
     share = width // replicas
     chunk = attention.shape[0] * share // members
     small_rows = small_params.size // width + 1
@@ -158,38 +272,63 @@
     dense_part = lax.dynamic_slice_in_dim(
         attention.reshape(attention.shape[0] * share, width), my_index * chunk, chunk, 0
     )
-    dense_part = lax.all_gather(
-        jnp.concatenate([dense_part, small_flat], axis=0).astype(jnp.bfloat16), "dp", axis=0
-    )
-    small_low = dense_part[:, chunk:].reshape(replicas, small_rows * width)
-    small_low = small_low[:, : small_params.size].reshape(replicas, small_params.shape[0], share)
-    small_low = small_low.transpose(1, 0, 2).reshape(small_params.shape[0], width)
-    dense_parts = in_order(shared(dense_part[:, :chunk], members), my_index)
-    dense_low = (
-        dense_parts.transpose(1, 0, 2, 3)
-        .reshape(replicas, attention.shape[0], share, width)
-        .transpose(1, 0, 2, 3)
-        .reshape(attention.shape[0], width, width)
-    )
     in_low, out_low, table_low = (
         lax.all_gather(expert_in.astype(jnp.bfloat16), "dp", axis=1, tiled=True),
         lax.all_gather(expert_out.astype(jnp.bfloat16), "dp", axis=1, tiled=True),
         lax.all_gather(embedding.astype(jnp.bfloat16), "dp", axis=1, tiled=True),
     )
-    gain_rows = small_low[:3].astype(jnp.float32)
-    router = small_low[3:].astype(jnp.float32)
+    core = lax.axis_index("dp") & 1
+    level = lax.axis_index("dp") >> 1
+    levels = replicas // 2
+
+    def by_core(value, axis):
+        other = dp_swap(value, 1, replicas)
+        first = jnp.where(core == 0, value, other)
+        return jnp.stack([first, jnp.where(core == 0, other, value)], axis=axis)
+
     group_ids = token_ids.reshape(-1)
     own_routes = lax.dynamic_slice_in_dim(
         routes.reshape(members * local_rows, TOP), my_index * local_rows, local_rows, 0
     )
-    local_ids = group_ids - my_index * vocab_rows
-    id_blocks = local_ids.reshape(group_count // lookup_rows, lookup_rows)
-    own_ids = lax.dynamic_slice_in_dim(group_ids, my_index * local_rows, local_rows, 0)
-    column_ids = lax.all_gather(own_ids, "dp", axis=0, tiled=True)
-    rows_table = jnp.concatenate(shared(embedding.astype(jnp.bfloat16), members), axis=0)
+    target_local = targets - my_index * vocab_rows
+    teacher_local = teacher_ids - my_index * vocab_rows
+    taken = label_weights(
+        jnp.concatenate([teacher_local, target_local[:, None]], axis=1),
+        jnp.concatenate([teacher_probs, jnp.ones_like(teacher_probs[:, :1])], axis=1),
+        vocab_rows,
+    )
+    rows_parts = shared(embedding.astype(jnp.bfloat16), members)
+    dense_part = jnp.concatenate([dense_part, small_flat], axis=0).astype(jnp.bfloat16)
+    dense_part, group_ids, rows_parts[1] = lax.optimization_barrier(
+        (dense_part, group_ids, rows_parts[1])
+    )
+    level_ids = in_order([dp_swap(group_ids, 2 * k, replicas) for k in range(levels)], level)
+    all_ids = by_core(level_ids, 1).reshape(replicas, members, local_rows)
+    column_ids = lax.dynamic_index_in_dim(all_ids, my_index, 1, keepdims=False).reshape(-1)
+    dense_part = in_order([dp_swap(dense_part, 2 * k, replicas) for k in range(levels)], level)
+    rows_parts[-1], taken, dense_part = lax.optimization_barrier(
+        (rows_parts[-1], taken, dense_part)
+    )
+
+    small_low = by_core(dense_part[:, chunk:], 1).reshape(replicas, small_rows * width)
+    small_low = small_low[:, : small_params.size].reshape(replicas, small_params.shape[0], share)
+    small_low = small_low.transpose(1, 0, 2).reshape(small_params.shape[0], width)
+    gain_rows = small_low[:3].astype(jnp.float32)
+    router = small_low[3:].astype(jnp.float32)
+    rows_table = jnp.concatenate(rows_parts, axis=0)
     places = partner_of(my_index, column_ids // vocab_rows, members) * vocab_rows
     places = places + column_ids % vocab_rows
     stream_parts = jnp.take(rows_table, places, axis=0, mode="clip")
+    dense_parts = shared(dense_part[:, :chunk], members)
+    stream_parts, dense_parts = lax.optimization_barrier((stream_parts, dense_parts))
+    dense_low = by_core(in_order(dense_parts, my_index), 2)
+    dense_low = (
+        dense_low.reshape(members, replicas, chunk, width)
+        .transpose(1, 0, 2, 3)
+        .reshape(replicas, attention.shape[0], share, width)
+        .transpose(1, 0, 2, 3)
+        .reshape(attention.shape[0], width, width)
+    )
     stream = lax.all_to_all(
         stream_parts, "dp", split_axis=0, concat_axis=1, tiled=True
     ).astype(jnp.float32)
@@ -272,13 +411,6 @@
     ).astype(jnp.bfloat16)
     group_final = lax.all_gather(final_rows, "expert", axis=0, tiled=True)
     logits = jnp.einsum("gd,vd->gv", group_final, table_low, preferred_element_type=jnp.float32)
-    target_local = targets - my_index * vocab_rows
-    teacher_local = teacher_ids - my_index * vocab_rows
-    taken = label_weights(
-        jnp.concatenate([teacher_local, target_local[:, None]], axis=1),
-        jnp.concatenate([teacher_probs, jnp.ones_like(teacher_probs[:, :1])], axis=1),
-        vocab_rows,
-    )
     taught = jnp.sum(taken * logits, axis=1)
     local_max = jnp.max(logits, axis=1)
     local_total = jnp.sum(jnp.exp(logits - local_max[:, None]), axis=1)
@@ -296,8 +428,10 @@
     logit_grad = ((2.0 * soft - taken) / loss_count).astype(jnp.bfloat16)
     embed_head = jnp.einsum(
         "gv,gd->vd", logit_grad, group_final, preferred_element_type=jnp.float32
-    )
-    final_parts = jnp.dot(logit_grad, table_low, preferred_element_type=jnp.float32)
+    ).astype(jnp.bfloat16)
+    embed_head, head_grad = lax.optimization_barrier((embed_head, logit_grad))
+    embed_sum = lax.psum_scatter(embed_head, "dp", scatter_dimension=1, tiled=True)
+    final_parts = jnp.dot(head_grad, table_low, preferred_element_type=jnp.float32)
     final_grad = sum(
         swap(
             lax.dynamic_slice_in_dim(
@@ -343,6 +477,11 @@
     in_grad = jnp.einsum("ecd,ecf->edf", arrived, hidden_grad, preferred_element_type=jnp.float32)
     rows_grad = jnp.einsum("ecf,edf->ecd", hidden_grad, in_low, preferred_element_type=jnp.float32)
     back_rows = sent_back(rows_grad.astype(jnp.bfloat16))
+    back_rows, out_grad, in_grad, embed_sum = lax.optimization_barrier(
+        (back_rows, out_grad.astype(jnp.bfloat16), in_grad.astype(jnp.bfloat16), embed_sum)
+    )
+    out_sum = lax.psum_scatter(out_grad, "dp", scatter_dimension=1, tiled=True)
+    in_sum = lax.psum_scatter(in_grad, "dp", scatter_dimension=1, tiled=True)
     moe_grad = moe_grad + jnp.dot(any_pick, back_rows, preferred_element_type=jnp.float32)
     grad_part, gain_two = norm_backward(normal_two, factor_two, gain_rows[1], moe_grad)
     grad_one = grad_two + grad_part
@@ -404,33 +543,6 @@
     )
     grad_part, gain_one = norm_backward(normal_one, factor_one, gain_rows[0], attn_in_grad)
     stream_grad = (grad_one + grad_part).astype(jnp.bfloat16)
-    group_grad = jnp.concatenate(shared(stream_grad, members), axis=0)
-    id_blocks = jnp.stack(in_order(list(local_ids.reshape(members, local_rows)), my_index))
-    id_blocks = id_blocks.reshape(group_count // lookup_rows, lookup_rows)
-
-    def add_rows(total, pair):
-        selector = (pair[0][:, None] == vocab_iota[None, :]).astype(jnp.bfloat16)
-        return (
-            total + jnp.einsum("tv,td->vd", selector, pair[1], preferred_element_type=jnp.float32),
-            None,
-        )
-
-    embed_grad, _ = lax.scan(
-        add_rows,
-        embed_head,
-        (id_blocks, group_grad.reshape(group_count // lookup_rows, lookup_rows, width)),
-    )
-    in_sum, out_sum, embed_sum = (
-        lax.psum_scatter(
-            in_grad.astype(jnp.bfloat16), "dp", scatter_dimension=1, tiled=True
-        ).astype(jnp.float32),
-        lax.psum_scatter(
-            out_grad.astype(jnp.bfloat16), "dp", scatter_dimension=1, tiled=True
-        ).astype(jnp.float32),
-        lax.psum_scatter(
-            embed_grad.astype(jnp.bfloat16), "dp", scatter_dimension=1, tiled=True
-        ).astype(jnp.float32),
-    )
     attention_grad = jnp.concatenate([qkv_grad, out_weight_grad[None]], axis=0)
     small_grad = jnp.concatenate([jnp.stack([gain_one, gain_two, gain_three]), router_grad], axis=0)
     dense_grads = (
@@ -439,16 +551,9 @@
         .reshape(replicas, members, chunk, width)
         .astype(jnp.bfloat16)
     )
-    dense_sum = sum(
-        swap(
-            lax.dynamic_index_in_dim(
-                dense_grads, partner_of(my_index, k, members), 1, keepdims=False
-            ),
-            k,
-            members,
-        ).astype(jnp.float32)
-        for k in range(members)
-    )
+    stream_grad, dense_grads = lax.optimization_barrier((stream_grad, dense_grads))
+    column_grad = lax.all_to_all(stream_grad, "dp", split_axis=1, concat_axis=0, tiled=True)
+    column_grads = shared(column_grad.T, members)
     small_grads = small_grad.reshape(-1, replicas, share).transpose(1, 0, 2).reshape(replicas, -1)
     small_grads = jnp.concatenate(
         [
@@ -458,14 +563,78 @@
         ],
         axis=1,
     ).reshape(replicas, small_rows, width)
-    small_grads = sum(shared(small_grads, members))
-    summed = lax.psum_scatter(
-        jnp.concatenate([dense_sum, small_grads], axis=1), "dp", scatter_dimension=0
-    )
-    small_sum = summed[chunk:].reshape(-1)
+
+    def spread(values):
+        return jnp.concatenate([part.astype(jnp.bfloat16) for part in in_thirds(values)], axis=1)
+
+    def joined(values):
+        parts = values.reshape(values.shape[0], -1, small_rows, width).astype(jnp.float32)
+        return jnp.sum(parts, axis=1)
+
+    def packed(dense, small):
+        return jnp.concatenate([dense.astype(jnp.bfloat16), spread(small)], axis=1)
+
+    def of_core(values, which):
+        values = values.reshape((levels, 2) + values.shape[1:])
+        return lax.dynamic_index_in_dim(values, which, 1, keepdims=False)
+
+    dense_sum = of_core(dense_grads, core).astype(jnp.float32) + dp_swap(
+        of_core(dense_grads, 1 - core), 1, replicas
+    ).astype(jnp.float32)
+    small_sum = of_core(small_grads, core) + joined(
+        dp_swap(spread(of_core(small_grads, 1 - core)), 1, replicas)
+    )
+    received = [
+        swap(
+            packed(
+                lax.dynamic_index_in_dim(
+                    dense_sum, partner_of(my_index, k, members), 1, keepdims=False
+                ),
+                small_sum,
+            ),
+            k,
+            members,
+        )
+        for k in range(members)
+    ]
+    token_rows = [
+        lax.dynamic_index_in_dim(
+            all_ids, partner_of(my_index, k, members), 1, keepdims=False
+        ).reshape(-1)
+        - my_index * vocab_rows
+        for k in range(members)
+    ]
+    column_grads[1], out_sum = lax.optimization_barrier((column_grads[1], out_sum))
+    third_out = nesterov_update(
+        expert_out,
+        expert_out_moment,
+        expert_out_average,
+        out_sum.astype(jnp.float32),
+        RATE_TABLE[2] * loss_count**0.5,
+    )
+    half = members // 2
+    stream_sum = add_rows(token_rows[:half], column_grads[:half], vocab_rows, None)
+    received, stream_sum = lax.optimization_barrier((received, stream_sum))
+    dense_sum = sum(part[:, :chunk].astype(jnp.float32) for part in received)
+    small_sum = sum(joined(part[:, chunk:]) for part in received)
+    message = packed(dense_sum, small_sum)
+    summed = lax.dynamic_index_in_dim(dense_sum, level, 0, keepdims=False)
+    small_sum = lax.dynamic_index_in_dim(small_sum, level, 0)
+    for k in range(1, levels):
+        part = dp_swap(lax.dynamic_index_in_dim(message, level ^ k, 0), 2 * k, replicas)
+        summed = summed + part[0, :chunk].astype(jnp.float32)
+        small_sum = small_sum + joined(part[:, chunk:])
+    small_sum = small_sum.reshape(-1)
+    column_grads[-1], third_out, summed = lax.optimization_barrier(
+        (column_grads[-1], third_out, summed)
+    )
+    stream_sum = add_rows(token_rows[half:], column_grads[half:], vocab_rows, stream_sum)
+    stream_sum, in_sum = lax.optimization_barrier((stream_sum, in_sum))
+    embed_sum = embed_sum.astype(jnp.float32) + stream_sum.T
+    in_sum = in_sum.astype(jnp.float32)
     loss_value = small_sum[small_params.size]
     small_sum = small_sum[: small_params.size].reshape(small_params.shape[0], share)
-    attention_sum = in_order(shared(summed[:chunk], members), my_index)
+    attention_sum = in_order(shared(summed, members), my_index)
     attention_sum = attention_sum.reshape(attention.shape[0], share, width)
     rate_base = loss_count**0.5
     first_out = nesterov_update(
@@ -473,9 +642,6 @@
     )
     second_out = nesterov_update(
         expert_in, expert_in_moment, expert_in_average, in_sum, RATE_TABLE[1] * rate_base
-    )
-    third_out = nesterov_update(
-        expert_out, expert_out_moment, expert_out_average, out_sum, RATE_TABLE[2] * rate_base
     )
     fourth_out = nesterov_update(
         embedding, embedding_moment, embedding_average, embed_sum, RATE_TABLE[3] * rate_base

time: 998 us -> 780 us (0.78)
  the two profiles are of different devices: /device:TPU:0 before, /device:TPU:8 now
where the time goes in v3:
time: 780 us; the launch traced here: 767 us
  matrix products  212 us (27%)
  waiting for transfers between devices  198 us (25%)
  local copies, waits for them, and re-layouts  107 us (14%)
  other arithmetic  102 us (13%)
  starting transfers between devices  60.3 us (8%)
  Pallas kernels  51.4 us (7%)
  blocking collectives  17.9 us (2%)
  between operations  17.4 us (2%)
    ppermute x30, waiting for transfers between devices, swap(): lax.ppermute(value, 'expert', partner_order(members)[k])  106 us
    pallas_call x2, Pallas kernels, add_rows(): pl.pallas_call(add_rows_kernel, out_shape=jax.ShapeDtypeStruct(shape, jnp...  51.4 us
    ppermute x14, waiting for transfers between devices, dp_swap(): lax.ppermute(value, 'dp', [(i, i ^ k) for i in range(replicas)])  39.5 us
    all_to_all x1, waiting for transfers between devices, shards(): lax.all_to_all(stream_parts, 'dp', split_axis=0, concat_axis=1, tiled=True)  33.5 us
    ppermute x30, starting transfers between devices, swap(): lax.ppermute(value, 'expert', partner_order(members)[k])  32.9 us
    dot_general x1, matrix products, shards(): jnp.einsum('ecd,efd->ecf', arrived_grad, out_low, preferred_element_type=...  21.2 us
    concatenate x2, local copies, waits for them, and re-layouts, shards(): rows_table = jnp.concatenate(rows_parts, axis=0)  20.4 us
    all_to_all x1, waiting for transfers between devices, shards(): lax.all_to_all(stream_grad, 'dp', split_axis=1, concat_axis=0, tiled=True)  18.9 us
  transfers between devices with their start and end apart: 52, of which 23 were waited for; matrix products, arithmetic and copies ran while one was open for 49% of the time, Pallas kernels for 7%

profile of v3, /device:TPU:8, one launch (start us, length us, event | category | flops | bytes accessed | tf_op | source)
XLA Modules:
  0.0 766.6 jit_solution(9275713088326694222)
XLA Ops:
  20.0 6.7 select_convert_fusion.2
  26.6 24.9 %collective-permute-done = bf16[8000,96]{0,1:T(8,128)(2,1)S(1)} collective-permute-done((bf16[8000,96]{0,1:T(8,128)(2,1)}, bf16[8000,96]{0,1:T(8,128)(2,1)S(1)}, u32[]{:S(2)}, u32[]{:S(2)}) %collective-permute-start) | collective-permute-done | bytes 1536032 | tf_op jit(solution)/shard_map/ppermute | solution.py:32
  60.5 15.4 %fusion = f32[256,63,128]{2,1,0:T(8,128)} fusion(pred[256,65,128]{2,1,0:T(8,128)(4,1)S(1)} %iota_compare_fusion, bf16[256,65,63]{1,2,0:T(8,128)(2,1)} %get-tuple-element.245, bf16[256,65,63]{1,2,0:T(8,128)(2,1)} %get-tuple-element.246, bf16[256,65,63]{1,2,0:T(8,128)(2,1)} %get-tuple-element.244), kind=kOutput, calls=%fused_computation.3 | convolution fusion | flops 836759040 | bytes 16677376 | tf_op jit(solution)/shard_map/pih,pil->phl/dot_general | solution.py:107
  75.9 9.2 %copy.330 = f32[256,63,128]{0,2,1:T(8,128)} copy(f32[256,63,128]{2,1,0:T(8,128)} %fusion) | data formatting | bytes 16515072 | tf_op jit(solution)/shard_map/pih,pil->phl/dot_general | solution.py:107
  85.1 7.2 slice.265
  96.8 6.4 collective-permute-done.3
  103.3 4.0 collective-permute-done.4
  107.3 6.6 collective-permute-done.5
  117.9 10.5 %concatenate.101 = bf16[32000,96]{0,1:T(8,128)(2,1)} concatenate(bf16[8000,96]{0,1:T(8,128)(2,1)} %convert_element_type.401, bf16[8000,96]{0,1:T(8,128)(2,1)S(1)} %copy-done.45, bf16[8000,96]{0,1:T(8,128)(2,1)} %collective-permute-done.1, bf16[8000,96]{0,1:T(8,128)(2,1)} %collective-permute-done.2), dimensions={0} | concatenate | bytes 12288000 | tf_op jit(solution)/shard_map/concatenate | solution.py:318
  128.3 9.9 %copy.332 = bf16[32000,96]{1,0:T(8,128)(2,1)} copy(bf16[32000,96]{0,1:T(8,128)(2,1)} %concatenate.101) | data formatting | bytes 12288000 | tf_op jit(solution)/shard_map/concatenate | solution.py:318
  138.3 15.8 %gather_fusion = bf16[4096,96]{1,0:T(8,128)(2,1)S(1)} fusion(bf16[32000,96]{1,0:T(8,128)(2,1)} %copy.332, s32[4096]{0:T(1024)S(1)} %broadcast_clamp_fusion), kind=kCustom, calls=%fused_computation | custom fusion | bytes 1589248 | tf_op jit(solution)/shard_map/jit(_take)/gather | solution.py:321
  160.6 3.5 all-to-all-start
  166.8 33.5 %all-to-all-done = bf16[8,512,96]{1,2,0:T(8,128)(2,1)S(1)} async-done(((bf16[8,512,96]{1,2,0:T(8,128)(2,1)}), bf16[8,512,96]{1,2,0:T(8,128)(2,1)S(1)}, u32[]{:S(2)}, u32[]{:S(2)}) %all-to-all-start) | async-done | bytes 786464 | tf_op jit(solution)/shard_map/all_to_all | solution.py:332
  219.4 3.7 fusion.57
  234.9 9.3 %collective-permute-done.15 = bf16[384,768]{1,0:T(8,128)(2,1)} collective-permute-done((bf16[384,768]{1,0:T(8,128)(2,1)}, bf16[384,768]{1,0:T(8,128)(2,1)}, u32[]{:S(2)}, u32[]{:S(2)}) %collective-permute-start.15) | collective-permute-done | bytes 589856 | tf_op jit(solution)/shard_map/ppermute | solution.py:32
  244.2 13.0 %collective-permute-done.16 = bf16[384,768]{1,0:T(8,128)(2,1)} collective-permute-done((bf16[384,768]{1,0:T(8,128)(2,1)}, bf16[384,768]{1,0:T(8,128)(2,1)}, u32[]{:S(2)}, u32[]{:S(2)}) %collective-permute-start.16) | collective-permute-done | bytes 589856 | tf_op jit(solution)/shard_map/ppermute | solution.py:32
  260.5 15.4 %fusion.142 = f32[2,768,3072]{2,1,0:T(8,128)} fusion(bf16[2,768,768]{2,1,0:T(8,128)(2,1)} %bitcast.316, bf16[2,768,3072]{2,1,0:T(8,128)(2,1)} %all-gather.6.cloned.1.call-done), kind=kOutput, calls=%fused_computation.419 | convolution fusion | flops 7247757312 | bytes 30670848 | tf_op jit(solution)/shard_map/ecd,edf->ecf/dot_general | solution.py:398
  275.9 15.6 %convolution_convert_fusion.6 = bf16[2,768,768]{2,1,0:T(8,128)(2,1)S(1)} fusion(bf16[2,3072,768]{2,1,0:T(8,128)(2,1)} %all-gather.8.cloned.1.call-done, f32[2,768,3072]{2,1,0:T(8,128)} %fusion.142), kind=kOutput, calls=%fused_computation.108 | convolution fusion | flops 7291404288 | bytes 30670848 | tf_op jit(solution)/shard_map/ecf,efd->ecd/dot_general | solution.py:400
  296.3 12.9 %collective-permute-done.18 = bf16[384,768]{1,0:T(8,128)(2,1)S(1)} collective-permute-done((bf16[384,768]{1,0:T(8,128)(2,1)}, bf16[384,768]{1,0:T(8,128)(2,1)S(1)}, u32[]{:S(2)}, u32[]{:S(2)}) %collective-permute-start.18) | collective-permute-done | bytes 589856 | tf_op jit(solution)/shard_map/ppermute | solution.py:32
  309.2 12.0 %collective-permute-done.19 = bf16[384,768]{1,0:T(8,128)(2,1)} collective-permute-done((bf16[384,768]{1,0:T(8,128)(2,1)}, bf16[384,768]{1,0:T(8,128)(2,1)}, u32[]{:S(2)}, u32[]{:S(2)}) %collective-permute-start.19) | collective-permute-done | bytes 589856 | tf_op jit(solution)/shard_map/ppermute | solution.py:32
  327.5 9.7 %all_gather.20 = bf16[256,768]{1,0:T(8,128)(2,1)} all-gather(bf16[64,768]{1,0:T(8,128)(2,1)S(1)} %convolution_convert_fusion.9), channel_id=1, replica_groups=mesh['dp'=8,'expert'=4] {'expert'}, dimensions={0}, use_global_device_ids=true | all-gather | bytes 491520 | tf_op jit(solution)/shard_map/all_gather | solution.py:412
  337.3 8.3 %fusion.140 = (f32[256]{0:T(256)S(1)}, f32[256,8000]{0,1:T(8,128)S(1)}) fusion(bf16[256,768]{1,0:T(8,128)(2,1)} %all_gather.20, bf16[8000,768]{0,1:T(8,128)(2,1)} %all-gather.10.cloned.1.call-done), kind=kOutput, calls=%fused_computation.417 | convolution fusion | flops 3147775744 | bytes 20874240 | tf_op jit(solution)/shard_map/gd,vd->gv/dot_general | solution.py:413
  345.6 4.6 exponential_reduce_fusion
  350.2 8.1 %all-gather.1 = f32[4,3,256]{2,1,0:T(4,128)S(1)} all-gather(f32[1,3,256]{2,1,0:T(4,128)S(1)} %maximum_bitcast_fusion.4), channel_id=2, replica_groups=mesh['dp'=8,'expert'=4] {'expert'}, dimensions={0}, use_global_device_ids=true | all-gather | bytes 15360 | tf_op jit(solution)/shard_map/all_gather | solution.py:417
  359.0 3.6 multiply_convert_fusion.2
  362.6 10.1 %convolution_convert_fusion = bf16[8000,768]{0,1:T(8,128)(2,1)} fusion(bf16[256,8000]{0,1:T(8,128)(2,1)} %multiply_convert_fusion.2, bf16[256,768]{1,0:T(8,128)(2,1)} %all_gather.20), kind=kOutput, calls=%fused_computation.17 | convolution fusion | flops 3151872000 | bytes 16777216 | tf_op jit(solution)/shard_map/gv,gd->vd/dot_general | solution.py:429
  372.9 12.4 %fusion.143 = f32[256,768]{1,0:T(8,128)S(1)} fusion(bf16[256,8000]{0,1:T(8,128)(2,1)} %multiply_convert_fusion.2, bf16[8000,768]{0,1:T(8,128)(2,1)} %all-gather.10.cloned.1.call-done), kind=kOutput, calls=%fused_computation.420 | convolution fusion | flops 3145728000 | bytes 17170432 | tf_op jit(solution)/shard_map/dot_general | solution.py:434
  407.2 11.4 %collective-permute-done.24 = bf16[384,768]{1,0:T(8,128)(2,1)S(1)} collective-permute-done((bf16[384,768]{1,0:T(8,128)(2,1)S(1)}, bf16[384,768]{1,0:T(8,128)(2,1)S(1)}, u32[]{:S(2)}, u32[]{:S(2)}) %collective-permute-start.24) | collective-permute-done | bytes 589856 | tf_op jit(solution)/shard_map/ppermute | solution.py:32
  418.5 6.9 collective-permute-done.25
  426.7 21.2 %fusion.12 = bf16[2,768,3072]{2,1,0:T(8,128)(2,1)} fusion(f32[2,768,3072]{2,1,0:T(8,128)} %fusion.142, bf16[2,768,768]{2,1,0:T(8,128)(2,1)S(1)} %bitcast.319, bf16[2,3072,768]{2,1,0:T(8,128)(2,1)S(1)} %bitcast.397), kind=kOutput, calls=%fused_computation.15 | convolution fusion | flops 7342129152 | bytes 40108032 | tf_op jit(solution)/shard_map/ecd,efd->ecf/dot_general | solution.py:472
  447.9 13.0 %convolution_convert_fusion.5 = bf16[2,768,768]{2,1,0:T(8,128)(2,1)S(1)} fusion(bf16[2,768,3072]{2,1,0:T(8,128)(2,1)} %fusion.12, bf16[2,768,3072]{2,1,0:T(8,128)(2,1)} %all-gather.6.cloned.1.call-done), kind=kOutput, calls=%fused_computation.107 | convolution fusion | flops 7248936960 | bytes 21233664 | tf_op jit(solution)/shard_map/ecf,edf->ecd/dot_general | solution.py:478
  465.6 13.5 %convolution_convert_fusion.1 = bf16[2,768,3072]{2,1,0:T(8,128)(2,1)} fusion(bf16[2,768,768]{2,1,0:T(8,128)(2,1)S(1)} %bitcast.317, bf16[2,768,3072]{2,1,0:T(8,128)(2,1)} %fusion.12), kind=kOutput, calls=%fused_computation.39 | convolution fusion | flops 7252475904 | bytes 21233664 | tf_op jit(solution)/shard_map/ecd,ecf->edf/dot_general | solution.py:477
  479.1 17.0 %convolution_convert_fusion.2 = bf16[2,3072,768]{2,1,0:T(8,128)(2,1)} fusion(bf16[2,768,768]{2,1,0:T(8,128)(2,1)S(1)} %bitcast.320, f32[2,768,3072]{2,1,0:T(8,128)} %fusion.142), kind=kOutput, calls=%fused_computation.40 | convolution fusion | flops 7294943232 | bytes 30670848 | tf_op jit(solution)/shard_map/ecf,ecd->efd/dot_general | solution.py:469
  515.0 3.5 fusion.41
  525.3 13.8 %multiply_reduce_fusion = (f32[12,512]{1,0:T(8,128)S(1)}, f32[12,512,512]{1,2,0:T(8,128)}) fusion(f32[12,512]{1,0:T(8,128)S(1)} %log_add_fusion, f32[12,512,512]{1,2,0:T(8,128)} %copy-done, pred[512,512]{0,1:T(8,128)(4,1)S(1)} %copy-done.17, bf16[512,12,64]{0,2,1:T(8,128)(2,1)} %bitcast.300, bf16[512,12,64]{0,2,1:T(8,128)(2,1)} %bitcast.298), kind=kOutput, calls=%fused_computation.19 | convolution fusion | flops 418375680 | bytes 27049984 | tf_op jit(solution)/shard_map/while/body/eval_jaxpr/qhd,khd->hqk/dot_general | solution.py:508
  539.1 7.4 multiply_convert_fusion.1
  551.8 6.0 multiply_convert_fusion.4
  560.1 8.9 %fusion.54 = bf16[12,64,512]{2,1,0:T(8,128)(2,1)} fusion(bf16[512,12,64]{0,2,1:T(8,128)(2,1)} %bitcast.301, f32[12,512]{1,0:T(8,128)S(1)} %log_add_fusion, f32[12,512,512]{1,2,0:T(8,128)} %copy-done, pred[512,512]{0,1:T(8,128)(4,1)S(1)} %copy-done.17), kind=kOutput, calls=%fused_computation.149 | convolution fusion | flops 415629312 | bytes 14442496 | tf_op jit(solution)/shard_map/while/body/eval_jaxpr/hqk,qhd->khd/dot_general | solution.py:502
  571.4 5.5 multiply_reduce_fusion.4
  589.1 7.8 %all-to-all-start.1 = ((bf16[512,8,96]{0,2,1:T(8,128)(2,1)}), bf16[512,8,96]{0,2,1:T(8,128)(2,1)S(1)}, u32[]{:S(2)}, u32[]{:S(2)}) async-start(bf16[512,8,96]{0,2,1:T(8,128)(2,1)} %bitcast.122), calls=%async_computation.2 | async-start | bytes 1572864 | tf_op jit(solution)/shard_map/all_to_all | solution.py:555
  601.6 18.9 %all-to-all-done.1 = bf16[512,8,96]{0,2,1:T(8,128)(2,1)S(1)} async-done(((bf16[512,8,96]{0,2,1:T(8,128)(2,1)}), bf16[512,8,96]{0,2,1:T(8,128)(2,1)S(1)}, u32[]{:S(2)}, u32[]{:S(2)}) %all-to-all-start.1) | async-done | bytes 786464 | tf_op jit(solution)/shard_map/all_to_all | solution.py:555
  633.6 7.5 collective-permute-done.35.refs_1_
  642.0 22.7 %shard_map.376.refs_2_ = f32[8064,128]{1,0:T(8,128)} custom-call(s32[64]{0:T(128)} %pad_add_fusion.8.count_ref, s32[64,128]{1,0:T(8,128)} %pad_add_fusion.4.row_ref, s32[64,128]{1,0:T(8,128)} %pad_add_fusion.5.source_ref, bf16[96,4096]{1,0:T(8,128)(2,1)} %bitcast.309, bf16[96,4096]{1,0:T(8,128)(2,1)} %copy-done.55), custom_call_target="tpu_custom_call" | custom-call | flops 8388608 | bytes 231735296 | tf_op jit(solution)/shard_map/pallas_call | solution.py:201
  672.4 4.9 collective-permute-start.36
  686.2 5.8 collective-permute-done.37
  692.1 11.3 %collective-permute-done.38 = bf16[1,102,768]{2,1,0:T(8,128)(2,1)S(1)} collective-permute-done((bf16[1,102,768]{2,1,0:T(8,128)(2,1)S(1)}, bf16[1,102,768]{2,1,0:T(8,128)(2,1)S(1)}, u32[]{:S(2)}, u32[]{:S(2)}) %collective-permute-start.38) | collective-permute-done | bytes 156704 | tf_op jit(solution)/shard_map/ppermute | solution.py:36
  707.0 28.6 %shard_map.377 = f32[96,8064]{1,0:T(8,128)} custom-call(s32[64]{0:T(128)} %pad_add_fusion.9.count_ref, s32[64,128]{1,0:T(8,128)} %pad_add_fusion.6.row_ref, s32[64,128]{1,0:T(8,128)} %pad_add_fusion.7.source_ref, bf16[96,4096]{1,0:T(8,128)(2,1)} %collective-permute-done.43.refs_0_, bf16[96,4096]{1,0:T(8,128)(2,1)} %collective-permute-done.39.refs_1_, ...), custom_call_target="tpu_custom_call" | custom-call | flops 8388608 | bytes 231735296 | tf_op jit(solution)/shard_map/pallas_call | solution.py:201
  735.9 7.3 fusion.125
  (581 shorter events, 213.6 us)
Async XLA Ops:
  7.2 253.4 %all-gather.6.cloned.1.call-start = ((), (), s32[]{:S(2)}) async-start(), calls=%async_computation.5 | async-start | bytes 10616832 | tf_op jit(solution)/shard_map/all_gather | solution.py:276
  10.1 265.8 %all-gather.8.cloned.1.call-start = ((), (), s32[]{:S(2)}) async-start(), calls=%async_computation.6 | async-start | bytes 10616832 | tf_op jit(solution)/shard_map/all_gather | solution.py:277
  13.2 324.1 %all-gather.10.cloned.1.call-start = ((), (), s32[]{:S(2)}) async-start(), calls=%async_computation.7 | async-start | bytes 13934592 | tf_op jit(solution)/shard_map/all_gather | solution.py:278
  14.6 37.0 %collective-permute-start = (bf16[8000,96]{0,1:T(8,128)(2,1)}, bf16[8000,96]{0,1:T(8,128)(2,1)S(1)}, u32[]{:S(2)}, u32[]{:S(2)}) collective-permute-start(bf16[8000,96]{0,1:T(8,128)(2,1)} %convert_element_type.401), channel_id=1, source_target_pairs={{0,1},{1,0},{2,3},{3,2},{4,5},{5,4},{6,7},{7,6},{8,9},{9,8},{10,11... | collective-permute-start | bytes 4608008 | tf_op jit(solution)/shard_map/ppermute | solution.py:32
  16.0 98.1 %collective-permute-start.2 = (bf16[8000,96]{0,1:T(8,128)(2,1)}, bf16[8000,96]{0,1:T(8,128)(2,1)}, u32[]{:S(2)}, u32[]{:S(2)}) collective-permute-start(bf16[8000,96]{0,1:T(8,128)(2,1)} %convert_element_type.401), channel_id=1, source_target_pairs={{0,3},{1,2},{2,1},{3,0},{4,7},{5,6},{6,5},{7,4},{8,11},{9,10},{10,... | collective-permute-start | bytes 4608008 | tf_op jit(solution)/shard_map/ppermute | solution.py:32
  17.5 100.3 %collective-permute-start.1 = (bf16[8000,96]{0,1:T(8,128)(2,1)}, bf16[8000,96]{0,1:T(8,128)(2,1)}, u32[]{:S(2)}, u32[]{:S(2)}) collective-permute-start(bf16[8000,96]{0,1:T(8,128)(2,1)} %convert_element_type.401), channel_id=1, source_target_pairs={{0,2},{1,3},{2,0},{3,1},{4,6},{5,7},{6,4},{7,5},{8,10},{9,11},{10,... | collective-permute-start | bytes 4608008 | tf_op jit(solution)/shard_map/ppermute | solution.py:32
  51.5 7.5 collective-permute-start.8
  53.1 5.9 collective-permute-start.6
  60.4 33.5 %collective-permute-start.9 = (s32[4,2048]{1,0:T(4,128)S(1)}, s32[4,2048]{1,0:T(4,128)S(1)}, u32[]{:S(2)}, u32[]{:S(2)}) collective-permute-start(s32[4,2048]{1,0:T(4,128)S(1)} %pad_add_fusion.3), channel_id=1, source_target_pairs={{0,4},{4,0},{8,12},{12,8},{16,20},{20,16},{24,28},{28,24},{1,5},{5... | collective-permute-start | bytes 98312 | tf_op jit(solution)/shard_map/ppermute | solution.py:36
  92.3 11.0 %collective-permute-start.3 = (bf16[98,768]{1,0:T(8,128)(2,1)S(1)}, bf16[98,768]{1,0:T(8,128)(2,1)S(1)}, u32[]{:S(2)}, u32[]{:S(2)}) collective-permute-start(bf16[98,768]{1,0:T(8,128)(2,1)S(1)} %pad_maximum_fusion.25), channel_id=1, source_target_pairs={{0,8},{4,12},{8,0},{12,4},{16,24},{20,28},{24,16},{28,20},{1,9},{5... | collective-permute-start | bytes 451592 | tf_op jit(solution)/shard_map/ppermute | solution.py:36
  92.5 14.7 %collective-permute-start.4 = (bf16[98,768]{1,0:T(8,128)(2,1)S(1)}, bf16[98,768]{1,0:T(8,128)(2,1)S(1)}, u32[]{:S(2)}, u32[]{:S(2)}) collective-permute-start(bf16[98,768]{1,0:T(8,128)(2,1)S(1)} %pad_maximum_fusion.25), channel_id=1, source_target_pairs={{0,16},{4,20},{8,24},{12,28},{16,0},{20,4},{24,8},{28,12},{1,17},{... | collective-permute-start | bytes 451592 | tf_op jit(solution)/shard_map/ppermute | solution.py:36
  93.9 20.0 %collective-permute-start.5 = (bf16[98,768]{1,0:T(8,128)(2,1)S(1)}, bf16[98,768]{1,0:T(8,128)(2,1)S(1)}, u32[]{:S(2)}, u32[]{:S(2)}) collective-permute-start(bf16[98,768]{1,0:T(8,128)(2,1)S(1)} %pad_maximum_fusion.25), channel_id=1, source_target_pairs={{0,24},{4,28},{8,16},{12,20},{16,8},{20,12},{24,0},{28,4},{1,25},{... | collective-permute-start | bytes 451592 | tf_op jit(solution)/shard_map/ppermute | solution.py:36
  114.2 39.9 %collective-permute-start.10 = (bf16[4,96,768]{2,1,0:T(8,128)(2,1)S(1)}, bf16[4,96,768]{2,1,0:T(8,128)(2,1)}, u32[]{:S(2)}, u32[]{:S(2)}) collective-permute-start(bf16[4,96,768]{2,1,0:T(8,128)(2,1)S(1)} %slice.205), channel_id=1, source_target_pairs={{0,1},{1,0},{2,3},{3,2},{4,5},{5,4},{6,7},{7,6},{8,9},{9,8},{10,11... | collective-permute-start | bytes 1769480 | tf_op jit(solution)/shard_map/ppermute | solution.py:32
  115.7 38.4 %collective-permute-start.11 = (bf16[4,96,768]{2,1,0:T(8,128)(2,1)S(1)}, bf16[4,96,768]{2,1,0:T(8,128)(2,1)}, u32[]{:S(2)}, u32[]{:S(2)}) collective-permute-start(bf16[4,96,768]{2,1,0:T(8,128)(2,1)S(1)} %slice.205), channel_id=1, source_target_pairs={{0,2},{1,3},{2,0},{3,1},{4,6},{5,7},{6,4},{7,5},{8,10},{9,11},{10,... | collective-permute-start | bytes 1769480 | tf_op jit(solution)/shard_map/ppermute | solution.py:32
  117.2 36.9 %collective-permute-start.12 = (bf16[4,96,768]{2,1,0:T(8,128)(2,1)S(1)}, bf16[4,96,768]{2,1,0:T(8,128)(2,1)}, u32[]{:S(2)}, u32[]{:S(2)}) collective-permute-start(bf16[4,96,768]{2,1,0:T(8,128)(2,1)S(1)} %slice.205), channel_id=1, source_target_pairs={{0,3},{1,2},{2,1},{3,0},{4,7},{5,6},{6,5},{7,4},{8,11},{9,10},{10,... | collective-permute-start | bytes 1769480 | tf_op jit(solution)/shard_map/ppermute | solution.py:32
  158.1 46.0 %collective-permute-start.13 = (bf16[4,4,96,768]{3,2,1,0:T(8,128)(2,1)}, bf16[4,4,96,768]{3,2,1,0:T(8,128)(2,1)}, u32[]{:S(2)}, u32[]{:S(2)}) collective-permute-start(bf16[4,4,96,768]{3,2,1,0:T(8,128)(2,1)} %pad_maximum_fusion.1), channel_id=1, source_target_pairs={{0,4},{4,0},{8,12},{12,8},{16,20},{20,16},{24,28},{28,24},{1,5},{5... | collective-permute-start | bytes 7077896 | tf_op jit(solution)/shard_map/ppermute | solution.py:36
  160.6 39.7 %all-to-all-start = ((bf16[8,512,96]{1,2,0:T(8,128)(2,1)}), bf16[8,512,96]{1,2,0:T(8,128)(2,1)S(1)}, u32[]{:S(2)}, u32[]{:S(2)}) async-start(bf16[8,512,96]{1,2,0:T(8,128)(2,1)} %copy.333), calls=%async_computation | async-start | bytes 1572864 | tf_op jit(solution)/shard_map/all_to_all | solution.py:332
  164.1 335.2 %reduce-scatter.4.cloned.1.call-start = ((), (), s32[]{:S(2)}) async-start(), calls=%async_computation.8 | async-start | bytes 13934592 | tf_op jit(solution)/shard_map/reduce_scatter | solution.py:433
  227.7 16.5 %collective-permute-start.15 = (bf16[384,768]{1,0:T(8,128)(2,1)}, bf16[384,768]{1,0:T(8,128)(2,1)}, u32[]{:S(2)}, u32[]{:S(2)}) collective-permute-start(bf16[384,768]{1,0:T(8,128)(2,1)} %get-tuple-element.220), channel_id=1, source_target_pairs={{0,1},{1,0},{2,3},{3,2},{4,5},{5,4},{6,7},{7,6},{8,9},{9,8},{10,11... | collective-permute-start | bytes 1769480 | tf_op jit(solution)/shard_map/ppermute | solution.py:32
  229.3 28.0 %collective-permute-start.16 = (bf16[384,768]{1,0:T(8,128)(2,1)}, bf16[384,768]{1,0:T(8,128)(2,1)}, u32[]{:S(2)}, u32[]{:S(2)}) collective-permute-start(bf16[384,768]{1,0:T(8,128)(2,1)} %get-tuple-element.219), channel_id=1, source_target_pairs={{0,2},{1,3},{2,0},{3,1},{4,6},{5,7},{6,4},{7,5},{8,10},{9,11},{10,... | collective-permute-start | bytes 1769480 | tf_op jit(solution)/shard_map/ppermute | solution.py:32
  230.7 26.5 %collective-permute-start.17 = (bf16[384,768]{1,0:T(8,128)(2,1)S(1)}, bf16[384,768]{1,0:T(8,128)(2,1)}, u32[]{:S(2)}, u32[]{:S(2)}) collective-permute-start(bf16[384,768]{1,0:T(8,128)(2,1)S(1)} %get-tuple-element.218), channel_id=1, source_target_pairs={{0,3},{1,2},{2,1},{3,0},{4,7},{5,6},{6,5},{7,4},{8,11},{9,10},{10,... | collective-permute-start | bytes 1769480 | tf_op jit(solution)/shard_map/ppermute | solution.py:32
  292.7 16.5 %collective-permute-start.18 = (bf16[384,768]{1,0:T(8,128)(2,1)}, bf16[384,768]{1,0:T(8,128)(2,1)S(1)}, u32[]{:S(2)}, u32[]{:S(2)}) collective-permute-start(bf16[384,768]{1,0:T(8,128)(2,1)} %bitcast.55), channel_id=1, source_target_pairs={{0,1},{1,0},{2,3},{3,2},{4,5},{5,4},{6,7},{7,6},{8,9},{9,8},{10,11... | collective-permute-start | bytes 1769480 | tf_op jit(solution)/shard_map/ppermute | solution.py:32
  293.9 27.2 %collective-permute-start.19 = (bf16[384,768]{1,0:T(8,128)(2,1)}, bf16[384,768]{1,0:T(8,128)(2,1)}, u32[]{:S(2)}, u32[]{:S(2)}) collective-permute-start(bf16[384,768]{1,0:T(8,128)(2,1)} %bitcast.57), channel_id=1, source_target_pairs={{0,2},{1,3},{2,0},{3,1},{4,6},{5,7},{6,4},{7,5},{8,10},{9,11},{10,... | collective-permute-start | bytes 1769480 | tf_op jit(solution)/shard_map/ppermute | solution.py:32
  294.8 26.3 %collective-permute-start.20 = (bf16[384,768]{1,0:T(8,128)(2,1)S(1)}, bf16[384,768]{1,0:T(8,128)(2,1)}, u32[]{:S(2)}, u32[]{:S(2)}) collective-permute-start(bf16[384,768]{1,0:T(8,128)(2,1)S(1)} %bitcast.332), channel_id=1, source_target_pairs={{0,3},{1,2},{2,1},{3,0},{4,7},{5,6},{6,5},{7,4},{8,11},{9,10},{10,... | collective-permute-start | bytes 1769480 | tf_op jit(solution)/shard_map/ppermute | solution.py:32
  372.8 268.4 %reduce-scatter.6.cloned.1.call-start = ((), (), s32[]{:S(2)}) async-start(), calls=%async_computation.9 | async-start | bytes 10616832 | tf_op jit(solution)/shard_map/reduce_scatter | solution.py:483
  387.6 7.0 collective-permute-start.22
  389.0 6.9 collective-permute-start.23
  403.6 14.9 %collective-permute-start.24 = (bf16[384,768]{1,0:T(8,128)(2,1)S(1)}, bf16[384,768]{1,0:T(8,128)(2,1)S(1)}, u32[]{:S(2)}, u32[]{:S(2)}) collective-permute-start(bf16[384,768]{1,0:T(8,128)(2,1)S(1)} %get-tuple-element.212), channel_id=1, source_target_pairs={{0,1},{1,0},{2,3},{3,2},{4,5},{5,4},{6,7},{7,6},{8,9},{9,8},{10,11... | collective-permute-start | bytes 1769480 | tf_op jit(solution)/shard_map/ppermute | solution.py:32
  404.9 20.6 %collective-permute-start.25 = (bf16[384,768]{1,0:T(8,128)(2,1)S(1)}, bf16[384,768]{1,0:T(8,128)(2,1)S(1)}, u32[]{:S(2)}, u32[]{:S(2)}) collective-permute-start(bf16[384,768]{1,0:T(8,128)(2,1)S(1)} %get-tuple-element.211), channel_id=1, source_target_pairs={{0,2},{1,3},{2,0},{3,1},{4,6},{5,7},{6,4},{7,5},{8,10},{9,11},{10,... | collective-permute-start | bytes 1769480 | tf_op jit(solution)/shard_map/ppermute | solution.py:32
  405.7 19.7 %collective-permute-start.26 = (bf16[384,768]{1,0:T(8,128)(2,1)S(1)}, bf16[384,768]{1,0:T(8,128)(2,1)S(1)}, u32[]{:S(2)}, u32[]{:S(2)}) collective-permute-start(bf16[384,768]{1,0:T(8,128)(2,1)S(1)} %get-tuple-element.210), channel_id=1, source_target_pairs={{0,3},{1,2},{2,1},{3,0},{4,7},{5,6},{6,5},{7,4},{8,11},{9,10},{10,... | collective-permute-start | bytes 1769480 | tf_op jit(solution)/shard_map/ppermute | solution.py:32
  462.1 34.0 %collective-permute-start.27 = (bf16[384,768]{1,0:T(8,128)(2,1)}, bf16[384,768]{1,0:T(8,128)(2,1)}, u32[]{:S(2)}, u32[]{:S(2)}) collective-permute-start(bf16[384,768]{1,0:T(8,128)(2,1)} %bitcast.80), channel_id=1, source_target_pairs={{0,1},{1,0},{2,3},{3,2},{4,5},{5,4},{6,7},{7,6},{8,9},{9,8},{10,11... | collective-permute-start | bytes 1769480 | tf_op jit(solution)/shard_map/ppermute | solution.py:32
  463.2 32.9 %collective-permute-start.28 = (bf16[384,768]{1,0:T(8,128)(2,1)}, bf16[384,768]{1,0:T(8,128)(2,1)}, u32[]{:S(2)}, u32[]{:S(2)}) collective-permute-start(bf16[384,768]{1,0:T(8,128)(2,1)} %bitcast.82), channel_id=1, source_target_pairs={{0,2},{1,3},{2,0},{3,1},{4,6},{5,7},{6,4},{7,5},{8,10},{9,11},{10,... | collective-permute-start | bytes 1769480 | tf_op jit(solution)/shard_map/ppermute | solution.py:32
  464.1 32.0 %collective-permute-start.29 = (bf16[384,768]{1,0:T(8,128)(2,1)S(1)}, bf16[384,768]{1,0:T(8,128)(2,1)}, u32[]{:S(2)}, u32[]{:S(2)}) collective-permute-start(bf16[384,768]{1,0:T(8,128)(2,1)S(1)} %bitcast.334), channel_id=1, source_target_pairs={{0,3},{1,2},{2,1},{3,0},{4,7},{5,6},{6,5},{7,4},{8,11},{9,10},{10,... | collective-permute-start | bytes 1769480 | tf_op jit(solution)/shard_map/ppermute | solution.py:32
  499.4 236.2 %reduce-scatter.8.cloned.1.call-start = ((), (), s32[]{:S(2)}) async-start(), calls=%async_computation.10 | async-start | bytes 10616832 | tf_op jit(solution)/shard_map/reduce_scatter | solution.py:484
  585.6 35.1 %collective-permute-start.30 = (bf16[4,4,96,768]{3,2,1,0:T(8,128)(2,1)}, bf16[4,4,96,768]{3,2,1,0:T(8,128)(2,1)}, u32[]{:S(2)}, u32[]{:S(2)}) collective-permute-start(bf16[4,4,96,768]{3,2,1,0:T(8,128)(2,1)} %dynamic-slice_bitcast_fusion), channel_id=1, source_target_pairs={{0,4},{4,0},{8,12},{12,8},{16,20},{20,16},{24,28},{28,24},{1,5},{5... | collective-permute-start | bytes 7077896 | tf_op jit(solution)/shard_map/ppermute | solution.py:36
  589.1 31.4 %all-to-all-start.1 = ((bf16[512,8,96]{0,2,1:T(8,128)(2,1)}), bf16[512,8,96]{0,2,1:T(8,128)(2,1)S(1)}, u32[]{:S(2)}, u32[]{:S(2)}) async-start(bf16[512,8,96]{0,2,1:T(8,128)(2,1)} %bitcast.122), calls=%async_computation.2 | async-start | bytes 1572864 | tf_op jit(solution)/shard_map/all_to_all | solution.py:555
  620.6 20.5 %collective-permute-start.35 = (bf16[96,4096]{1,0:T(8,128)(2,1)S(1)}, bf16[96,4096]{1,0:T(8,128)(2,1)S(1)}, u32[]{:S(2)}, u32[]{:S(2)}) collective-permute-start(bf16[96,4096]{1,0:T(8,128)(2,1)S(1)} %bitcast.306), channel_id=1, source_target_pairs={{0,1},{1,0},{2,3},{3,2},{4,5},{5,4},{6,7},{7,6},{8,9},{9,8},{10,11... | collective-permute-start | bytes 2359304 | tf_op jit(solution)/shard_map/ppermute | solution.py:32
  625.5 39.3 %collective-permute-start.32 = (bf16[4,102,768]{2,0,1:T(4,128)(2,1)}, bf16[4,102,768]{2,0,1:T(4,128)(2,1)S(1)}, u32[]{:S(2)}, u32[]{:S(2)}) collective-permute-start(bf16[4,102,768]{2,0,1:T(4,128)(2,1)} %copy.371), channel_id=1, source_target_pairs={{0,1},{1,0},{2,3},{3,2},{4,5},{5,4},{6,7},{7,6},{8,9},{9,8},{10,11... | collective-permute-start | bytes 1880072 | tf_op jit(solution)/shard_map/ppermute | solution.py:32
  628.4 36.4 %collective-permute-start.33 = (bf16[4,102,768]{2,0,1:T(4,128)(2,1)}, bf16[4,102,768]{2,0,1:T(4,128)(2,1)S(1)}, u32[]{:S(2)}, u32[]{:S(2)}) collective-permute-start(bf16[4,102,768]{2,0,1:T(4,128)(2,1)} %copy.375), channel_id=1, source_target_pairs={{0,2},{1,3},{2,0},{3,1},{4,6},{5,7},{6,4},{7,5},{8,10},{9,11},{10,... | collective-permute-start | bytes 1880072 | tf_op jit(solution)/shard_map/ppermute | solution.py:32
  629.4 37.8 %collective-permute-start.34 = (bf16[4,102,768]{2,0,1:T(4,128)(2,1)}, bf16[4,102,768]{2,0,1:T(4,128)(2,1)}, u32[]{:S(2)}, u32[]{:S(2)}) collective-permute-start(bf16[4,102,768]{2,0,1:T(4,128)(2,1)} %copy.379), channel_id=1, source_target_pairs={{0,3},{1,2},{2,1},{3,0},{4,7},{5,6},{6,5},{7,4},{8,11},{9,10},{10,... | collective-permute-start | bytes 1880072 | tf_op jit(solution)/shard_map/ppermute | solution.py:32
  632.3 71.1 %collective-permute-start.39 = (bf16[96,4096]{1,0:T(8,128)(2,1)S(1)}, bf16[96,4096]{1,0:T(8,128)(2,1)}, u32[]{:S(2)}, u32[]{:S(2)}) collective-permute-start(bf16[96,4096]{1,0:T(8,128)(2,1)S(1)} %bitcast.307), channel_id=1, source_target_pairs={{0,3},{1,2},{2,1},{3,0},{4,7},{5,6},{6,5},{7,4},{8,11},{9,10},{10,... | collective-permute-start | bytes 2359304 | tf_op jit(solution)/shard_map/ppermute | solution.py:32
  641.1 65.9 %collective-permute-start.43 = (bf16[96,4096]{1,0:T(8,128)(2,1)S(1)}, bf16[96,4096]{1,0:T(8,128)(2,1)}, u32[]{:S(2)}, u32[]{:S(2)}) collective-permute-start(bf16[96,4096]{1,0:T(8,128)(2,1)S(1)} %bitcast.308), channel_id=1, source_target_pairs={{0,2},{1,3},{2,0},{3,1},{4,6},{5,7},{6,4},{7,5},{8,10},{9,11},{10,... | collective-permute-start | bytes 2359304 | tf_op jit(solution)/shard_map/ppermute | solution.py:32
  672.4 13.8 %collective-permute-start.36 = (bf16[1,102,768]{2,1,0:T(8,128)(2,1)S(1)}, bf16[1,102,768]{2,1,0:T(8,128)(2,1)S(1)}, u32[]{:S(2)}, u32[]{:S(2)}) collective-permute-start(bf16[1,102,768]{2,1,0:T(8,128)(2,1)S(1)} %get-tuple-element.237), channel_id=1, source_target_pairs={{0,8},{4,12},{8,0},{12,4},{16,24},{20,28},{24,16},{28,20},{1,9},{5... | collective-permute-start | bytes 470024 | tf_op jit(solution)/shard_map/ppermute | solution.py:36
  677.3 14.7 %collective-permute-start.37 = (bf16[1,102,768]{2,1,0:T(8,128)(2,1)S(1)}, bf16[1,102,768]{2,1,0:T(8,128)(2,1)S(1)}, u32[]{:S(2)}, u32[]{:S(2)}) collective-permute-start(bf16[1,102,768]{2,1,0:T(8,128)(2,1)S(1)} %get-tuple-element.239), channel_id=1, source_target_pairs={{0,16},{4,20},{8,24},{12,28},{16,0},{20,4},{24,8},{28,12},{1,17},{... | collective-permute-start | bytes 470024 | tf_op jit(solution)/shard_map/ppermute | solution.py:36
  677.3 26.0 %collective-permute-start.38 = (bf16[1,102,768]{2,1,0:T(8,128)(2,1)S(1)}, bf16[1,102,768]{2,1,0:T(8,128)(2,1)S(1)}, u32[]{:S(2)}, u32[]{:S(2)}) collective-permute-start(bf16[1,102,768]{2,1,0:T(8,128)(2,1)S(1)} %get-tuple-element.238), channel_id=1, source_target_pairs={{0,24},{4,28},{8,16},{12,20},{16,8},{20,12},{24,0},{28,4},{1,25},{... | collective-permute-start | bytes 470024 | tf_op jit(solution)/shard_map/ppermute | solution.py:36
  703.4 51.3 %collective-permute-start.40 = (f32[96,768]{1,0:T(8,128)S(1)}, f32[96,768]{1,0:T(8,128)}, u32[]{:S(2)}, u32[]{:S(2)}) collective-permute-start(f32[96,768]{1,0:T(8,128)S(1)} %add_bitcast_fusion), channel_id=1, source_target_pairs={{0,1},{1,0},{2,3},{3,2},{4,5},{5,4},{6,7},{7,6},{8,9},{9,8},{10,11... | collective-permute-start | bytes 884744 | tf_op jit(solution)/shard_map/ppermute | solution.py:32
  705.2 49.5 %collective-permute-start.41 = (f32[96,768]{1,0:T(8,128)S(1)}, f32[96,768]{1,0:T(8,128)}, u32[]{:S(2)}, u32[]{:S(2)}) collective-permute-start(f32[96,768]{1,0:T(8,128)S(1)} %add_bitcast_fusion), channel_id=1, source_target_pairs={{0,2},{1,3},{2,0},{3,1},{4,6},{5,7},{6,4},{7,5},{8,10},{9,11},{10,... | collective-permute-start | bytes 884744 | tf_op jit(solution)/shard_map/ppermute | solution.py:32
  705.4 49.3 %collective-permute-start.42 = (f32[96,768]{1,0:T(8,128)S(1)}, f32[96,768]{1,0:T(8,128)}, u32[]{:S(2)}, u32[]{:S(2)}) collective-permute-start(f32[96,768]{1,0:T(8,128)S(1)} %add_bitcast_fusion), channel_id=1, source_target_pairs={{0,3},{1,2},{2,1},{3,0},{4,7},{5,6},{6,5},{7,4},{8,11},{9,10},{10,... | collective-permute-start | bytes 884744 | tf_op jit(solution)/shard_map/ppermute | solution.py:32
  (132 other events, 1146.4 us)
Sparse Core Ops, SparseCore 0:
  10.2 92.5 all-gather.5
  105.0 105.5 all-gather.7
  212.8 115.7 all-gather.9
  372.9 126.0 reduce-scatter.3
  501.3 97.8 reduce-scatter.5
  601.4 113.5 reduce-scatter.7

commit v4 on v3

--- a/solution.py
+++ b/solution.py
@@ -1,3 +1,4 @@
+import functools
 import math
 
 import jax
@@ -70,17 +71,6 @@
     earlier = (place[None, :] < place[:, None]).astype(jnp.bfloat16)
     before = jnp.dot(earlier, hits.astype(jnp.bfloat16), preferred_element_type=jnp.float32)
     return jnp.sum(before.astype(jnp.int32) * hits, axis=1).reshape(block_routes.shape)
-
-
-def block_scores(query, keys, seg_ids, block_index, length, block_rows, scaling):
-    start = block_index * block_rows
-    first_row = start // length * length
-    scores = jnp.einsum("qhd,khd->hqk", query, keys, preferred_element_type=jnp.float32) * scaling
-    query_place = start - first_row + jnp.arange(block_rows)
-    allowed = (jnp.arange(length)[None, :] <= query_place[:, None]) & (
-        seg_ids[None, :] == seg_ids[:, None]
-    )
-    return (jnp.where(allowed[None], scores, MASKED_SCORE), query, keys, first_row)
 
 
 def in_thirds(values):
@@ -164,6 +154,137 @@
         return 0
 
     lax.fori_loop(0, sums[0].shape[0] // LANES, finish, 0)
+
+
+def attend_kernel(scaling, q_ref, k_ref, v_ref, row_ref, column_ref, out_ref):
+    length = q_ref.shape[0]
+    rows = math.gcd(length, LANES)
+    half = lax.broadcasted_iota(jnp.int32, (1, LANES), 1) // HEAD
+    across = (((1,), (1,)), ((), ()))
+    for block in range(length // rows):
+        mine, seen = slice(block * rows, (block + 1) * rows), slice(0, (block + 1) * rows)
+        keys, values = k_ref[seen, :], v_ref[seen, :]
+        mixed = jnp.zeros((rows, LANES), jnp.float32)
+        for part in range(LANES // HEAD):
+            chosen = (half == part).astype(jnp.float32)
+            query = q_ref[mine, :] * chosen.astype(jnp.bfloat16)
+            scores = lax.dot_general(query, keys, across, preferred_element_type=jnp.float32)
+            scores = scores * scaling
+            row_place = lax.broadcasted_iota(jnp.int32, scores.shape, 0) + block * rows
+            column_place = lax.broadcasted_iota(jnp.int32, scores.shape, 1)
+            allowed = (column_place <= row_place) & (row_ref[mine, :] == column_ref[:, seen])
+            scores = jnp.where(allowed, scores, MASKED_SCORE)
+            powers = jnp.exp(scores - jnp.max(scores, axis=1, keepdims=True))
+            soft = (powers / jnp.sum(powers, axis=1, keepdims=True)).astype(jnp.bfloat16)
+            mixed += chosen * jnp.dot(soft, values, preferred_element_type=jnp.float32)
+        out_ref[mine, :] = mixed.astype(jnp.bfloat16)
+
+
+def attend(projected, seg_ids, sequences, scaling):
+    _, count, width = projected.shape
+    length = count // sequences
+
+    def of(j):
+        return pl.BlockSpec((None, length, LANES), lambda s, h: (j, s, h))
+
+    return pl.pallas_call(
+        functools.partial(attend_kernel, scaling),
+        grid=(sequences, width // LANES),
+        out_shape=jax.ShapeDtypeStruct((count, width), jnp.bfloat16),
+        in_specs=[
+            of(0),
+            of(1),
+            of(2),
+            pl.BlockSpec((length, 1), lambda s, h: (s, 0)),
+            pl.BlockSpec((1, length), lambda s, h: (0, s)),
+        ],
+        out_specs=pl.BlockSpec((length, LANES), lambda s, h: (s, h)),
+        compiler_params=pltpu.CompilerParams(vmem_limit_bytes=VMEM_LIMIT),
+        cost_estimate=pl.CostEstimate(
+            flops=16 * count * length * width, bytes_accessed=8 * count * width, transcendentals=0
+        ),
+    )(projected, projected, projected, seg_ids[:, None], seg_ids[None, :])
+
+
+def attend_back_kernel(scaling, q_ref, k_ref, v_ref, grad_ref, row_ref, column_ref, out_ref):
+    length = q_ref.shape[0]
+    rows = math.gcd(length, LANES)
+    half = lax.broadcasted_iota(jnp.int32, (1, LANES), 1) // HEAD
+    across = (((1,), (1,)), ((), ()))
+    down = (((0,), (0,)), ((), ()))
+
+    def product(a, b, dims):
+        return lax.dot_general(a, b, dims, preferred_element_type=jnp.float32)
+
+    def put(slot, place, values, first):
+        if first:
+            out_ref[slot, place, :] = values
+        else:
+            out_ref[slot, place, :] += values
+
+    for part in range(LANES // HEAD):
+        chosen = (half == part).astype(jnp.float32)
+        only = chosen.astype(jnp.bfloat16)
+        for block in range(length // rows):
+            mine, seen = slice(block * rows, (block + 1) * rows), slice(0, (block + 1) * rows)
+            fresh = part == 0
+            query = q_ref[mine, :] * only
+            grad = grad_ref[mine, :] * only
+            keys, values = k_ref[seen, :], v_ref[seen, :]
+            scores = product(query, keys, across) * scaling
+            row_place = lax.broadcasted_iota(jnp.int32, scores.shape, 0) + block * rows
+            column_place = lax.broadcasted_iota(jnp.int32, scores.shape, 1)
+            allowed = (column_place <= row_place) & (row_ref[mine, :] == column_ref[:, seen])
+            scores = jnp.where(allowed, scores, MASKED_SCORE)
+            powers = jnp.exp(scores - jnp.max(scores, axis=1, keepdims=True))
+            soft = powers / jnp.sum(powers, axis=1, keepdims=True)
+            weight_grad = product(grad, values, across)
+            score_grad = soft * (
+                weight_grad - jnp.sum(soft * weight_grad, axis=1, keepdims=True)
+            )
+            score_grad = score_grad.astype(jnp.bfloat16)
+            put(0, mine, product(score_grad, keys, (((1,), (0,)), ((), ()))) * (scaling * chosen), fresh)
+            key_grad = product(score_grad, query, down) * scaling
+            value_grad = product(soft.astype(jnp.bfloat16), grad, down)
+            if fresh:
+                key_new = slice(block * rows, (block + 1) * rows)
+                if block:
+                    old = slice(0, block * rows)
+                    put(1, old, key_grad[: block * rows], False)
+                    put(2, old, value_grad[: block * rows], False)
+                put(1, key_new, key_grad[block * rows :], True)
+                put(2, key_new, value_grad[block * rows :], True)
+            else:
+                put(1, seen, key_grad, False)
+                put(2, seen, value_grad, False)
+
+
+def attend_back(projected, grad, seg_ids, sequences, scaling):
+    _, count, width = projected.shape
+    length = count // sequences
+    head_block = pl.BlockSpec((length, LANES), lambda s, h: (s, h))
+
+    def of(j):
+        return pl.BlockSpec((None, length, LANES), lambda s, h: (j, s, h))
+
+    return pl.pallas_call(
+        functools.partial(attend_back_kernel, scaling),
+        grid=(sequences, width // LANES),
+        out_shape=jax.ShapeDtypeStruct((3, count, width), jnp.float32),
+        in_specs=[
+            of(0),
+            of(1),
+            of(2),
+            head_block,
+            pl.BlockSpec((length, 1), lambda s, h: (s, 0)),
+            pl.BlockSpec((1, length), lambda s, h: (0, s)),
+        ],
+        out_specs=pl.BlockSpec((3, length, LANES), lambda s, h: (0, s, h)),
+        compiler_params=pltpu.CompilerParams(vmem_limit_bytes=VMEM_LIMIT),
+        cost_estimate=pl.CostEstimate(
+            flops=40 * count * length * width, bytes_accessed=20 * count * width, transcendentals=0
+        ),
+    )(projected, projected, projected, grad, seg_ids[:, None], seg_ids[None, :])
 
 
 def row_lists(local_ids, vocab_rows, offset):
@@ -252,15 +373,12 @@
     length = segments.shape[1]
     local_rows = segments.shape[0] * length
     width = attention.shape[2]
-    head_count = width // HEAD
     local_experts = expert_in.shape[0]
     experts = local_experts * members
     vocab_rows = embedding.shape[0]
     capacity = max(2, 3 * local_rows * TOP // (2 * experts))
     loss_local = positions.shape[0]
     loss_count = loss_local * members * replicas
-    block_rows = min(512, length)
-    block_count = local_rows // block_rows
     scaling = HEAD ** (-0.5)
     highest_precision = lax.Precision.HIGHEST
     share = width // replicas
@@ -298,28 +416,33 @@
         vocab_rows,
     )
     rows_parts = shared(embedding.astype(jnp.bfloat16), members)
+    id_rows = -(-2 * group_ids.shape[0] // width)
+    digits = jnp.concatenate([group_ids >> 8, group_ids & 255])
+    digits = jnp.pad(digits, (0, id_rows * width - digits.shape[0])).reshape(id_rows, width)
     dense_part = jnp.concatenate([dense_part, small_flat], axis=0).astype(jnp.bfloat16)
-    dense_part, group_ids, rows_parts[1] = lax.optimization_barrier(
-        (dense_part, group_ids, rows_parts[1])
-    )
-    level_ids = in_order([dp_swap(group_ids, 2 * k, replicas) for k in range(levels)], level)
-    all_ids = by_core(level_ids, 1).reshape(replicas, members, local_rows)
+    dense_part = jnp.concatenate([dense_part, digits.astype(jnp.bfloat16)], axis=0)
+    dense_part, rows_parts[1] = lax.optimization_barrier((dense_part, rows_parts[1]))
+    rows_parts[-1], taken = lax.optimization_barrier((rows_parts[-1], taken))
+    dense_part = in_order([dp_swap(dense_part, 2 * k, replicas) for k in range(levels)], level)
+    others = by_core(dense_part[:, chunk:], 1).reshape(replicas, small_rows + id_rows, width)
+    small_low, digits = others[:, :small_rows], others[:, small_rows:].reshape(replicas, -1)
+    digits = digits[:, : 2 * group_ids.shape[0]].astype(jnp.int32)
+    digits = digits.reshape(replicas, 2, members, local_rows)
+    all_ids = digits[:, 0] * 256 + digits[:, 1]
     column_ids = lax.dynamic_index_in_dim(all_ids, my_index, 1, keepdims=False).reshape(-1)
-    dense_part = in_order([dp_swap(dense_part, 2 * k, replicas) for k in range(levels)], level)
-    rows_parts[-1], taken, dense_part = lax.optimization_barrier(
-        (rows_parts[-1], taken, dense_part)
-    )
-
-    small_low = by_core(dense_part[:, chunk:], 1).reshape(replicas, small_rows * width)
+    small_low = small_low.reshape(replicas, small_rows * width)
     small_low = small_low[:, : small_params.size].reshape(replicas, small_params.shape[0], share)
     small_low = small_low.transpose(1, 0, 2).reshape(small_params.shape[0], width)
     gain_rows = small_low[:3].astype(jnp.float32)
     router = small_low[3:].astype(jnp.float32)
+    rows_parts[-1], dense_part = lax.optimization_barrier(
+        (rows_parts[-1], dense_part[:, :chunk])
+    )
     rows_table = jnp.concatenate(rows_parts, axis=0)
     places = partner_of(my_index, column_ids // vocab_rows, members) * vocab_rows
     places = places + column_ids % vocab_rows
     stream_parts = jnp.take(rows_table, places, axis=0, mode="clip")
-    dense_parts = shared(dense_part[:, :chunk], members)
+    dense_parts = shared(dense_part, members)
     stream_parts, dense_parts = lax.optimization_barrier((stream_parts, dense_parts))
     dense_low = by_core(in_order(dense_parts, my_index), 2)
     dense_low = (
@@ -337,28 +460,9 @@
     projected = jnp.einsum(
         "td,jde->jte", attn_in, dense_low[:3], preferred_element_type=jnp.float32
     ).astype(jnp.bfloat16)
-    query = projected[0].reshape(local_rows, head_count, HEAD)
-    keys = projected[1].reshape(local_rows, head_count, HEAD)
-    values = projected[2].reshape(local_rows, head_count, HEAD)
     seg_ids = segments.reshape(-1)
 
-    def forward_block(block_index):
-        scores, query_block, key_block, first_row = block_scores(
-            query, keys, seg_ids, block_index, length, block_rows, scaling
-        )
-        highest = jnp.max(scores, axis=-1, keepdims=True)
-        powers = jnp.exp(scores - highest)
-        totals = jnp.sum(powers, axis=-1, keepdims=True)
-        mixed_block = jnp.einsum(
-            "hqk,khd->qhd",
-            (powers / totals).astype(jnp.bfloat16),
-            values,
-            preferred_element_type=jnp.float32,
-        )
-        return (mixed_block, (highest + jnp.log(totals))[..., 0])
-
-    mixed_blocks, log_totals = lax.map(forward_block, jnp.arange(block_count))
-    mixed = mixed_blocks.reshape(local_rows, width).astype(jnp.bfloat16)
+    mixed = attend(projected, seg_ids, local_rows // length, scaling)
     hidden_one = stream + jnp.dot(mixed, dense_low[3], preferred_element_type=jnp.float32)
     normal_two, factor_two = normal_parts(hidden_one)
     moe_in = (normal_two * gain_rows[1]).astype(jnp.bfloat16)
@@ -490,50 +594,10 @@
     mixed_grad = jnp.einsum(
         "td,cd->tc", attn_grad, dense_low[3], preferred_element_type=jnp.float32
     )
-    mixed_grad = mixed_grad.astype(jnp.bfloat16).reshape(local_rows, head_count, HEAD)
-
-    def backward_block(carry, inputs):
-        keys_grad, values_grad = carry
-        block_index, log_block = inputs
-        scores, query_block, key_block, first_row = block_scores(
-            query, keys, seg_ids, block_index, length, block_rows, scaling
-        )
-        soft_block = jnp.exp(scores - log_block[..., None])
-        value_part = jnp.einsum(
-            "hqk,qhd->khd",
-            soft_block.astype(jnp.bfloat16),
-            mixed_grad,
-            preferred_element_type=jnp.float32,
-        )
-        weight_grad = jnp.einsum(
-            "qhd,khd->hqk", mixed_grad, values, preferred_element_type=jnp.float32
-        )
-        score_grad = soft_block * (
-            weight_grad - jnp.sum(soft_block * weight_grad, axis=-1, keepdims=True)
-        )
-        score_grad = score_grad.astype(jnp.bfloat16)
-        query_part = (
-            jnp.einsum("hqk,khd->qhd", score_grad, key_block, preferred_element_type=jnp.float32)
-            * scaling
-        )
-        key_part = (
-            jnp.einsum("hqk,qhd->khd", score_grad, query_block, preferred_element_type=jnp.float32)
-            * scaling
-        )
-        keys_grad = keys_grad + key_part
-        values_grad = values_grad + value_part
-        return ((keys_grad, values_grad), query_part)
-
-    zero_grad = jnp.zeros((local_rows, head_count, HEAD), jnp.float32)
-    (keys_grad, values_grad), query_parts = lax.scan(
-        backward_block, (zero_grad, zero_grad), (jnp.arange(block_count), log_totals)
-    )
-    projected_grad = jnp.stack(
-        [
-            query_parts.reshape(local_rows, width),
-            keys_grad.reshape(local_rows, width),
-            values_grad.reshape(local_rows, width),
-        ]
+    mixed_grad = mixed_grad.astype(jnp.bfloat16)
+
+    projected_grad = attend_back(
+        projected, mixed_grad, seg_ids, local_rows // length, scaling
     ).astype(jnp.bfloat16)
     qkv_grad = jnp.einsum(
         "td,jte->jde", attn_in, projected_grad, preferred_element_type=jnp.float32
@@ -629,9 +693,7 @@
         (column_grads[-1], third_out, summed)
     )
     stream_sum = add_rows(token_rows[half:], column_grads[half:], vocab_rows, stream_sum)
-    stream_sum, in_sum = lax.optimization_barrier((stream_sum, in_sum))
     embed_sum = embed_sum.astype(jnp.float32) + stream_sum.T
-    in_sum = in_sum.astype(jnp.float32)
     loss_value = small_sum[small_params.size]
     small_sum = small_sum[: small_params.size].reshape(small_params.shape[0], share)
     attention_sum = in_order(shared(summed, members), my_index)
@@ -640,14 +702,17 @@
     first_out = nesterov_update(
         attention, attention_moment, attention_average, attention_sum, RATE_TABLE[0] * rate_base
     )
-    second_out = nesterov_update(
-        expert_in, expert_in_moment, expert_in_average, in_sum, RATE_TABLE[1] * rate_base
-    )
     fourth_out = nesterov_update(
         embedding, embedding_moment, embedding_average, embed_sum, RATE_TABLE[3] * rate_base
     )
     fifth_out = nesterov_update(
         small_params, small_moment, small_average, small_sum, RATE_TABLE[4] * rate_base
+    )
+    first_out, fourth_out, fifth_out, in_sum = lax.optimization_barrier(
+        (first_out, fourth_out, fifth_out, in_sum)
+    )
+    second_out = nesterov_update(
+        expert_in, expert_in_moment, expert_in_average, in_sum.astype(jnp.float32), RATE_TABLE[1] * rate_base
     )
     return (loss_value,) + first_out + second_out + third_out + fourth_out + fifth_out
 

time: 780 us -> 764 us (0.979)
  the two profiles are of different devices: /device:TPU:8 before, /device:TPU:0 now
where the time goes in v4:
time: 764 us; the launch traced here: 748 us
  waiting for transfers between devices  196 us (26%)
  matrix products  182 us (24%)
  Pallas kernels  98.5 us (13%)
  local copies, waits for them, and re-layouts  92.5 us (12%)
  other arithmetic  88.6 us (12%)
  starting transfers between devices  54.9 us (7%)
  blocking collectives  17.9 us (2%)
  between operations  17.4 us (2%)
    ppermute x30, waiting for transfers between devices, swap(): lax.ppermute(value, 'expert', partner_order(members)[k])  103 us
    pallas_call x2, Pallas kernels, add_rows(): pl.pallas_call(add_rows_kernel, out_shape=jax.ShapeDtypeStruct(shape, jnp...  53 us
    all_to_all x1, waiting for transfers between devices, shards(): lax.all_to_all(stream_parts, 'dp', split_axis=0, concat_axis=1, tiled=True)  40.3 us
    ppermute x30, starting transfers between devices, swap(): lax.ppermute(value, 'expert', partner_order(members)[k])  35.8 us
    all_to_all x1, waiting for transfers between devices, shards(): lax.all_to_all(stream_grad, 'dp', split_axis=1, concat_axis=0, tiled=True)  29 us
    pallas_call x1, Pallas kernels, attend_back(): pl.pallas_call(functools.partial(attend_back_kernel, scaling), grid=(sequ...  26.6 us
    dot_general x1, matrix products, shards(): jnp.einsum('ecd,efd->ecf', arrived_grad, out_low, preferred_element_type=...  21.5 us
    concatenate x2, local copies, waits for them, and re-layouts, shards(): rows_table = jnp.concatenate(rows_parts, axis=0)  20.5 us
  transfers between devices with their start and end apart: 48, of which 18 were waited for; matrix products, arithmetic and copies ran while one was open for 42% of the time, Pallas kernels for 13%

profile of v4, /device:TPU:0, one launch (start us, length us, event | category | flops | bytes accessed | tf_op | source)
XLA Modules:
  0.0 748.5 jit_solution(1582189597086281909)
XLA Ops:
  20.0 6.0 iota_compare_fusion
  27.0 5.2 select_convert_fusion.2
  32.2 20.3 %collective-permute-done = bf16[8000,96]{0,1:T(8,128)(2,1)} collective-permute-done((bf16[8000,96]{0,1:T(8,128)(2,1)}, bf16[8000,96]{0,1:T(8,128)(2,1)}, u32[]{:S(2)}, u32[]{:S(2)}) %collective-permute-start) | collective-permute-done | bytes 1536032 | tf_op jit(solution)/shard_map/ppermute | solution.py:33
  57.2 18.4 %fusion = f32[256,63,128]{2,1,0:T(8,128)} fusion(pred[256,65,128]{2,1,0:T(8,128)(4,1)} %iota_compare_fusion, bf16[256,65,63]{1,2,0:T(8,128)(2,1)} %get-tuple-element.211, bf16[256,65,63]{1,2,0:T(8,128)(2,1)} %get-tuple-element.212, bf16[256,65,63]{1,2,0:T(8,128)(2,1)S(1)} %get-tuple-element.210), kind=kOutput, calls=%fused_computation.3 | convolution fusion | flops 836759040 | bytes 16677376 | tf_op jit(solution)/shard_map/pih,pil->phl/dot_general | solution.py:97
  75.6 9.2 %copy.298 = f32[256,63,128]{0,2,1:T(8,128)} copy(f32[256,63,128]{2,1,0:T(8,128)} %fusion) | data formatting | bytes 16515072 | tf_op jit(solution)/shard_map/pih,pil->phl/dot_general | solution.py:97
  84.8 7.1 slice.273
  95.9 10.6 %concatenate.110 = bf16[32000,96]{0,1:T(8,128)(2,1)} concatenate(bf16[8000,96]{0,1:T(8,128)(2,1)} %convert_element_type.384, bf16[8000,96]{0,1:T(8,128)(2,1)} %collective-permute-done, bf16[8000,96]{0,1:T(8,128)(2,1)} %collective-permute-done.1, bf16[8000,96]{0,1:T(8,128)(2,1)} %collective-permute-done.2), dimensions={0} | concatenate | bytes 12288000 | tf_op jit(solution)/shard_map/concatenate | solution.py:441
  106.5 9.9 %copy.300 = bf16[32000,96]{1,0:T(8,128)(2,1)} copy(bf16[32000,96]{0,1:T(8,128)(2,1)} %concatenate.110) | data formatting | bytes 12288000 | tf_op jit(solution)/shard_map/concatenate | solution.py:441
  117.5 15.8 %gather_fusion = bf16[4096,96]{1,0:T(8,128)(2,1)S(1)} fusion(bf16[32000,96]{1,0:T(8,128)(2,1)} %copy.300, s32[4096]{0:T(1024)S(1)} %broadcast_clamp_fusion), kind=kCustom, calls=%fused_computation | custom fusion | bytes 1589248 | tf_op jit(solution)/shard_map/jit(_take)/gather | solution.py:444
  139.2 5.2 all-to-all-start
  146.5 40.3 %all-to-all-done = bf16[8,512,96]{1,2,0:T(8,128)(2,1)S(1)} async-done(((bf16[8,512,96]{1,2,0:T(8,128)(2,1)}), bf16[8,512,96]{1,2,0:T(8,128)(2,1)S(1)}, u32[]{:S(2)}, u32[]{:S(2)}) %all-to-all-start) | async-done | bytes 786464 | tf_op jit(solution)/shard_map/all_to_all | solution.py:455
  195.0 3.5 convert_bitcast_fusion.q_ref.k_ref.v_ref
  198.5 18.9 %shard_map.373 = bf16[512,768]{1,0:T(8,128)(2,1)} custom-call(bf16[3,512,768]{2,1,0:T(8,128)(2,1)} %convert_bitcast_fusion.q_ref.k_ref.v_ref, bf16[3,512,768]{2,1,0:T(8,128)(2,1)} %convert_bitcast_fusion.q_ref.k_ref.v_ref, bf16[3,512,768]{2,1,0:T(8,128)(2,1)} %convert_bitcast_fusion.q_ref.k_ref.v_ref, s32[512,1]{1,0:T(8,128)} %copy.306.row_ref, ...), custom_call_target="tpu_custom_call" | custom-call | flops 3221225472 | bytes 3145728 | tf_op jit(solution)/shard_map/pallas_call | solution.py:190
  230.2 9.3 %collective-permute-done.11 = bf16[384,768]{1,0:T(8,128)(2,1)} collective-permute-done((bf16[384,768]{1,0:T(8,128)(2,1)}, bf16[384,768]{1,0:T(8,128)(2,1)}, u32[]{:S(2)}, u32[]{:S(2)}) %collective-permute-start.11) | collective-permute-done | bytes 589856 | tf_op jit(solution)/shard_map/ppermute | solution.py:33
  239.6 12.5 %collective-permute-done.12 = bf16[384,768]{1,0:T(8,128)(2,1)} collective-permute-done((bf16[384,768]{1,0:T(8,128)(2,1)}, bf16[384,768]{1,0:T(8,128)(2,1)}, u32[]{:S(2)}, u32[]{:S(2)}) %collective-permute-start.12) | collective-permute-done | bytes 589856 | tf_op jit(solution)/shard_map/ppermute | solution.py:33
  255.4 15.4 %fusion.128 = f32[2,768,3072]{2,1,0:T(8,128)} fusion(bf16[2,768,768]{2,1,0:T(8,128)(2,1)} %bitcast.300, bf16[2,768,3072]{2,1,0:T(8,128)(2,1)} %all-gather.6.cloned.1.call-done), kind=kOutput, calls=%fused_computation.395 | convolution fusion | flops 7247757312 | bytes 30670848 | tf_op jit(solution)/shard_map/ecd,edf->ecf/dot_general | solution.py:502
  270.8 15.6 %convolution_convert_fusion.6 = bf16[2,768,768]{2,1,0:T(8,128)(2,1)S(1)} fusion(bf16[2,3072,768]{2,1,0:T(8,128)(2,1)} %all-gather.8.cloned.1.call-done, f32[2,768,3072]{2,1,0:T(8,128)} %fusion.128), kind=kOutput, calls=%fused_computation.96 | convolution fusion | flops 7291404288 | bytes 30670848 | tf_op jit(solution)/shard_map/ecf,efd->ecd/dot_general | solution.py:504
  291.2 12.8 %collective-permute-done.14 = bf16[384,768]{1,0:T(8,128)(2,1)S(1)} collective-permute-done((bf16[384,768]{1,0:T(8,128)(2,1)}, bf16[384,768]{1,0:T(8,128)(2,1)S(1)}, u32[]{:S(2)}, u32[]{:S(2)}) %collective-permute-start.14) | collective-permute-done | bytes 589856 | tf_op jit(solution)/shard_map/ppermute | solution.py:33
  304.0 11.1 %collective-permute-done.15 = bf16[384,768]{1,0:T(8,128)(2,1)} collective-permute-done((bf16[384,768]{1,0:T(8,128)(2,1)}, bf16[384,768]{1,0:T(8,128)(2,1)}, u32[]{:S(2)}, u32[]{:S(2)}) %collective-permute-start.15) | collective-permute-done | bytes 589856 | tf_op jit(solution)/shard_map/ppermute | solution.py:33
  321.6 9.7 %all_gather.20 = bf16[256,768]{1,0:T(8,128)(2,1)} all-gather(bf16[64,768]{1,0:T(8,128)(2,1)S(1)} %convolution_convert_fusion.9), channel_id=1, replica_groups=mesh['dp'=8,'expert'=4] {'expert'}, dimensions={0}, use_global_device_ids=true | all-gather | bytes 491520 | tf_op jit(solution)/shard_map/all_gather | solution.py:516
  331.3 9.6 %all-gather.10.cloned.1.call-done = bf16[8000,768]{0,1:T(8,128)(2,1)} async-done(((bf16[8000,96]{0,1:T(8,128)(2,1)}), bf16[8000,768]{0,1:T(8,128)(2,1)}) %all-gather.10.cloned.1.call-update) | async-done | bytes 12288016 | tf_op jit(solution)/shard_map/all_gather | solution.py:396
  340.8 8.5 %fusion.126 = (f32[256]{0:T(256)S(1)}, f32[256,8000]{0,1:T(8,128)S(1)}) fusion(bf16[256,768]{1,0:T(8,128)(2,1)} %all_gather.20, bf16[8000,768]{0,1:T(8,128)(2,1)} %all-gather.10.cloned.1.call-done), kind=kOutput, calls=%fused_computation.393 | convolution fusion | flops 3147775744 | bytes 20874240 | tf_op jit(solution)/shard_map/gd,vd->gv/dot_general | solution.py:517
  349.3 4.6 exponential_reduce_fusion
  354.0 8.3 %all-gather.1 = f32[4,3,256]{2,1,0:T(4,128)S(1)} all-gather(f32[1,3,256]{2,1,0:T(4,128)S(1)} %maximum_bitcast_fusion.4), channel_id=2, replica_groups=mesh['dp'=8,'expert'=4] {'expert'}, dimensions={0}, use_global_device_ids=true | all-gather | bytes 15360 | tf_op jit(solution)/shard_map/all_gather | solution.py:521
  362.9 3.2 multiply_convert_fusion.1
  366.1 10.2 %convolution_convert_fusion = bf16[8000,768]{0,1:T(8,128)(2,1)} fusion(bf16[256,8000]{0,1:T(8,128)(2,1)} %multiply_convert_fusion.1, bf16[256,768]{1,0:T(8,128)(2,1)} %all_gather.20), kind=kOutput, calls=%fused_computation.17 | convolution fusion | flops 3151872000 | bytes 16777216 | tf_op jit(solution)/shard_map/gv,gd->vd/dot_general | solution.py:533
  376.5 13.8 %fusion.129 = f32[256,768]{1,0:T(8,128)S(1)} fusion(bf16[256,8000]{0,1:T(8,128)(2,1)} %multiply_convert_fusion.1, bf16[8000,768]{0,1:T(8,128)(2,1)} %all-gather.10.cloned.1.call-done), kind=kOutput, calls=%fused_computation.396 | convolution fusion | flops 3145728000 | bytes 17170432 | tf_op jit(solution)/shard_map/dot_general | solution.py:538
  398.4 3.1 collective-permute-done.18
  411.7 12.8 %collective-permute-done.20 = bf16[384,768]{1,0:T(8,128)(2,1)S(1)} collective-permute-done((bf16[384,768]{1,0:T(8,128)(2,1)S(1)}, bf16[384,768]{1,0:T(8,128)(2,1)S(1)}, u32[]{:S(2)}, u32[]{:S(2)}) %collective-permute-start.20) | collective-permute-done | bytes 589856 | tf_op jit(solution)/shard_map/ppermute | solution.py:33
  424.5 8.7 %collective-permute-done.21 = bf16[384,768]{1,0:T(8,128)(2,1)S(1)} collective-permute-done((bf16[384,768]{1,0:T(8,128)(2,1)S(1)}, bf16[384,768]{1,0:T(8,128)(2,1)S(1)}, u32[]{:S(2)}, u32[]{:S(2)}) %collective-permute-start.21) | collective-permute-done | bytes 589856 | tf_op jit(solution)/shard_map/ppermute | solution.py:33
  434.4 21.5 %fusion.12 = bf16[2,768,3072]{2,1,0:T(8,128)(2,1)} fusion(f32[2,768,3072]{2,1,0:T(8,128)} %fusion.128, bf16[2,768,768]{2,1,0:T(8,128)(2,1)S(1)} %bitcast.303, bf16[2,3072,768]{2,1,0:T(8,128)(2,1)S(1)} %bitcast.370), kind=kOutput, calls=%fused_computation.15 | convolution fusion | flops 7342129152 | bytes 40108032 | tf_op jit(solution)/shard_map/ecd,efd->ecf/dot_general | solution.py:576
  456.0 13.0 %convolution_convert_fusion.5 = bf16[2,768,768]{2,1,0:T(8,128)(2,1)S(1)} fusion(bf16[2,768,3072]{2,1,0:T(8,128)(2,1)} %fusion.12, bf16[2,768,3072]{2,1,0:T(8,128)(2,1)} %all-gather.6.cloned.1.call-done), kind=kOutput, calls=%fused_computation.95 | convolution fusion | flops 7248936960 | bytes 21233664 | tf_op jit(solution)/shard_map/ecf,edf->ecd/dot_general | solution.py:582
  473.6 13.6 %convolution_convert_fusion.1 = bf16[2,768,3072]{2,1,0:T(8,128)(2,1)} fusion(bf16[2,768,768]{2,1,0:T(8,128)(2,1)S(1)} %bitcast.301, bf16[2,768,3072]{2,1,0:T(8,128)(2,1)} %fusion.12), kind=kOutput, calls=%fused_computation.31 | convolution fusion | flops 7252475904 | bytes 21233664 | tf_op jit(solution)/shard_map/ecd,ecf->edf/dot_general | solution.py:581
  487.2 17.0 %convolution_convert_fusion.2 = bf16[2,3072,768]{2,1,0:T(8,128)(2,1)} fusion(bf16[2,768,768]{2,1,0:T(8,128)(2,1)S(1)} %bitcast.304, f32[2,768,3072]{2,1,0:T(8,128)} %fusion.128), kind=kOutput, calls=%fused_computation.32 | convolution fusion | flops 7294943232 | bytes 30670848 | tf_op jit(solution)/shard_map/ecf,ecd->efd/dot_general | solution.py:573
  519.6 3.5 fusion.35
  527.6 26.6 %shard_map.374 = f32[3,512,768]{2,1,0:T(8,128)} custom-call(bf16[3,512,768]{2,1,0:T(8,128)(2,1)} %convert_bitcast_fusion.q_ref.k_ref.v_ref, bf16[3,512,768]{2,1,0:T(8,128)(2,1)} %convert_bitcast_fusion.q_ref.k_ref.v_ref, bf16[3,512,768]{2,1,0:T(8,128)(2,1)} %convert_bitcast_fusion.q_ref.k_ref.v_ref, bf16[512,768]{1,0:T(8,128)(2,1)} %convolution_convert_fusion.8.grad_ref, ...), custom_call_target="tpu_custom_call" | custom-call | flops 8053063680 | bytes 7864320 | tf_op jit(solution)/shard_map/pallas_call | solution.py:270
  554.2 5.7 multiply_reduce_fusion.3
  570.9 3.8 all-to-all-start.1
  579.7 29.0 %all-to-all-done.1 = bf16[512,8,96]{0,2,1:T(8,128)(2,1)S(1)} async-done(((bf16[512,8,96]{0,2,1:T(8,128)(2,1)}), bf16[512,8,96]{0,2,1:T(8,128)(2,1)S(1)}, u32[]{:S(2)}, u32[]{:S(2)}) %all-to-all-start.1) | async-done | bytes 786464 | tf_op jit(solution)/shard_map/all_to_all | solution.py:619
  609.6 3.2 convert_add_fusion
  622.5 6.7 collective-permute-done.31.refs_1_
  630.1 23.4 %shard_map.375.refs_2_ = f32[8064,128]{1,0:T(8,128)} custom-call(s32[64]{0:T(128)} %pad_add_fusion.5.count_ref, s32[64,128]{1,0:T(8,128)} %pad_add_fusion.1.row_ref, s32[64,128]{1,0:T(8,128)} %pad_add_fusion.2.source_ref, bf16[96,4096]{1,0:T(8,128)(2,1)} %bitcast.294, bf16[96,4096]{1,0:T(8,128)(2,1)} %copy-done.40), custom_call_target="tpu_custom_call" | custom-call | flops 8388608 | bytes 231735296 | tf_op jit(solution)/shard_map/pallas_call | solution.py:322
  670.8 3.6 collective-permute-done.32
  674.3 5.7 collective-permute-done.33
  680.1 4.4 collective-permute-done.34
  688.4 29.5 %shard_map.376 = f32[96,8064]{1,0:T(8,128)} custom-call(s32[64]{0:T(128)} %pad_add_fusion.6.count_ref, s32[64,128]{1,0:T(8,128)} %pad_add_fusion.3.row_ref, s32[64,128]{1,0:T(8,128)} %pad_add_fusion.4.source_ref, bf16[96,4096]{1,0:T(8,128)(2,1)} %collective-permute-done.39.refs_0_, bf16[96,4096]{1,0:T(8,128)(2,1)} %collective-permute-done.35.refs_1_, ...), custom_call_target="tpu_custom_call" | custom-call | flops 8388608 | bytes 231735296 | tf_op jit(solution)/shard_map/pallas_call | solution.py:322
  717.9 6.0 fusion.114
  734.3 4.6 fusion.111
  (507 shorter events, 170.6 us)
Async XLA Ops:
  7.2 248.2 %all-gather.6.cloned.1.call-start = ((), (), s32[]{:S(2)}) async-start(), calls=%async_computation.5 | async-start | bytes 10616832 | tf_op jit(solution)/shard_map/all_gather | solution.py:394
  10.1 260.7 %all-gather.8.cloned.1.call-start = ((), (), s32[]{:S(2)}) async-start(), calls=%async_computation.6 | async-start | bytes 10616832 | tf_op jit(solution)/shard_map/all_gather | solution.py:395
  13.2 327.6 %all-gather.10.cloned.1.call-start = ((), (), s32[]{:S(2)}) async-start(), calls=%async_computation.7 | async-start | bytes 13934592 | tf_op jit(solution)/shard_map/all_gather | solution.py:396
  14.6 37.9 %collective-permute-start = (bf16[8000,96]{0,1:T(8,128)(2,1)}, bf16[8000,96]{0,1:T(8,128)(2,1)}, u32[]{:S(2)}, u32[]{:S(2)}) collective-permute-start(bf16[8000,96]{0,1:T(8,128)(2,1)} %convert_element_type.384), channel_id=1, source_target_pairs={{0,1},{1,0},{2,3},{3,2},{4,5},{5,4},{6,7},{7,6},{8,9},{9,8},{10,11... | collective-permute-start | bytes 4608008 | tf_op jit(solution)/shard_map/ppermute | solution.py:33
  17.5 74.4 %collective-permute-start.2 = (bf16[8000,96]{0,1:T(8,128)(2,1)}, bf16[8000,96]{0,1:T(8,128)(2,1)}, u32[]{:S(2)}, u32[]{:S(2)}) collective-permute-start(bf16[8000,96]{0,1:T(8,128)(2,1)} %convert_element_type.384), channel_id=1, source_target_pairs={{0,3},{1,2},{2,1},{3,0},{4,7},{5,6},{6,5},{7,4},{8,11},{9,10},{10,... | collective-permute-start | bytes 4608008 | tf_op jit(solution)/shard_map/ppermute | solution.py:33
  19.0 76.9 %collective-permute-start.1 = (bf16[8000,96]{0,1:T(8,128)(2,1)}, bf16[8000,96]{0,1:T(8,128)(2,1)}, u32[]{:S(2)}, u32[]{:S(2)}) collective-permute-start(bf16[8000,96]{0,1:T(8,128)(2,1)} %convert_element_type.384), channel_id=1, source_target_pairs={{0,2},{1,3},{2,0},{3,1},{4,6},{5,7},{6,4},{7,5},{8,10},{9,11},{10,... | collective-permute-start | bytes 4608008 | tf_op jit(solution)/shard_map/ppermute | solution.py:33
  52.5 39.4 %collective-permute-start.3 = (bf16[104,768]{1,0:T(8,128)(2,1)S(1)}, bf16[104,768]{1,0:T(8,128)(2,1)S(1)}, u32[]{:S(2)}, u32[]{:S(2)}) collective-permute-start(bf16[104,768]{1,0:T(8,128)(2,1)S(1)} %pad_maximum_fusion.22), channel_id=1, source_target_pairs={{0,8},{4,12},{8,0},{12,4},{16,24},{20,28},{24,16},{28,20},{1,9},{5... | collective-permute-start | bytes 479240 | tf_op jit(solution)/shard_map/ppermute | solution.py:37
  54.6 37.3 %collective-permute-start.4 = (bf16[104,768]{1,0:T(8,128)(2,1)S(1)}, bf16[104,768]{1,0:T(8,128)(2,1)S(1)}, u32[]{:S(2)}, u32[]{:S(2)}) collective-permute-start(bf16[104,768]{1,0:T(8,128)(2,1)S(1)} %pad_maximum_fusion.22), channel_id=1, source_target_pairs={{0,16},{4,20},{8,24},{12,28},{16,0},{20,4},{24,8},{28,12},{1,17},{... | collective-permute-start | bytes 479240 | tf_op jit(solution)/shard_map/ppermute | solution.py:37
  57.2 34.7 %collective-permute-start.5 = (bf16[104,768]{1,0:T(8,128)(2,1)S(1)}, bf16[104,768]{1,0:T(8,128)(2,1)S(1)}, u32[]{:S(2)}, u32[]{:S(2)}) collective-permute-start(bf16[104,768]{1,0:T(8,128)(2,1)S(1)} %pad_maximum_fusion.22), channel_id=1, source_target_pairs={{0,24},{4,28},{8,16},{12,20},{16,8},{20,12},{24,0},{28,4},{1,25},{... | collective-permute-start | bytes 479240 | tf_op jit(solution)/shard_map/ppermute | solution.py:37
  92.1 24.3 %collective-permute-start.6 = (bf16[4,8,768]{2,1,0:T(8,128)(2,1)S(1)}, bf16[4,8,768]{2,1,0:T(8,128)(2,1)S(1)}, u32[]{:S(2)}, u32[]{:S(2)}) collective-permute-start(bf16[4,8,768]{2,1,0:T(8,128)(2,1)S(1)} %pad_maximum_fusion.24), channel_id=1, source_target_pairs={{0,4},{4,0},{8,12},{12,8},{16,20},{20,16},{24,28},{28,24},{1,5},{5... | collective-permute-start | bytes 147464 | tf_op jit(solution)/shard_map/ppermute | solution.py:37
  92.3 40.9 %collective-permute-start.7 = (bf16[4,96,768]{2,1,0:T(8,128)(2,1)S(1)}, bf16[4,96,768]{2,1,0:T(8,128)(2,1)S(1)}, u32[]{:S(2)}, u32[]{:S(2)}) collective-permute-start(bf16[4,96,768]{2,1,0:T(8,128)(2,1)S(1)} %slice.274), channel_id=1, source_target_pairs={{0,1},{1,0},{2,3},{3,2},{4,5},{5,4},{6,7},{7,6},{8,9},{9,8},{10,11... | collective-permute-start | bytes 1769480 | tf_op jit(solution)/shard_map/ppermute | solution.py:33
  94.2 39.0 %collective-permute-start.8 = (bf16[4,96,768]{2,1,0:T(8,128)(2,1)S(1)}, bf16[4,96,768]{2,1,0:T(8,128)(2,1)}, u32[]{:S(2)}, u32[]{:S(2)}) collective-permute-start(bf16[4,96,768]{2,1,0:T(8,128)(2,1)S(1)} %slice.274), channel_id=1, source_target_pairs={{0,2},{1,3},{2,0},{3,1},{4,6},{5,7},{6,4},{7,5},{8,10},{9,11},{10,... | collective-permute-start | bytes 1769480 | tf_op jit(solution)/shard_map/ppermute | solution.py:33
  95.8 37.5 %collective-permute-start.9 = (bf16[4,96,768]{2,1,0:T(8,128)(2,1)S(1)}, bf16[4,96,768]{2,1,0:T(8,128)(2,1)}, u32[]{:S(2)}, u32[]{:S(2)}) collective-permute-start(bf16[4,96,768]{2,1,0:T(8,128)(2,1)S(1)} %slice.274), channel_id=1, source_target_pairs={{0,3},{1,2},{2,1},{3,0},{4,7},{5,6},{6,5},{7,4},{8,11},{9,10},{10,... | collective-permute-start | bytes 1769480 | tf_op jit(solution)/shard_map/ppermute | solution.py:33
  137.0 53.6 %collective-permute-start.10 = (bf16[4,4,96,768]{3,2,1,0:T(8,128)(2,1)}, bf16[4,4,96,768]{3,2,1,0:T(8,128)(2,1)}, u32[]{:S(2)}, u32[]{:S(2)}) collective-permute-start(bf16[4,4,96,768]{3,2,1,0:T(8,128)(2,1)} %pad_maximum_fusion.1), channel_id=1, source_target_pairs={{0,4},{4,0},{8,12},{12,8},{16,20},{20,16},{24,28},{28,24},{1,5},{5... | collective-permute-start | bytes 7077896 | tf_op jit(solution)/shard_map/ppermute | solution.py:37
  139.2 47.6 %all-to-all-start = ((bf16[8,512,96]{1,2,0:T(8,128)(2,1)}), bf16[8,512,96]{1,2,0:T(8,128)(2,1)S(1)}, u32[]{:S(2)}, u32[]{:S(2)}) async-start(bf16[8,512,96]{1,2,0:T(8,128)(2,1)} %copy.301), calls=%async_computation | async-start | bytes 1572864 | tf_op jit(solution)/shard_map/all_to_all | solution.py:455
  144.3 363.0 %reduce-scatter.4.cloned.1.call-start = ((), (), s32[]{:S(2)}) async-start(), calls=%async_computation.8 | async-start | bytes 13934592 | tf_op jit(solution)/shard_map/reduce_scatter | solution.py:537
  223.0 16.6 %collective-permute-start.11 = (bf16[384,768]{1,0:T(8,128)(2,1)}, bf16[384,768]{1,0:T(8,128)(2,1)}, u32[]{:S(2)}, u32[]{:S(2)}) collective-permute-start(bf16[384,768]{1,0:T(8,128)(2,1)} %get-tuple-element.191), channel_id=1, source_target_pairs={{0,1},{1,0},{2,3},{3,2},{4,5},{5,4},{6,7},{7,6},{8,9},{9,8},{10,11... | collective-permute-start | bytes 1769480 | tf_op jit(solution)/shard_map/ppermute | solution.py:33
  224.6 27.5 %collective-permute-start.12 = (bf16[384,768]{1,0:T(8,128)(2,1)}, bf16[384,768]{1,0:T(8,128)(2,1)}, u32[]{:S(2)}, u32[]{:S(2)}) collective-permute-start(bf16[384,768]{1,0:T(8,128)(2,1)} %get-tuple-element.190), channel_id=1, source_target_pairs={{0,2},{1,3},{2,0},{3,1},{4,6},{5,7},{6,4},{7,5},{8,10},{9,11},{10,... | collective-permute-start | bytes 1769480 | tf_op jit(solution)/shard_map/ppermute | solution.py:33
  226.1 25.9 %collective-permute-start.13 = (bf16[384,768]{1,0:T(8,128)(2,1)S(1)}, bf16[384,768]{1,0:T(8,128)(2,1)}, u32[]{:S(2)}, u32[]{:S(2)}) collective-permute-start(bf16[384,768]{1,0:T(8,128)(2,1)S(1)} %get-tuple-element.189), channel_id=1, source_target_pairs={{0,3},{1,2},{2,1},{3,0},{4,7},{5,6},{6,5},{7,4},{8,11},{9,10},{10,... | collective-permute-start | bytes 1769480 | tf_op jit(solution)/shard_map/ppermute | solution.py:33
  287.6 16.5 %collective-permute-start.14 = (bf16[384,768]{1,0:T(8,128)(2,1)}, bf16[384,768]{1,0:T(8,128)(2,1)S(1)}, u32[]{:S(2)}, u32[]{:S(2)}) collective-permute-start(bf16[384,768]{1,0:T(8,128)(2,1)} %bitcast.45), channel_id=1, source_target_pairs={{0,1},{1,0},{2,3},{3,2},{4,5},{5,4},{6,7},{7,6},{8,9},{9,8},{10,11... | collective-permute-start | bytes 1769480 | tf_op jit(solution)/shard_map/ppermute | solution.py:33
  288.8 26.4 %collective-permute-start.15 = (bf16[384,768]{1,0:T(8,128)(2,1)}, bf16[384,768]{1,0:T(8,128)(2,1)}, u32[]{:S(2)}, u32[]{:S(2)}) collective-permute-start(bf16[384,768]{1,0:T(8,128)(2,1)} %bitcast.47), channel_id=1, source_target_pairs={{0,2},{1,3},{2,0},{3,1},{4,6},{5,7},{6,4},{7,5},{8,10},{9,11},{10,... | collective-permute-start | bytes 1769480 | tf_op jit(solution)/shard_map/ppermute | solution.py:33
  289.6 25.6 %collective-permute-start.16 = (bf16[384,768]{1,0:T(8,128)(2,1)S(1)}, bf16[384,768]{1,0:T(8,128)(2,1)}, u32[]{:S(2)}, u32[]{:S(2)}) collective-permute-start(bf16[384,768]{1,0:T(8,128)(2,1)S(1)} %bitcast.316), channel_id=1, source_target_pairs={{0,3},{1,2},{2,1},{3,0},{4,7},{5,6},{6,5},{7,4},{8,11},{9,10},{10,... | collective-permute-start | bytes 1769480 | tf_op jit(solution)/shard_map/ppermute | solution.py:33
  376.4 253.7 %reduce-scatter.6.cloned.1.call-start = ((), (), s32[]{:S(2)}) async-start(), calls=%async_computation.9 | async-start | bytes 10616832 | tf_op jit(solution)/shard_map/reduce_scatter | solution.py:587
  392.0 6.5 collective-permute-start.17
  393.4 8.1 %collective-permute-start.18 = (f32[64,768]{1,0:T(8,128)}, f32[64,768]{1,0:T(8,128)}, u32[]{:S(2)}, u32[]{:S(2)}) collective-permute-start(f32[64,768]{1,0:T(8,128)} %get-tuple-element.202), channel_id=1, source_target_pairs={{0,2},{1,3},{2,0},{3,1},{4,6},{5,7},{6,4},{7,5},{8,10},{9,11},{10,... | collective-permute-start | bytes 589832 | tf_op jit(solution)/shard_map/ppermute | solution.py:33
  393.6 8.0 %collective-permute-start.19 = (f32[64,768]{1,0:T(8,128)}, f32[64,768]{1,0:T(8,128)}, u32[]{:S(2)}, u32[]{:S(2)}) collective-permute-start(f32[64,768]{1,0:T(8,128)} %get-tuple-element.201), channel_id=1, source_target_pairs={{0,3},{1,2},{2,1},{3,0},{4,7},{5,6},{6,5},{7,4},{8,11},{9,10},{10,... | collective-permute-start | bytes 589832 | tf_op jit(solution)/shard_map/ppermute | solution.py:33
  408.2 16.3 %collective-permute-start.20 = (bf16[384,768]{1,0:T(8,128)(2,1)S(1)}, bf16[384,768]{1,0:T(8,128)(2,1)S(1)}, u32[]{:S(2)}, u32[]{:S(2)}) collective-permute-start(bf16[384,768]{1,0:T(8,128)(2,1)S(1)} %get-tuple-element.183), channel_id=1, source_target_pairs={{0,1},{1,0},{2,3},{3,2},{4,5},{5,4},{6,7},{7,6},{8,9},{9,8},{10,11... | collective-permute-start | bytes 1769480 | tf_op jit(solution)/shard_map/ppermute | solution.py:33
  409.3 23.9 %collective-permute-start.21 = (bf16[384,768]{1,0:T(8,128)(2,1)S(1)}, bf16[384,768]{1,0:T(8,128)(2,1)S(1)}, u32[]{:S(2)}, u32[]{:S(2)}) collective-permute-start(bf16[384,768]{1,0:T(8,128)(2,1)S(1)} %get-tuple-element.182), channel_id=1, source_target_pairs={{0,2},{1,3},{2,0},{3,1},{4,6},{5,7},{6,4},{7,5},{8,10},{9,11},{10,... | collective-permute-start | bytes 1769480 | tf_op jit(solution)/shard_map/ppermute | solution.py:33
  410.3 22.9 %collective-permute-start.22 = (bf16[384,768]{1,0:T(8,128)(2,1)S(1)}, bf16[384,768]{1,0:T(8,128)(2,1)S(1)}, u32[]{:S(2)}, u32[]{:S(2)}) collective-permute-start(bf16[384,768]{1,0:T(8,128)(2,1)S(1)} %get-tuple-element.181), channel_id=1, source_target_pairs={{0,3},{1,2},{2,1},{3,0},{4,7},{5,6},{6,5},{7,4},{8,11},{9,10},{10,... | collective-permute-start | bytes 1769480 | tf_op jit(solution)/shard_map/ppermute | solution.py:33
  470.1 34.1 %collective-permute-start.23 = (bf16[384,768]{1,0:T(8,128)(2,1)}, bf16[384,768]{1,0:T(8,128)(2,1)}, u32[]{:S(2)}, u32[]{:S(2)}) collective-permute-start(bf16[384,768]{1,0:T(8,128)(2,1)} %bitcast.70), channel_id=1, source_target_pairs={{0,1},{1,0},{2,3},{3,2},{4,5},{5,4},{6,7},{7,6},{8,9},{9,8},{10,11... | collective-permute-start | bytes 1769480 | tf_op jit(solution)/shard_map/ppermute | solution.py:33
  470.9 33.4 %collective-permute-start.24 = (bf16[384,768]{1,0:T(8,128)(2,1)}, bf16[384,768]{1,0:T(8,128)(2,1)}, u32[]{:S(2)}, u32[]{:S(2)}) collective-permute-start(bf16[384,768]{1,0:T(8,128)(2,1)} %bitcast.72), channel_id=1, source_target_pairs={{0,2},{1,3},{2,0},{3,1},{4,6},{5,7},{6,4},{7,5},{8,10},{9,11},{10,... | collective-permute-start | bytes 1769480 | tf_op jit(solution)/shard_map/ppermute | solution.py:33
  472.0 32.2 %collective-permute-start.25 = (bf16[384,768]{1,0:T(8,128)(2,1)S(1)}, bf16[384,768]{1,0:T(8,128)(2,1)}, u32[]{:S(2)}, u32[]{:S(2)}) collective-permute-start(bf16[384,768]{1,0:T(8,128)(2,1)S(1)} %bitcast.318), channel_id=1, source_target_pairs={{0,3},{1,2},{2,1},{3,0},{4,7},{5,6},{6,5},{7,4},{8,11},{9,10},{10,... | collective-permute-start | bytes 1769480 | tf_op jit(solution)/shard_map/ppermute | solution.py:33
  507.4 225.6 %reduce-scatter.8.cloned.1.call-start = ((), (), s32[]{:S(2)}) async-start(), calls=%async_computation.10 | async-start | bytes 10616832 | tf_op jit(solution)/shard_map/reduce_scatter | solution.py:588
  568.4 41.2 %collective-permute-start.26 = (bf16[4,4,96,768]{3,2,1,0:T(8,128)(2,1)}, bf16[4,4,96,768]{3,2,1,0:T(8,128)(2,1)}, u32[]{:S(2)}, u32[]{:S(2)}) collective-permute-start(bf16[4,4,96,768]{3,2,1,0:T(8,128)(2,1)} %dynamic-slice_bitcast_fusion), channel_id=1, source_target_pairs={{0,4},{4,0},{8,12},{12,8},{16,20},{20,16},{24,28},{28,24},{1,5},{5... | collective-permute-start | bytes 7077896 | tf_op jit(solution)/shard_map/ppermute | solution.py:37
  570.9 37.7 %all-to-all-start.1 = ((bf16[512,8,96]{0,2,1:T(8,128)(2,1)}), bf16[512,8,96]{0,2,1:T(8,128)(2,1)S(1)}, u32[]{:S(2)}, u32[]{:S(2)}) async-start(bf16[512,8,96]{0,2,1:T(8,128)(2,1)} %bitcast.99), calls=%async_computation.2 | async-start | bytes 1572864 | tf_op jit(solution)/shard_map/all_to_all | solution.py:619
  578.1 1.4 collective-permute-start.27
  608.7 20.5 %collective-permute-start.31 = (bf16[96,4096]{1,0:T(8,128)(2,1)S(1)}, bf16[96,4096]{1,0:T(8,128)(2,1)S(1)}, u32[]{:S(2)}, u32[]{:S(2)}) collective-permute-start(bf16[96,4096]{1,0:T(8,128)(2,1)S(1)} %bitcast.291), channel_id=1, source_target_pairs={{0,1},{1,0},{2,3},{3,2},{4,5},{5,4},{6,7},{7,6},{8,9},{9,8},{10,11... | collective-permute-start | bytes 2359304 | tf_op jit(solution)/shard_map/ppermute | solution.py:33
  614.3 39.3 %collective-permute-start.28 = (bf16[4,102,768]{2,0,1:T(4,128)(2,1)}, bf16[4,102,768]{2,0,1:T(4,128)(2,1)S(1)}, u32[]{:S(2)}, u32[]{:S(2)}) collective-permute-start(bf16[4,102,768]{2,0,1:T(4,128)(2,1)} %copy.333), channel_id=1, source_target_pairs={{0,1},{1,0},{2,3},{3,2},{4,5},{5,4},{6,7},{7,6},{8,9},{9,8},{10,11... | collective-permute-start | bytes 1880072 | tf_op jit(solution)/shard_map/ppermute | solution.py:33
  616.5 37.1 %collective-permute-start.29 = (bf16[4,102,768]{2,0,1:T(4,128)(2,1)}, bf16[4,102,768]{2,0,1:T(4,128)(2,1)S(1)}, u32[]{:S(2)}, u32[]{:S(2)}) collective-permute-start(bf16[4,102,768]{2,0,1:T(4,128)(2,1)} %copy.337), channel_id=1, source_target_pairs={{0,2},{1,3},{2,0},{3,1},{4,6},{5,7},{6,4},{7,5},{8,10},{9,11},{10,... | collective-permute-start | bytes 1880072 | tf_op jit(solution)/shard_map/ppermute | solution.py:33
  618.4 38.2 %collective-permute-start.30 = (bf16[4,102,768]{2,0,1:T(4,128)(2,1)}, bf16[4,102,768]{2,0,1:T(4,128)(2,1)}, u32[]{:S(2)}, u32[]{:S(2)}) collective-permute-start(bf16[4,102,768]{2,0,1:T(4,128)(2,1)} %copy.341), channel_id=1, source_target_pairs={{0,3},{1,2},{2,1},{3,0},{4,7},{5,6},{6,5},{7,4},{8,11},{9,10},{10,... | collective-permute-start | bytes 1880072 | tf_op jit(solution)/shard_map/ppermute | solution.py:33
  621.1 63.4 %collective-permute-start.35 = (bf16[96,4096]{1,0:T(8,128)(2,1)S(1)}, bf16[96,4096]{1,0:T(8,128)(2,1)}, u32[]{:S(2)}, u32[]{:S(2)}) collective-permute-start(bf16[96,4096]{1,0:T(8,128)(2,1)S(1)} %bitcast.292), channel_id=1, source_target_pairs={{0,3},{1,2},{2,1},{3,0},{4,7},{5,6},{6,5},{7,4},{8,11},{9,10},{10,... | collective-permute-start | bytes 2359304 | tf_op jit(solution)/shard_map/ppermute | solution.py:33
  629.2 59.2 %collective-permute-start.39 = (bf16[96,4096]{1,0:T(8,128)(2,1)S(1)}, bf16[96,4096]{1,0:T(8,128)(2,1)}, u32[]{:S(2)}, u32[]{:S(2)}) collective-permute-start(bf16[96,4096]{1,0:T(8,128)(2,1)S(1)} %bitcast.293), channel_id=1, source_target_pairs={{0,2},{1,3},{2,0},{3,1},{4,6},{5,7},{6,4},{7,5},{8,10},{9,11},{10,... | collective-permute-start | bytes 2359304 | tf_op jit(solution)/shard_map/ppermute | solution.py:33
  661.7 12.6 %collective-permute-start.32 = (bf16[1,102,768]{2,1,0:T(8,128)(2,1)S(1)}, bf16[1,102,768]{2,1,0:T(8,128)(2,1)S(1)}, u32[]{:S(2)}, u32[]{:S(2)}) collective-permute-start(bf16[1,102,768]{2,1,0:T(8,128)(2,1)S(1)} %get-tuple-element.203), channel_id=1, source_target_pairs={{0,8},{4,12},{8,0},{12,4},{16,24},{20,28},{24,16},{28,20},{1,9},{5... | collective-permute-start | bytes 470024 | tf_op jit(solution)/shard_map/ppermute | solution.py:37
  661.8 18.3 %collective-permute-start.33 = (bf16[1,102,768]{2,1,0:T(8,128)(2,1)S(1)}, bf16[1,102,768]{2,1,0:T(8,128)(2,1)S(1)}, u32[]{:S(2)}, u32[]{:S(2)}) collective-permute-start(bf16[1,102,768]{2,1,0:T(8,128)(2,1)S(1)} %get-tuple-element.205), channel_id=1, source_target_pairs={{0,16},{4,20},{8,24},{12,28},{16,0},{20,4},{24,8},{28,12},{1,17},{... | collective-permute-start | bytes 470024 | tf_op jit(solution)/shard_map/ppermute | solution.py:37
  663.6 20.9 %collective-permute-start.34 = (bf16[1,102,768]{2,1,0:T(8,128)(2,1)S(1)}, bf16[1,102,768]{2,1,0:T(8,128)(2,1)S(1)}, u32[]{:S(2)}, u32[]{:S(2)}) collective-permute-start(bf16[1,102,768]{2,1,0:T(8,128)(2,1)S(1)} %get-tuple-element.204), channel_id=1, source_target_pairs={{0,24},{4,28},{8,16},{12,20},{16,8},{20,12},{24,0},{28,4},{1,25},{... | collective-permute-start | bytes 470024 | tf_op jit(solution)/shard_map/ppermute | solution.py:37
  684.6 43.8 %collective-permute-start.36 = (f32[96,768]{1,0:T(8,128)S(1)}, f32[96,768]{1,0:T(8,128)}, u32[]{:S(2)}, u32[]{:S(2)}) collective-permute-start(f32[96,768]{1,0:T(8,128)S(1)} %add_bitcast_fusion), channel_id=1, source_target_pairs={{0,1},{1,0},{2,3},{3,2},{4,5},{5,4},{6,7},{7,6},{8,9},{9,8},{10,11... | collective-permute-start | bytes 884744 | tf_op jit(solution)/shard_map/ppermute | solution.py:33
  685.8 42.6 %collective-permute-start.37 = (f32[96,768]{1,0:T(8,128)S(1)}, f32[96,768]{1,0:T(8,128)}, u32[]{:S(2)}, u32[]{:S(2)}) collective-permute-start(f32[96,768]{1,0:T(8,128)S(1)} %add_bitcast_fusion), channel_id=1, source_target_pairs={{0,2},{1,3},{2,0},{3,1},{4,6},{5,7},{6,4},{7,5},{8,10},{9,11},{10,... | collective-permute-start | bytes 884744 | tf_op jit(solution)/shard_map/ppermute | solution.py:33
  686.7 41.7 %collective-permute-start.38 = (f32[96,768]{1,0:T(8,128)S(1)}, f32[96,768]{1,0:T(8,128)}, u32[]{:S(2)}, u32[]{:S(2)}) collective-permute-start(f32[96,768]{1,0:T(8,128)S(1)} %add_bitcast_fusion), channel_id=1, source_target_pairs={{0,3},{1,2},{2,1},{3,0},{4,7},{5,6},{6,5},{7,4},{8,11},{9,10},{10,... | collective-permute-start | bytes 884744 | tf_op jit(solution)/shard_map/ppermute | solution.py:33
  (97 other events, 1023.4 us)
Sparse Core Ops, SparseCore 0:
  10.2 106.9 all-gather.5
  119.4 105.7 all-gather.7
  227.3 113.4 all-gather.9
  376.5 124.6 reduce-scatter.3
  507.5 110.0 reduce-scatter.5
  619.8 111.5 reduce-scatter.7

commit v5 on v4

--- a/solution.py
+++ b/solution.py
@@ -303,17 +303,24 @@
     return counts, rows, origin
 
 
-def add_rows(local_ids, grads, vocab_rows, start):
+def takes_kernel(pieces, piece, width):
+    return piece * pieces * 2 <= GRID_ROWS and width <= LANES and piece % LANES == 0
+
+
+def all_lists(local_ids, vocab_rows):
+    lists = [row_lists(ids, vocab_rows, k * ids.shape[0]) for k, ids in enumerate(local_ids)]
+    return tuple(jnp.concatenate(parts, axis=0) for parts in zip(*lists))
+
+
+def add_rows(local_ids, lists, grads, vocab_rows, start):
     width, piece = grads[0].shape
-    if piece * len(grads) * 2 > GRID_ROWS or width > LANES or piece % LANES:
+    if not takes_kernel(len(grads), piece, width):
         vocab_iota = jnp.arange(vocab_rows, dtype=jnp.int32)
         total = jnp.zeros((width, vocab_rows), jnp.float32) if start is None else start
         for ids, part in zip(local_ids, grads):
             hits = (ids[:, None] == vocab_iota[None, :]).astype(jnp.bfloat16)
             total = total + jnp.dot(part, hits, preferred_element_type=jnp.float32)
         return total
-    lists = [row_lists(ids, vocab_rows, k * piece) for k, ids in enumerate(local_ids)]
-    lists = [jnp.concatenate(parts, axis=0) for parts in zip(*lists)]
     smem = pl.BlockSpec(memory_space=pltpu.SMEM)
     vmem = pl.BlockSpec(memory_space=pltpu.VMEM)
     padded_rows = -(-(vocab_rows + 1) // LANES) * LANES
@@ -455,6 +462,21 @@
     stream = lax.all_to_all(
         stream_parts, "dp", split_axis=0, concat_axis=1, tiled=True
     ).astype(jnp.float32)
+    token_rows = [
+        lax.dynamic_index_in_dim(
+            all_ids, partner_of(my_index, k, members), 1, keepdims=False
+        ).reshape(-1)
+        - my_index * vocab_rows
+        for k in range(members)
+    ]
+    half = members // 2
+    early_lists = late_lists = None
+    if takes_kernel(half, replicas * local_rows, share):
+        early_lists = all_lists(token_rows[:half], vocab_rows)
+        late_lists = all_lists(token_rows[half:], vocab_rows)
+        stream, early_lists, late_lists = lax.optimization_barrier(
+            (stream, early_lists, late_lists)
+        )
     normal_one, factor_one = normal_parts(stream)
     attn_in = (normal_one * gain_rows[0]).astype(jnp.bfloat16)
     projected = jnp.einsum(
@@ -661,13 +683,6 @@
         )
         for k in range(members)
     ]
-    token_rows = [
-        lax.dynamic_index_in_dim(
-            all_ids, partner_of(my_index, k, members), 1, keepdims=False
-        ).reshape(-1)
-        - my_index * vocab_rows
-        for k in range(members)
-    ]
     column_grads[1], out_sum = lax.optimization_barrier((column_grads[1], out_sum))
     third_out = nesterov_update(
         expert_out,
@@ -676,8 +691,7 @@
         out_sum.astype(jnp.float32),
         RATE_TABLE[2] * loss_count**0.5,
     )
-    half = members // 2
-    stream_sum = add_rows(token_rows[:half], column_grads[:half], vocab_rows, None)
+    stream_sum = add_rows(token_rows[:half], early_lists, column_grads[:half], vocab_rows, None)
     received, stream_sum = lax.optimization_barrier((received, stream_sum))
     dense_sum = sum(part[:, :chunk].astype(jnp.float32) for part in received)
     small_sum = sum(joined(part[:, chunk:]) for part in received)
@@ -692,7 +706,7 @@
     column_grads[-1], third_out, summed = lax.optimization_barrier(
         (column_grads[-1], third_out, summed)
     )
-    stream_sum = add_rows(token_rows[half:], column_grads[half:], vocab_rows, stream_sum)
+    stream_sum = add_rows(token_rows[half:], late_lists, column_grads[half:], vocab_rows, stream_sum)
     embed_sum = embed_sum.astype(jnp.float32) + stream_sum.T
     loss_value = small_sum[small_params.size]
     small_sum = small_sum[: small_params.size].reshape(small_params.shape[0], share)

time: 764 us -> 758 us (level)
    reduce_scatter x1, waiting for transfers between devices: 0.01 us -> 10.2 us  [shards(): in_sum = lax.psum_scatter(in_grad, 'dp', scatter_dimension=1, tiled=True)]
    all_gather x1, waiting for transfers between devices: 9.57 us -> 0.01 us  [shards(): lax.all_gather(embedding.astype(jnp.bfloat16), 'dp', axis=1, tiled=True)]
    ppermute x30, waiting for transfers between devices: 103 us -> 94.8 us  [swap(): lax.ppermute(value, 'expert', partner_order(members)[k])]
  transfers between devices with their start and end apart: 48 -> 48, of which waited for: 18 -> 19; matrix products, arithmetic and copies ran while one was open for 42% -> 43% of each run, Pallas kernels for 13% -> 13%
where the time goes in v5:
time: 758 us; the launch traced here: 746 us
  waiting for transfers between devices  189 us (25%)
  matrix products  184 us (24%)
  Pallas kernels  97 us (13%)
  other arithmetic  93.5 us (12%)
  local copies, waits for them, and re-layouts  88.3 us (12%)
  starting transfers between devices  59.3 us (8%)
  blocking collectives  17.9 us (2%)
  between operations  17.3 us (2%)
    ppermute x30, waiting for transfers between devices, swap(): lax.ppermute(value, 'expert', partner_order(members)[k])  94.8 us
    pallas_call x2, Pallas kernels, add_rows(): pl.pallas_call(add_rows_kernel, out_shape=jax.ShapeDtypeStruct(shape, jnp...  51.6 us
    all_to_all x1, waiting for transfers between devices, shards(): lax.all_to_all(stream_parts, 'dp', split_axis=0, concat_axis=1, tiled=True)  39 us
    ppermute x30, starting transfers between devices, swap(): lax.ppermute(value, 'expert', partner_order(members)[k])  37.9 us
    all_to_all x1, waiting for transfers between devices, shards(): lax.all_to_all(stream_grad, 'dp', split_axis=1, concat_axis=0, tiled=True)  29 us
    pallas_call x1, Pallas kernels, attend_back(): pl.pallas_call(functools.partial(attend_back_kernel, scaling), grid=(sequ...  26.6 us
    dot_general x1, matrix products, shards(): jnp.einsum('ecd,efd->ecf', arrived_grad, out_low, preferred_element_type=...  21.5 us
    concatenate x2, local copies, waits for them, and re-layouts, shards(): rows_table = jnp.concatenate(rows_parts, axis=0)  20.5 us
  transfers between devices with their start and end apart: 48, of which 19 were waited for; matrix products, arithmetic and copies ran while one was open for 43% of the time, Pallas kernels for 13%

profile of v5, /device:TPU:0, one launch (start us, length us, event | category | flops | bytes accessed | tf_op | source)
XLA Modules:
  0.0 745.6 jit_solution(6920190440302330745)
XLA Ops:
  19.7 6.0 iota_compare_fusion
  25.7 5.3 select_convert_fusion.2
  31.0 18.4 %fusion = f32[256,63,128]{2,1,0:T(8,128)} fusion(pred[256,65,128]{2,1,0:T(8,128)(4,1)} %iota_compare_fusion, bf16[256,65,63]{1,2,0:T(8,128)(2,1)} %get-tuple-element.225, bf16[256,65,63]{1,2,0:T(8,128)(2,1)} %get-tuple-element.226, bf16[256,65,63]{1,2,0:T(8,128)(2,1)S(1)} %get-tuple-element.224), kind=kOutput, calls=%fused_computation.3 | convolution fusion | flops 836759040 | bytes 16677376 | tf_op jit(solution)/shard_map/pih,pil->phl/dot_general | solution.py:97
  57.8 9.2 %copy.250 = f32[256,63,128]{0,2,1:T(8,128)} copy(f32[256,63,128]{2,1,0:T(8,128)} %fusion) | data formatting | bytes 16515072 | tf_op jit(solution)/shard_map/pih,pil->phl/dot_general | solution.py:97
  67.0 7.1 slice.273
  75.5 10.7 %collective-permute-done.2 = bf16[8000,96]{0,1:T(8,128)(2,1)} collective-permute-done((bf16[8000,96]{0,1:T(8,128)(2,1)}, bf16[8000,96]{0,1:T(8,128)(2,1)}, u32[]{:S(2)}, u32[]{:S(2)}) %collective-permute-start.2) | collective-permute-done | bytes 1536032 | tf_op jit(solution)/shard_map/ppermute | solution.py:33
  90.1 10.6 %concatenate.110 = bf16[32000,96]{0,1:T(8,128)(2,1)} concatenate(bf16[8000,96]{0,1:T(8,128)(2,1)} %convert_element_type.376, bf16[8000,96]{0,1:T(8,128)(2,1)} %collective-permute-done, bf16[8000,96]{0,1:T(8,128)(2,1)} %collective-permute-done.1, bf16[8000,96]{0,1:T(8,128)(2,1)} %collective-permute-done.2), dimensions={0} | concatenate | bytes 12288000 | tf_op jit(solution)/shard_map/concatenate | solution.py:448
  100.7 9.9 %copy.252 = bf16[32000,96]{1,0:T(8,128)(2,1)} copy(bf16[32000,96]{0,1:T(8,128)(2,1)} %concatenate.110) | data formatting | bytes 12288000 | tf_op jit(solution)/shard_map/concatenate | solution.py:448
  115.2 3.3 select_reduce_fusion.1
  118.7 15.4 %gather_fusion = bf16[4096,96]{1,0:T(8,128)(2,1)S(1)} fusion(bf16[32000,96]{1,0:T(8,128)(2,1)} %copy.252, s32[4096]{0:T(1024)S(1)} %broadcast_clamp_fusion), kind=kCustom, calls=%fused_computation | custom fusion | bytes 1589248 | tf_op jit(solution)/shard_map/jit(_take)/gather | solution.py:451
  134.7 4.3 select_reduce_fusion
  139.1 4.3 select_reduce_fusion.5
  150.5 7.6 %all-to-all-start = ((bf16[8,512,96]{1,2,0:T(8,128)(2,1)}), bf16[8,512,96]{1,2,0:T(8,128)(2,1)S(1)}, u32[]{:S(2)}, u32[]{:S(2)}) async-start(bf16[8,512,96]{1,2,0:T(8,128)(2,1)} %copy.253), calls=%async_computation | async-start | bytes 1572864 | tf_op jit(solution)/shard_map/all_to_all | solution.py:462
  161.4 39.0 %all-to-all-done = bf16[8,512,96]{1,2,0:T(8,128)(2,1)S(1)} async-done(((bf16[8,512,96]{1,2,0:T(8,128)(2,1)}), bf16[8,512,96]{1,2,0:T(8,128)(2,1)S(1)}, u32[]{:S(2)}, u32[]{:S(2)}) %all-to-all-start) | async-done | bytes 786464 | tf_op jit(solution)/shard_map/all_to_all | solution.py:462
  205.1 3.5 convert_bitcast_fusion.q_ref.k_ref.v_ref
  208.6 18.8 %shard_map.373 = bf16[512,768]{1,0:T(8,128)(2,1)} custom-call(bf16[3,512,768]{2,1,0:T(8,128)(2,1)} %convert_bitcast_fusion.q_ref.k_ref.v_ref, bf16[3,512,768]{2,1,0:T(8,128)(2,1)} %convert_bitcast_fusion.q_ref.k_ref.v_ref, bf16[3,512,768]{2,1,0:T(8,128)(2,1)} %convert_bitcast_fusion.q_ref.k_ref.v_ref, s32[512,1]{1,0:T(8,128)} %copy.258.row_ref, ...), custom_call_target="tpu_custom_call" | custom-call | flops 3221225472 | bytes 3145728 | tf_op jit(solution)/shard_map/pallas_call | solution.py:190
  240.3 9.3 %collective-permute-done.11 = bf16[384,768]{1,0:T(8,128)(2,1)} collective-permute-done((bf16[384,768]{1,0:T(8,128)(2,1)}, bf16[384,768]{1,0:T(8,128)(2,1)}, u32[]{:S(2)}, u32[]{:S(2)}) %collective-permute-start.11) | collective-permute-done | bytes 589856 | tf_op jit(solution)/shard_map/ppermute | solution.py:33
  249.6 12.7 %collective-permute-done.12 = bf16[384,768]{1,0:T(8,128)(2,1)} collective-permute-done((bf16[384,768]{1,0:T(8,128)(2,1)}, bf16[384,768]{1,0:T(8,128)(2,1)}, u32[]{:S(2)}, u32[]{:S(2)}) %collective-permute-start.12) | collective-permute-done | bytes 589856 | tf_op jit(solution)/shard_map/ppermute | solution.py:33
  265.6 15.4 %fusion.127 = f32[2,768,3072]{2,1,0:T(8,128)} fusion(bf16[2,768,768]{2,1,0:T(8,128)(2,1)} %bitcast.296, bf16[2,768,3072]{2,1,0:T(8,128)(2,1)} %all-gather.6.cloned.1.call-done), kind=kOutput, calls=%fused_computation.392 | convolution fusion | flops 7247757312 | bytes 30670848 | tf_op jit(solution)/shard_map/ecd,edf->ecf/dot_general | solution.py:524
  281.0 15.6 %convolution_convert_fusion.6 = bf16[2,768,768]{2,1,0:T(8,128)(2,1)S(1)} fusion(bf16[2,3072,768]{2,1,0:T(8,128)(2,1)} %all-gather.8.cloned.1.call-done, f32[2,768,3072]{2,1,0:T(8,128)} %fusion.127), kind=kOutput, calls=%fused_computation.96 | convolution fusion | flops 7291404288 | bytes 30670848 | tf_op jit(solution)/shard_map/ecf,efd->ecd/dot_general | solution.py:526
  301.4 12.8 %collective-permute-done.14 = bf16[384,768]{1,0:T(8,128)(2,1)S(1)} collective-permute-done((bf16[384,768]{1,0:T(8,128)(2,1)}, bf16[384,768]{1,0:T(8,128)(2,1)S(1)}, u32[]{:S(2)}, u32[]{:S(2)}) %collective-permute-start.14) | collective-permute-done | bytes 589856 | tf_op jit(solution)/shard_map/ppermute | solution.py:33
  314.3 11.7 %collective-permute-done.15 = bf16[384,768]{1,0:T(8,128)(2,1)} collective-permute-done((bf16[384,768]{1,0:T(8,128)(2,1)}, bf16[384,768]{1,0:T(8,128)(2,1)}, u32[]{:S(2)}, u32[]{:S(2)}) %collective-permute-start.15) | collective-permute-done | bytes 589856 | tf_op jit(solution)/shard_map/ppermute | solution.py:33
  332.4 9.9 %all_gather.20 = bf16[256,768]{1,0:T(8,128)(2,1)} all-gather(bf16[64,768]{1,0:T(8,128)(2,1)S(1)} %convolution_convert_fusion.9), channel_id=1, replica_groups=mesh['dp'=8,'expert'=4] {'expert'}, dimensions={0}, use_global_device_ids=true | all-gather | bytes 491520 | tf_op jit(solution)/shard_map/all_gather | solution.py:538
  342.3 8.5 %fusion.125 = (f32[256]{0:T(256)S(1)}, f32[256,8000]{0,1:T(8,128)S(1)}) fusion(bf16[256,768]{1,0:T(8,128)(2,1)} %all_gather.20, bf16[8000,768]{0,1:T(8,128)(2,1)} %all-gather.10.cloned.1.call-done), kind=kOutput, calls=%fused_computation.390 | convolution fusion | flops 3147775744 | bytes 20874240 | tf_op jit(solution)/shard_map/gd,vd->gv/dot_general | solution.py:539
  350.8 4.6 exponential_reduce_fusion
  355.5 8.0 %all-gather.1 = f32[4,3,256]{2,1,0:T(4,128)S(1)} all-gather(f32[1,3,256]{2,1,0:T(4,128)S(1)} %maximum_bitcast_fusion.4), channel_id=2, replica_groups=mesh['dp'=8,'expert'=4] {'expert'}, dimensions={0}, use_global_device_ids=true | all-gather | bytes 15360 | tf_op jit(solution)/shard_map/all_gather | solution.py:543
  367.3 10.2 %convolution_convert_fusion = bf16[8000,768]{0,1:T(8,128)(2,1)} fusion(bf16[256,8000]{0,1:T(8,128)(2,1)} %multiply_convert_fusion.1, bf16[256,768]{1,0:T(8,128)(2,1)} %all_gather.20), kind=kOutput, calls=%fused_computation.17 | convolution fusion | flops 3151872000 | bytes 16777216 | tf_op jit(solution)/shard_map/gv,gd->vd/dot_general | solution.py:555
  377.6 13.7 %fusion.128 = f32[256,768]{1,0:T(8,128)S(1)} fusion(bf16[256,8000]{0,1:T(8,128)(2,1)} %multiply_convert_fusion.1, bf16[8000,768]{0,1:T(8,128)(2,1)} %all-gather.10.cloned.1.call-done), kind=kOutput, calls=%fused_computation.393 | convolution fusion | flops 3145728000 | bytes 17170432 | tf_op jit(solution)/shard_map/dot_general | solution.py:560
  411.9 12.8 %collective-permute-done.20 = bf16[384,768]{1,0:T(8,128)(2,1)S(1)} collective-permute-done((bf16[384,768]{1,0:T(8,128)(2,1)S(1)}, bf16[384,768]{1,0:T(8,128)(2,1)S(1)}, u32[]{:S(2)}, u32[]{:S(2)}) %collective-permute-start.20) | collective-permute-done | bytes 589856 | tf_op jit(solution)/shard_map/ppermute | solution.py:33
  424.6 8.2 %collective-permute-done.21 = bf16[384,768]{1,0:T(8,128)(2,1)S(1)} collective-permute-done((bf16[384,768]{1,0:T(8,128)(2,1)S(1)}, bf16[384,768]{1,0:T(8,128)(2,1)S(1)}, u32[]{:S(2)}, u32[]{:S(2)}) %collective-permute-start.21) | collective-permute-done | bytes 589856 | tf_op jit(solution)/shard_map/ppermute | solution.py:33
  434.1 21.5 %fusion.12 = bf16[2,768,3072]{2,1,0:T(8,128)(2,1)} fusion(f32[2,768,3072]{2,1,0:T(8,128)} %fusion.127, bf16[2,768,768]{2,1,0:T(8,128)(2,1)S(1)} %bitcast.299, bf16[2,3072,768]{2,1,0:T(8,128)(2,1)S(1)} %bitcast.366), kind=kOutput, calls=%fused_computation.15 | convolution fusion | flops 7342129152 | bytes 40108032 | tf_op jit(solution)/shard_map/ecd,efd->ecf/dot_general | solution.py:598
  455.7 13.0 %convolution_convert_fusion.5 = bf16[2,768,768]{2,1,0:T(8,128)(2,1)S(1)} fusion(bf16[2,768,3072]{2,1,0:T(8,128)(2,1)} %fusion.12, bf16[2,768,3072]{2,1,0:T(8,128)(2,1)} %all-gather.6.cloned.1.call-done), kind=kOutput, calls=%fused_computation.95 | convolution fusion | flops 7248936960 | bytes 21233664 | tf_op jit(solution)/shard_map/ecf,edf->ecd/dot_general | solution.py:604
  473.3 13.6 %convolution_convert_fusion.1 = bf16[2,768,3072]{2,1,0:T(8,128)(2,1)} fusion(bf16[2,768,768]{2,1,0:T(8,128)(2,1)S(1)} %bitcast.297, bf16[2,768,3072]{2,1,0:T(8,128)(2,1)} %fusion.12), kind=kOutput, calls=%fused_computation.31 | convolution fusion | flops 7252475904 | bytes 21233664 | tf_op jit(solution)/shard_map/ecd,ecf->edf/dot_general | solution.py:603
  486.9 16.9 %convolution_convert_fusion.2 = bf16[2,3072,768]{2,1,0:T(8,128)(2,1)} fusion(bf16[2,768,768]{2,1,0:T(8,128)(2,1)S(1)} %bitcast.300, f32[2,768,3072]{2,1,0:T(8,128)} %fusion.127), kind=kOutput, calls=%fused_computation.32 | convolution fusion | flops 7294943232 | bytes 30670848 | tf_op jit(solution)/shard_map/ecf,ecd->efd/dot_general | solution.py:595
  507.8 3.5 fusion.35
  516.0 26.6 %shard_map.374 = f32[3,512,768]{2,1,0:T(8,128)} custom-call(bf16[3,512,768]{2,1,0:T(8,128)(2,1)} %convert_bitcast_fusion.q_ref.k_ref.v_ref, bf16[3,512,768]{2,1,0:T(8,128)(2,1)} %convert_bitcast_fusion.q_ref.k_ref.v_ref, bf16[3,512,768]{2,1,0:T(8,128)(2,1)} %convert_bitcast_fusion.q_ref.k_ref.v_ref, bf16[512,768]{1,0:T(8,128)(2,1)} %convolution_convert_fusion.8.grad_ref, ...), custom_call_target="tpu_custom_call" | custom-call | flops 8053063680 | bytes 7864320 | tf_op jit(solution)/shard_map/pallas_call | solution.py:270
  542.6 5.8 multiply_reduce_fusion.3
  558.1 3.8 all-to-all-start.1
  566.9 29.0 %all-to-all-done.1 = bf16[512,8,96]{0,2,1:T(8,128)(2,1)S(1)} async-done(((bf16[512,8,96]{0,2,1:T(8,128)(2,1)}), bf16[512,8,96]{0,2,1:T(8,128)(2,1)S(1)}, u32[]{:S(2)}, u32[]{:S(2)}) %all-to-all-start.1) | async-done | bytes 786464 | tf_op jit(solution)/shard_map/all_to_all | solution.py:641
  609.1 7.3 collective-permute-done.31.refs_1_
  617.9 22.9 %shard_map.375.refs_2_ = f32[8064,128]{1,0:T(8,128)} custom-call(s32[64]{0:T(128)} %pad_add_fusion.5.count_ref, s32[64,128]{1,0:T(8,128)} %pad_add_fusion.1.row_ref, s32[64,128]{1,0:T(8,128)} %pad_add_fusion.2.source_ref, bf16[96,4096]{1,0:T(8,128)(2,1)} %bitcast.290, bf16[96,4096]{1,0:T(8,128)(2,1)} %copy-done.38), custom_call_target="tpu_custom_call" | custom-call | flops 8388608 | bytes 231735296 | tf_op jit(solution)/shard_map/pallas_call | solution.py:329
  640.8 3.6 collective-permute-done.30
  658.6 5.1 collective-permute-done.32
  667.0 5.8 collective-permute-done.34
  677.6 28.7 %shard_map.376 = f32[96,8064]{1,0:T(8,128)} custom-call(s32[64]{0:T(128)} %pad_add_fusion.6.count_ref, s32[64,128]{1,0:T(8,128)} %pad_add_fusion.3.row_ref, s32[64,128]{1,0:T(8,128)} %pad_add_fusion.4.source_ref, bf16[96,4096]{1,0:T(8,128)(2,1)} %collective-permute-done.39.refs_0_, bf16[96,4096]{1,0:T(8,128)(2,1)} %collective-permute-done.35.refs_1_, ...), custom_call_target="tpu_custom_call" | custom-call | flops 8388608 | bytes 231735296 | tf_op jit(solution)/shard_map/pallas_call | solution.py:329
  706.3 6.0 fusion.113
  721.3 10.2 %reduce-scatter.8.cloned.1.call-done = bf16[2,96,3072]{2,1,0:T(8,128)(2,1)} async-done(((bf16[2,768,3072]{2,1,0:T(8,128)(2,1)}), bf16[2,96,3072]{2,1,0:T(8,128)(2,1)}) %reduce-scatter.8.cloned.1.call-update) | async-done | bytes 1179664 | tf_op jit(solution)/shard_map/reduce_scatter | solution.py:610
  731.5 4.6 fusion.110
  (520 shorter events, 173.7 us)
Async XLA Ops:
  7.2 258.4 %all-gather.6.cloned.1.call-start = ((), (), s32[]{:S(2)}) async-start(), calls=%async_computation.5 | async-start | bytes 10616832 | tf_op jit(solution)/shard_map/all_gather | solution.py:401
  10.1 270.9 %all-gather.8.cloned.1.call-start = ((), (), s32[]{:S(2)}) async-start(), calls=%async_computation.6 | async-start | bytes 10616832 | tf_op jit(solution)/shard_map/all_gather | solution.py:402
  13.2 329.1 %all-gather.10.cloned.1.call-start = ((), (), s32[]{:S(2)}) async-start(), calls=%async_computation.7 | async-start | bytes 13934592 | tf_op jit(solution)/shard_map/all_gather | solution.py:403
  14.5 37.9 %collective-permute-start = (bf16[8000,96]{0,1:T(8,128)(2,1)}, bf16[8000,96]{0,1:T(8,128)(2,1)}, u32[]{:S(2)}, u32[]{:S(2)}) collective-permute-start(bf16[8000,96]{0,1:T(8,128)(2,1)} %convert_element_type.376), channel_id=1, source_target_pairs={{0,1},{1,0},{2,3},{3,2},{4,5},{5,4},{6,7},{7,6},{8,9},{9,8},{10,11... | collective-permute-start | bytes 4608008 | tf_op jit(solution)/shard_map/ppermute | solution.py:33
  17.5 68.7 %collective-permute-start.2 = (bf16[8000,96]{0,1:T(8,128)(2,1)}, bf16[8000,96]{0,1:T(8,128)(2,1)}, u32[]{:S(2)}, u32[]{:S(2)}) collective-permute-start(bf16[8000,96]{0,1:T(8,128)(2,1)} %convert_element_type.376), channel_id=1, source_target_pairs={{0,3},{1,2},{2,1},{3,0},{4,7},{5,6},{6,5},{7,4},{8,11},{9,10},{10,... | collective-permute-start | bytes 4608008 | tf_op jit(solution)/shard_map/ppermute | solution.py:33
  19.0 71.1 %collective-permute-start.1 = (bf16[8000,96]{0,1:T(8,128)(2,1)}, bf16[8000,96]{0,1:T(8,128)(2,1)}, u32[]{:S(2)}, u32[]{:S(2)}) collective-permute-start(bf16[8000,96]{0,1:T(8,128)(2,1)} %convert_element_type.376), channel_id=1, source_target_pairs={{0,2},{1,3},{2,0},{3,1},{4,6},{5,7},{6,4},{7,5},{8,10},{9,11},{10,... | collective-permute-start | bytes 4608008 | tf_op jit(solution)/shard_map/ppermute | solution.py:33
  52.5 33.7 %collective-permute-start.3 = (bf16[104,768]{1,0:T(8,128)(2,1)S(1)}, bf16[104,768]{1,0:T(8,128)(2,1)S(1)}, u32[]{:S(2)}, u32[]{:S(2)}) collective-permute-start(bf16[104,768]{1,0:T(8,128)(2,1)S(1)} %pad_maximum_fusion.22), channel_id=1, source_target_pairs={{0,8},{4,12},{8,0},{12,4},{16,24},{20,28},{24,16},{28,20},{1,9},{5... | collective-permute-start | bytes 479240 | tf_op jit(solution)/shard_map/ppermute | solution.py:37
  54.6 31.5 %collective-permute-start.4 = (bf16[104,768]{1,0:T(8,128)(2,1)S(1)}, bf16[104,768]{1,0:T(8,128)(2,1)S(1)}, u32[]{:S(2)}, u32[]{:S(2)}) collective-permute-start(bf16[104,768]{1,0:T(8,128)(2,1)S(1)} %pad_maximum_fusion.22), channel_id=1, source_target_pairs={{0,16},{4,20},{8,24},{12,28},{16,0},{20,4},{24,8},{28,12},{1,17},{... | collective-permute-start | bytes 479240 | tf_op jit(solution)/shard_map/ppermute | solution.py:37
  57.2 28.9 %collective-permute-start.5 = (bf16[104,768]{1,0:T(8,128)(2,1)S(1)}, bf16[104,768]{1,0:T(8,128)(2,1)S(1)}, u32[]{:S(2)}, u32[]{:S(2)}) collective-permute-start(bf16[104,768]{1,0:T(8,128)(2,1)S(1)} %pad_maximum_fusion.22), channel_id=1, source_target_pairs={{0,24},{4,28},{8,16},{12,20},{16,8},{20,12},{24,0},{28,4},{1,25},{... | collective-permute-start | bytes 479240 | tf_op jit(solution)/shard_map/ppermute | solution.py:37
  86.3 24.3 %collective-permute-start.6 = (bf16[4,8,768]{2,1,0:T(8,128)(2,1)S(1)}, bf16[4,8,768]{2,1,0:T(8,128)(2,1)S(1)}, u32[]{:S(2)}, u32[]{:S(2)}) collective-permute-start(bf16[4,8,768]{2,1,0:T(8,128)(2,1)S(1)} %pad_maximum_fusion.24), channel_id=1, source_target_pairs={{0,4},{4,0},{8,12},{12,8},{16,20},{20,16},{24,28},{28,24},{1,5},{5... | collective-permute-start | bytes 147464 | tf_op jit(solution)/shard_map/ppermute | solution.py:37
  86.5 56.9 %collective-permute-start.7 = (bf16[4,96,768]{2,1,0:T(8,128)(2,1)S(1)}, bf16[4,96,768]{2,1,0:T(8,128)(2,1)S(1)}, u32[]{:S(2)}, u32[]{:S(2)}) collective-permute-start(bf16[4,96,768]{2,1,0:T(8,128)(2,1)S(1)} %slice.274), channel_id=1, source_target_pairs={{0,1},{1,0},{2,3},{3,2},{4,5},{5,4},{6,7},{7,6},{8,9},{9,8},{10,11... | collective-permute-start | bytes 1769480 | tf_op jit(solution)/shard_map/ppermute | solution.py:33
  88.1 55.3 %collective-permute-start.8 = (bf16[4,96,768]{2,1,0:T(8,128)(2,1)S(1)}, bf16[4,96,768]{2,1,0:T(8,128)(2,1)S(1)}, u32[]{:S(2)}, u32[]{:S(2)}) collective-permute-start(bf16[4,96,768]{2,1,0:T(8,128)(2,1)S(1)} %slice.274), channel_id=1, source_target_pairs={{0,2},{1,3},{2,0},{3,1},{4,6},{5,7},{6,4},{7,5},{8,10},{9,11},{10,... | collective-permute-start | bytes 1769480 | tf_op jit(solution)/shard_map/ppermute | solution.py:33
  88.6 54.8 %collective-permute-start.9 = (bf16[4,96,768]{2,1,0:T(8,128)(2,1)S(1)}, bf16[4,96,768]{2,1,0:T(8,128)(2,1)S(1)}, u32[]{:S(2)}, u32[]{:S(2)}) collective-permute-start(bf16[4,96,768]{2,1,0:T(8,128)(2,1)S(1)} %slice.274), channel_id=1, source_target_pairs={{0,3},{1,2},{2,1},{3,0},{4,7},{5,6},{6,5},{7,4},{8,11},{9,10},{10,... | collective-permute-start | bytes 1769480 | tf_op jit(solution)/shard_map/ppermute | solution.py:33
  146.1 55.2 %collective-permute-start.10 = (bf16[4,4,96,768]{3,2,1,0:T(8,128)(2,1)}, bf16[4,4,96,768]{3,2,1,0:T(8,128)(2,1)}, u32[]{:S(2)}, u32[]{:S(2)}) collective-permute-start(bf16[4,4,96,768]{3,2,1,0:T(8,128)(2,1)} %pad_maximum_fusion.1), channel_id=1, source_target_pairs={{0,4},{4,0},{8,12},{12,8},{16,20},{20,16},{24,28},{28,24},{1,5},{5... | collective-permute-start | bytes 7077896 | tf_op jit(solution)/shard_map/ppermute | solution.py:37
  150.5 49.9 %all-to-all-start = ((bf16[8,512,96]{1,2,0:T(8,128)(2,1)}), bf16[8,512,96]{1,2,0:T(8,128)(2,1)S(1)}, u32[]{:S(2)}, u32[]{:S(2)}) async-start(bf16[8,512,96]{1,2,0:T(8,128)(2,1)} %copy.253), calls=%async_computation | async-start | bytes 1572864 | tf_op jit(solution)/shard_map/all_to_all | solution.py:462
  158.1 348.8 %reduce-scatter.4.cloned.1.call-start = ((), (), s32[]{:S(2)}) async-start(), calls=%async_computation.8 | async-start | bytes 13934592 | tf_op jit(solution)/shard_map/reduce_scatter | solution.py:559
  233.1 16.5 %collective-permute-start.11 = (bf16[384,768]{1,0:T(8,128)(2,1)}, bf16[384,768]{1,0:T(8,128)(2,1)}, u32[]{:S(2)}, u32[]{:S(2)}) collective-permute-start(bf16[384,768]{1,0:T(8,128)(2,1)} %get-tuple-element.205), channel_id=1, source_target_pairs={{0,1},{1,0},{2,3},{3,2},{4,5},{5,4},{6,7},{7,6},{8,9},{9,8},{10,11... | collective-permute-start | bytes 1769480 | tf_op jit(solution)/shard_map/ppermute | solution.py:33
  234.5 27.7 %collective-permute-start.12 = (bf16[384,768]{1,0:T(8,128)(2,1)}, bf16[384,768]{1,0:T(8,128)(2,1)}, u32[]{:S(2)}, u32[]{:S(2)}) collective-permute-start(bf16[384,768]{1,0:T(8,128)(2,1)} %get-tuple-element.204), channel_id=1, source_target_pairs={{0,2},{1,3},{2,0},{3,1},{4,6},{5,7},{6,4},{7,5},{8,10},{9,11},{10,... | collective-permute-start | bytes 1769480 | tf_op jit(solution)/shard_map/ppermute | solution.py:33
  236.0 26.3 %collective-permute-start.13 = (bf16[384,768]{1,0:T(8,128)(2,1)S(1)}, bf16[384,768]{1,0:T(8,128)(2,1)}, u32[]{:S(2)}, u32[]{:S(2)}) collective-permute-start(bf16[384,768]{1,0:T(8,128)(2,1)S(1)} %get-tuple-element.203), channel_id=1, source_target_pairs={{0,3},{1,2},{2,1},{3,0},{4,7},{5,6},{6,5},{7,4},{8,11},{9,10},{10,... | collective-permute-start | bytes 1769480 | tf_op jit(solution)/shard_map/ppermute | solution.py:33
  297.8 16.5 %collective-permute-start.14 = (bf16[384,768]{1,0:T(8,128)(2,1)}, bf16[384,768]{1,0:T(8,128)(2,1)S(1)}, u32[]{:S(2)}, u32[]{:S(2)}) collective-permute-start(bf16[384,768]{1,0:T(8,128)(2,1)} %bitcast.42), channel_id=1, source_target_pairs={{0,1},{1,0},{2,3},{3,2},{4,5},{5,4},{6,7},{7,6},{8,9},{9,8},{10,11... | collective-permute-start | bytes 1769480 | tf_op jit(solution)/shard_map/ppermute | solution.py:33
  299.0 26.9 %collective-permute-start.15 = (bf16[384,768]{1,0:T(8,128)(2,1)}, bf16[384,768]{1,0:T(8,128)(2,1)}, u32[]{:S(2)}, u32[]{:S(2)}) collective-permute-start(bf16[384,768]{1,0:T(8,128)(2,1)} %bitcast.44), channel_id=1, source_target_pairs={{0,2},{1,3},{2,0},{3,1},{4,6},{5,7},{6,4},{7,5},{8,10},{9,11},{10,... | collective-permute-start | bytes 1769480 | tf_op jit(solution)/shard_map/ppermute | solution.py:33
  300.0 26.0 %collective-permute-start.16 = (bf16[384,768]{1,0:T(8,128)(2,1)S(1)}, bf16[384,768]{1,0:T(8,128)(2,1)}, u32[]{:S(2)}, u32[]{:S(2)}) collective-permute-start(bf16[384,768]{1,0:T(8,128)(2,1)S(1)} %bitcast.313), channel_id=1, source_target_pairs={{0,3},{1,2},{2,1},{3,0},{4,7},{5,6},{6,5},{7,4},{8,11},{9,10},{10,... | collective-permute-start | bytes 1769480 | tf_op jit(solution)/shard_map/ppermute | solution.py:33
  377.6 240.4 %reduce-scatter.6.cloned.1.call-start = ((), (), s32[]{:S(2)}) async-start(), calls=%async_computation.9 | async-start | bytes 10616832 | tf_op jit(solution)/shard_map/reduce_scatter | solution.py:609
  393.0 5.9 collective-permute-start.17
  393.0 8.7 %collective-permute-start.18 = (f32[64,768]{1,0:T(8,128)}, f32[64,768]{1,0:T(8,128)}, u32[]{:S(2)}, u32[]{:S(2)}) collective-permute-start(f32[64,768]{1,0:T(8,128)} %get-tuple-element.216), channel_id=1, source_target_pairs={{0,2},{1,3},{2,0},{3,1},{4,6},{5,7},{6,4},{7,5},{8,10},{9,11},{10,... | collective-permute-start | bytes 589832 | tf_op jit(solution)/shard_map/ppermute | solution.py:33
  394.0 7.7 %collective-permute-start.19 = (f32[64,768]{1,0:T(8,128)}, f32[64,768]{1,0:T(8,128)}, u32[]{:S(2)}, u32[]{:S(2)}) collective-permute-start(f32[64,768]{1,0:T(8,128)} %get-tuple-element.215), channel_id=1, source_target_pairs={{0,3},{1,2},{2,1},{3,0},{4,7},{5,6},{6,5},{7,4},{8,11},{9,10},{10,... | collective-permute-start | bytes 589832 | tf_op jit(solution)/shard_map/ppermute | solution.py:33
  408.3 16.3 %collective-permute-start.20 = (bf16[384,768]{1,0:T(8,128)(2,1)S(1)}, bf16[384,768]{1,0:T(8,128)(2,1)S(1)}, u32[]{:S(2)}, u32[]{:S(2)}) collective-permute-start(bf16[384,768]{1,0:T(8,128)(2,1)S(1)} %get-tuple-element.197), channel_id=1, source_target_pairs={{0,1},{1,0},{2,3},{3,2},{4,5},{5,4},{6,7},{7,6},{8,9},{9,8},{10,11... | collective-permute-start | bytes 1769480 | tf_op jit(solution)/shard_map/ppermute | solution.py:33
  409.8 23.1 %collective-permute-start.21 = (bf16[384,768]{1,0:T(8,128)(2,1)S(1)}, bf16[384,768]{1,0:T(8,128)(2,1)S(1)}, u32[]{:S(2)}, u32[]{:S(2)}) collective-permute-start(bf16[384,768]{1,0:T(8,128)(2,1)S(1)} %get-tuple-element.196), channel_id=1, source_target_pairs={{0,2},{1,3},{2,0},{3,1},{4,6},{5,7},{6,4},{7,5},{8,10},{9,11},{10,... | collective-permute-start | bytes 1769480 | tf_op jit(solution)/shard_map/ppermute | solution.py:33
  410.6 22.3 %collective-permute-start.22 = (bf16[384,768]{1,0:T(8,128)(2,1)S(1)}, bf16[384,768]{1,0:T(8,128)(2,1)S(1)}, u32[]{:S(2)}, u32[]{:S(2)}) collective-permute-start(bf16[384,768]{1,0:T(8,128)(2,1)S(1)} %get-tuple-element.195), channel_id=1, source_target_pairs={{0,3},{1,2},{2,1},{3,0},{4,7},{5,6},{6,5},{7,4},{8,11},{9,10},{10,... | collective-permute-start | bytes 1769480 | tf_op jit(solution)/shard_map/ppermute | solution.py:33
  469.8 33.9 %collective-permute-start.23 = (bf16[384,768]{1,0:T(8,128)(2,1)}, bf16[384,768]{1,0:T(8,128)(2,1)}, u32[]{:S(2)}, u32[]{:S(2)}) collective-permute-start(bf16[384,768]{1,0:T(8,128)(2,1)} %bitcast.67), channel_id=1, source_target_pairs={{0,1},{1,0},{2,3},{3,2},{4,5},{5,4},{6,7},{7,6},{8,9},{9,8},{10,11... | collective-permute-start | bytes 1769480 | tf_op jit(solution)/shard_map/ppermute | solution.py:33
  471.4 32.3 %collective-permute-start.24 = (bf16[384,768]{1,0:T(8,128)(2,1)}, bf16[384,768]{1,0:T(8,128)(2,1)}, u32[]{:S(2)}, u32[]{:S(2)}) collective-permute-start(bf16[384,768]{1,0:T(8,128)(2,1)} %bitcast.69), channel_id=1, source_target_pairs={{0,2},{1,3},{2,0},{3,1},{4,6},{5,7},{6,4},{7,5},{8,10},{9,11},{10,... | collective-permute-start | bytes 1769480 | tf_op jit(solution)/shard_map/ppermute | solution.py:33
  471.7 32.1 %collective-permute-start.25 = (bf16[384,768]{1,0:T(8,128)(2,1)S(1)}, bf16[384,768]{1,0:T(8,128)(2,1)}, u32[]{:S(2)}, u32[]{:S(2)}) collective-permute-start(bf16[384,768]{1,0:T(8,128)(2,1)S(1)} %bitcast.315), channel_id=1, source_target_pairs={{0,3},{1,2},{2,1},{3,0},{4,7},{5,6},{6,5},{7,4},{8,11},{9,10},{10,... | collective-permute-start | bytes 1769480 | tf_op jit(solution)/shard_map/ppermute | solution.py:33
  507.0 224.5 %reduce-scatter.8.cloned.1.call-start = ((), (), s32[]{:S(2)}) async-start(), calls=%async_computation.10 | async-start | bytes 10616832 | tf_op jit(solution)/shard_map/reduce_scatter | solution.py:610
  557.0 40.7 %collective-permute-start.26 = (bf16[4,4,96,768]{3,2,1,0:T(8,128)(2,1)}, bf16[4,4,96,768]{3,2,1,0:T(8,128)(2,1)}, u32[]{:S(2)}, u32[]{:S(2)}) collective-permute-start(bf16[4,4,96,768]{3,2,1,0:T(8,128)(2,1)} %dynamic-slice_bitcast_fusion), channel_id=1, source_target_pairs={{0,4},{4,0},{8,12},{12,8},{16,20},{20,16},{24,28},{28,24},{1,5},{5... | collective-permute-start | bytes 7077896 | tf_op jit(solution)/shard_map/ppermute | solution.py:37
  558.1 37.7 %all-to-all-start.1 = ((bf16[512,8,96]{0,2,1:T(8,128)(2,1)}), bf16[512,8,96]{0,2,1:T(8,128)(2,1)S(1)}, u32[]{:S(2)}, u32[]{:S(2)}) async-start(bf16[512,8,96]{0,2,1:T(8,128)(2,1)} %bitcast.95), calls=%async_computation.2 | async-start | bytes 1572864 | tf_op jit(solution)/shard_map/all_to_all | solution.py:641
  565.4 1.4 collective-permute-start.27
  595.9 20.5 %collective-permute-start.31 = (bf16[96,4096]{1,0:T(8,128)(2,1)S(1)}, bf16[96,4096]{1,0:T(8,128)(2,1)S(1)}, u32[]{:S(2)}, u32[]{:S(2)}) collective-permute-start(bf16[96,4096]{1,0:T(8,128)(2,1)S(1)} %bitcast.287), channel_id=1, source_target_pairs={{0,1},{1,0},{2,3},{3,2},{4,5},{5,4},{6,7},{7,6},{8,9},{9,8},{10,11... | collective-permute-start | bytes 2359304 | tf_op jit(solution)/shard_map/ppermute | solution.py:33
  602.3 38.5 %collective-permute-start.28 = (bf16[4,102,768]{2,0,1:T(4,128)(2,1)}, bf16[4,102,768]{2,0,1:T(4,128)(2,1)S(1)}, u32[]{:S(2)}, u32[]{:S(2)}) collective-permute-start(bf16[4,102,768]{2,0,1:T(4,128)(2,1)} %copy.284), channel_id=1, source_target_pairs={{0,1},{1,0},{2,3},{3,2},{4,5},{5,4},{6,7},{7,6},{8,9},{9,8},{10,11... | collective-permute-start | bytes 1880072 | tf_op jit(solution)/shard_map/ppermute | solution.py:33
  603.6 37.2 %collective-permute-start.29 = (bf16[4,102,768]{2,0,1:T(4,128)(2,1)}, bf16[4,102,768]{2,0,1:T(4,128)(2,1)S(1)}, u32[]{:S(2)}, u32[]{:S(2)}) collective-permute-start(bf16[4,102,768]{2,0,1:T(4,128)(2,1)} %copy.288), channel_id=1, source_target_pairs={{0,2},{1,3},{2,0},{3,1},{4,6},{5,7},{6,4},{7,5},{8,10},{9,11},{10,... | collective-permute-start | bytes 1880072 | tf_op jit(solution)/shard_map/ppermute | solution.py:33
  606.2 38.2 %collective-permute-start.30 = (bf16[4,102,768]{2,0,1:T(4,128)(2,1)}, bf16[4,102,768]{2,0,1:T(4,128)(2,1)}, u32[]{:S(2)}, u32[]{:S(2)}) collective-permute-start(bf16[4,102,768]{2,0,1:T(4,128)(2,1)} %copy.292), channel_id=1, source_target_pairs={{0,3},{1,2},{2,1},{3,0},{4,7},{5,6},{6,5},{7,4},{8,11},{9,10},{10,... | collective-permute-start | bytes 1880072 | tf_op jit(solution)/shard_map/ppermute | solution.py:33
  607.9 65.0 %collective-permute-start.35 = (bf16[96,4096]{1,0:T(8,128)(2,1)S(1)}, bf16[96,4096]{1,0:T(8,128)(2,1)}, u32[]{:S(2)}, u32[]{:S(2)}) collective-permute-start(bf16[96,4096]{1,0:T(8,128)(2,1)S(1)} %bitcast.288), channel_id=1, source_target_pairs={{0,3},{1,2},{2,1},{3,0},{4,7},{5,6},{6,5},{7,4},{8,11},{9,10},{10,... | collective-permute-start | bytes 2359304 | tf_op jit(solution)/shard_map/ppermute | solution.py:33
  616.4 61.1 %collective-permute-start.39 = (bf16[96,4096]{1,0:T(8,128)(2,1)S(1)}, bf16[96,4096]{1,0:T(8,128)(2,1)}, u32[]{:S(2)}, u32[]{:S(2)}) collective-permute-start(bf16[96,4096]{1,0:T(8,128)(2,1)S(1)} %bitcast.289), channel_id=1, source_target_pairs={{0,2},{1,3},{2,0},{3,1},{4,6},{5,7},{6,4},{7,5},{8,10},{9,11},{10,... | collective-permute-start | bytes 2359304 | tf_op jit(solution)/shard_map/ppermute | solution.py:33
  649.6 14.2 %collective-permute-start.32 = (bf16[1,102,768]{2,1,0:T(8,128)(2,1)S(1)}, bf16[1,102,768]{2,1,0:T(8,128)(2,1)S(1)}, u32[]{:S(2)}, u32[]{:S(2)}) collective-permute-start(bf16[1,102,768]{2,1,0:T(8,128)(2,1)S(1)} %get-tuple-element.217), channel_id=1, source_target_pairs={{0,8},{4,12},{8,0},{12,4},{16,24},{20,28},{24,16},{28,20},{1,9},{5... | collective-permute-start | bytes 470024 | tf_op jit(solution)/shard_map/ppermute | solution.py:37
  649.6 17.4 %collective-permute-start.33 = (bf16[1,102,768]{2,1,0:T(8,128)(2,1)S(1)}, bf16[1,102,768]{2,1,0:T(8,128)(2,1)S(1)}, u32[]{:S(2)}, u32[]{:S(2)}) collective-permute-start(bf16[1,102,768]{2,1,0:T(8,128)(2,1)S(1)} %get-tuple-element.219), channel_id=1, source_target_pairs={{0,16},{4,20},{8,24},{12,28},{16,0},{20,4},{24,8},{28,12},{1,17},{... | collective-permute-start | bytes 470024 | tf_op jit(solution)/shard_map/ppermute | solution.py:37
  651.4 21.4 %collective-permute-start.34 = (bf16[1,102,768]{2,1,0:T(8,128)(2,1)S(1)}, bf16[1,102,768]{2,1,0:T(8,128)(2,1)S(1)}, u32[]{:S(2)}, u32[]{:S(2)}) collective-permute-start(bf16[1,102,768]{2,1,0:T(8,128)(2,1)S(1)} %get-tuple-element.218), channel_id=1, source_target_pairs={{0,24},{4,28},{8,16},{12,20},{16,8},{20,12},{24,0},{28,4},{1,25},{... | collective-permute-start | bytes 470024 | tf_op jit(solution)/shard_map/ppermute | solution.py:37
  672.9 43.8 %collective-permute-start.36 = (f32[96,768]{1,0:T(8,128)S(1)}, f32[96,768]{1,0:T(8,128)}, u32[]{:S(2)}, u32[]{:S(2)}) collective-permute-start(f32[96,768]{1,0:T(8,128)S(1)} %add_bitcast_fusion), channel_id=1, source_target_pairs={{0,1},{1,0},{2,3},{3,2},{4,5},{5,4},{6,7},{7,6},{8,9},{9,8},{10,11... | collective-permute-start | bytes 884744 | tf_op jit(solution)/shard_map/ppermute | solution.py:33
  673.7 43.1 %collective-permute-start.37 = (f32[96,768]{1,0:T(8,128)S(1)}, f32[96,768]{1,0:T(8,128)}, u32[]{:S(2)}, u32[]{:S(2)}) collective-permute-start(f32[96,768]{1,0:T(8,128)S(1)} %add_bitcast_fusion), channel_id=1, source_target_pairs={{0,2},{1,3},{2,0},{3,1},{4,6},{5,7},{6,4},{7,5},{8,10},{9,11},{10,... | collective-permute-start | bytes 884744 | tf_op jit(solution)/shard_map/ppermute | solution.py:33
  676.1 40.6 %collective-permute-start.38 = (f32[96,768]{1,0:T(8,128)S(1)}, f32[96,768]{1,0:T(8,128)}, u32[]{:S(2)}, u32[]{:S(2)}) collective-permute-start(f32[96,768]{1,0:T(8,128)S(1)} %add_bitcast_fusion), channel_id=1, source_target_pairs={{0,3},{1,2},{2,1},{3,0},{4,7},{5,6},{6,5},{7,4},{8,11},{9,10},{10,... | collective-permute-start | bytes 884744 | tf_op jit(solution)/shard_map/ppermute | solution.py:33
  (104 other events, 1003.4 us)
Sparse Core Ops, SparseCore 0:
  10.2 106.8 all-gather.5
  119.3 105.7 all-gather.7
  227.4 113.4 all-gather.9
  377.7 125.6 reduce-scatter.3
  507.0 110.6 reduce-scatter.5
  620.0 111.5 reduce-scatter.7
